TPU v7x, 32 devices: a whole 2x2x4 slice. The times are simulated.
32 devices in a mesh: dp: 16 (over z, x, core), tensor: 2 (over y).
Axes of the slice: x: 2, y: 2, z: 4, core: 2. Of those that a mesh axis runs over, the one named last changes fastest.
Arguments:
- inputs: bfloat16 [16384, 1024], P(('dp', 'tensor')), may hold values from -6 to 6
- seg_ids: int32 [32, 512], P('dp'), may hold values from 0 to 15, never falling along the last dimension, each value on 1 to 384 neighbouring positions
- qkv_weight: float32 [2, 3, 1024, 1024], P(None, None, 'dp', 'tensor'), may hold values from -0.1875 to 0.1875
- out_weight: float32 [2, 1024, 1024], P(None, 'tensor', 'dp'), may hold values from -1.5 to 1.5
- up_weight: float32 [2, 1024, 4096], P(None, 'dp', 'tensor'), may hold values from -0.1875 to 0.1875
- down_weight: float32 [2, 4096, 1024], P(None, 'tensor', 'dp'), may hold values from -0.09375 to 0.09375
- norm_gains: float32 [2, 2, 1024], P(None, None, ('dp', 'tensor')), may hold values from 0.5 to 1.5
- row_biases: float32 [2, 6, 1024], P(None, None, ('dp', 'tensor')), may hold values from -2.5 to 2.5
- ff_bias: float32 [2, 4096], P(None, ('dp', 'tensor')), may hold values from -2.5 to 2.5
- cotangent: float32 [16384, 1024], P(('dp', 'tensor')), may hold values from -6 to 6
Outputs:
- outputs: bfloat16 [16384, 1024], P(('dp', 'tensor'))
- input_grad: float32 [16384, 1024], P(('dp', 'tensor'))
- qkv_grad: float32 [2, 3, 1024, 1024], P(None, None, 'dp', 'tensor')
- out_grad: float32 [2, 1024, 1024], P(None, 'tensor', 'dp')
- up_grad: float32 [2, 1024, 4096], P(None, 'dp', 'tensor')
- down_grad: float32 [2, 4096, 1024], P(None, 'tensor', 'dp')
- gains_grad: float32 [2, 2, 1024], P(None, None, ('dp', 'tensor'))
- biases_grad: float32 [2, 6, 1024], P(None, None, ('dp', 'tensor'))
- ff_bias_grad: float32 [2, 4096], P(None, ('dp', 'tensor'))
Inputs may be any that keep to these rules, and one draw needn't show every extreme that they name: `seg_ids`: within each sequence the document numbers never fall, and each document has 1 to 384 positions.
All inputs are finite; a program needn't handle non-finite values.
Results may differ from a plain program's by a relative error of at most 0.035.
Values may be sent and summed in bfloat16 or wider, within the bound.
No kernel may reach another device: no remote copies, remote signals or barrier semaphores. Data moves between devices by JAX's collectives and lax.ppermute only.
A program may use at most 256 MiB of HBM per device.

v0:
```python
from functools import partial

import jax
import jax.numpy as jnp
from jax import lax
from jax.sharding import PartitionSpec as P

HD = 64


EPSILON = 1e-06
HALF_ROOT = 0.7071067811865476
INV_ROOT_TAU = 0.3989422804014327


def normed(summed, gain_row, shift_row):
    centre = summed - jnp.mean(summed, axis=-1, keepdims=True)
    spread = jnp.mean(centre * centre, axis=-1, keepdims=True)
    return centre * lax.rsqrt(spread + EPSILON) * gain_row + shift_row


def gelu_slope(hidden_in):
    return (
        0.5 * (1.0 + lax.erf(hidden_in * HALF_ROOT))
        + hidden_in * jnp.exp(-0.5 * hidden_in * hidden_in) * INV_ROOT_TAU
    )


def collect(local_rows):
    return lax.all_gather(local_rows, "tensor", axis=0, tiled=True)


def reduce_rows(term_fn, row_count):
    return lax.psum_scatter(
        term_fn(jnp.int32(0), row_count * lax.axis_size("tensor")).astype(jnp.bfloat16),
        "tensor",
        scatter_dimension=0,
        tiled=True,
    ).astype(jnp.float32)


def project(operand, matrix, first_row, row_span):
    return jnp.dot(operand, matrix, preferred_element_type=jnp.float32)


def project_back(operand, matrix, first_row, row_span):
    return jnp.einsum("rf,df->rd", operand, matrix, preferred_element_type=jnp.float32)


def project_triple(operand, matrix, first_row, row_span):
    return jnp.einsum("rkc,kdc->rd", operand, matrix, preferred_element_type=jnp.float32)


def split_heads(matrix):
    return matrix.reshape(matrix.shape[0], matrix.shape[1] // HD, HD)


def masked_scores(query_heads, key_heads, segment):
    scores = jnp.einsum(
        "qhe,khe->hqk", query_heads, key_heads, preferred_element_type=jnp.float32
    ) * HD ** (-0.5)
    same_doc = segment[:, None] == segment[None, :]
    return jnp.where(same_doc[None], scores, -jnp.inf)


def attend_block(pieces):
    queries, key_rows, values, segment = pieces
    scores = masked_scores(split_heads(queries), split_heads(key_rows), segment)
    row_max = jnp.max(scores, axis=-1, keepdims=True)
    exp_scores = jnp.exp(scores - row_max)
    exp_total = jnp.sum(exp_scores, axis=-1, keepdims=True)
    attn_probs = (exp_scores / exp_total).astype(jnp.bfloat16)
    mixture = jnp.einsum(
        "hqk,khe->qhe", attn_probs, split_heads(values), preferred_element_type=jnp.float32
    )
    return (
        mixture.reshape(queries.shape).astype(jnp.bfloat16),
        (row_max + jnp.log(exp_total))[..., 0],
    )


def attend_back(pieces):
    queries, key_rows, values, segment, grad_mix, logsum = pieces
    query_heads = split_heads(queries)
    key_heads = split_heads(key_rows)
    value_heads = split_heads(values)
    grad_heads = split_heads(grad_mix)
    attn_probs = jnp.exp(masked_scores(query_heads, key_heads, segment) - logsum[..., None])
    grad_values = jnp.einsum(
        "hqk,qhe->khe",
        attn_probs.astype(jnp.bfloat16),
        grad_heads,
        preferred_element_type=jnp.float32,
    )
    grad_probs = jnp.einsum(
        "qhe,khe->hqk", grad_heads, value_heads, preferred_element_type=jnp.float32
    )
    inner_sum = jnp.sum(grad_probs * attn_probs, axis=-1, keepdims=True)
    grad_scores = (attn_probs * (grad_probs - inner_sum)).astype(jnp.bfloat16)
    grad_queries = jnp.einsum(
        "hqk,khe->qhe", grad_scores, key_heads, preferred_element_type=jnp.float32
    ) * HD ** (-0.5)
    grad_keys = jnp.einsum(
        "hqk,qhe->khe", grad_scores, query_heads, preferred_element_type=jnp.float32
    ) * HD ** (-0.5)
    stacked = jnp.stack([grad_queries, grad_keys, grad_values], axis=1)
    return stacked.reshape(queries.shape[0], 3, queries.shape[1]).astype(jnp.bfloat16)


def on_device(
    inputs,
    seg_ids,
    qkv_weight,
    out_weight,
    up_weight,
    down_weight,
    norm_gains,
    row_biases,
    ff_bias,
    cotangent,
):
    gain_rows, shift_rows, up_shifts = (
        lax.all_gather(norm_gains, ("dp", "tensor"), axis=2, tiled=True),
        lax.all_gather(row_biases, ("dp", "tensor"), axis=2, tiled=True),
        lax.all_gather(ff_bias, ("dp", "tensor"), axis=1, tiled=True),
    )
    tensor_rank = lax.axis_index("tensor")
    row_count = inputs.shape[0]
    model_width = inputs.shape[1]
    seq_count, length = seg_ids.shape
    head_cols = qkv_weight.shape[3]
    hidden = up_weight.shape[2]
    full_hidden = up_shifts.shape[1]
    layers = qkv_weight.shape[0]
    stream = inputs.astype(jnp.float32)
    stored = []
    for layer_index in range(layers):
        qkv_mat, out_mat, up_mat, down_mat = (
            lax.all_gather(qkv_weight[layer_index].astype(jnp.bfloat16), "dp", axis=1, tiled=True),
            lax.all_gather(out_weight[layer_index].astype(jnp.bfloat16), "dp", axis=1, tiled=True),
            lax.all_gather(up_weight[layer_index].astype(jnp.bfloat16), "dp", axis=0, tiled=True),
            lax.all_gather(down_weight[layer_index].astype(jnp.bfloat16), "dp", axis=1, tiled=True),
        )
        shifts = shift_rows[layer_index]
        query_shift = lax.dynamic_slice_in_dim(shifts[0], tensor_rank * head_cols, head_cols)
        value_shift = lax.dynamic_slice_in_dim(shifts[1], tensor_rank * head_cols, head_cols)
        up_shift = lax.dynamic_slice_in_dim(up_shifts[layer_index], tensor_rank * hidden, hidden)
        gathered = collect(stream.astype(jnp.bfloat16))
        projected = jnp.einsum("rd,kdc->rkc", gathered, qkv_mat, preferred_element_type=jnp.float32)
        projected = (
            projected + jnp.stack([query_shift, jnp.zeros_like(query_shift), value_shift])
        ).astype(jnp.bfloat16)
        by_sequence = projected.reshape(seq_count, length, 3, head_cols)
        mixture, logsum = lax.map(
            attend_block,
            (by_sequence[:, :, 0], by_sequence[:, :, 1], by_sequence[:, :, 2], seg_ids),
        )
        mixture = mixture.reshape(seq_count * length, head_cols)
        attended = reduce_rows(partial(project, mixture, out_mat), row_count)
        first_sum = stream + (attended + shifts[2])
        normed_mid = normed(first_sum, gain_rows[layer_index, 0], shifts[3])
        gathered_mid = collect(normed_mid.astype(jnp.bfloat16))
        hidden_in = jnp.dot(gathered_mid, up_mat, preferred_element_type=jnp.float32) + up_shift
        hidden_out = jax.nn.gelu(hidden_in, approximate=False).astype(jnp.bfloat16)
        branch_out = reduce_rows(partial(project, hidden_out, down_mat), row_count)
        second_sum = normed_mid + (branch_out + shifts[4])
        stream = normed(second_sum, gain_rows[layer_index, 1], shifts[5])
        stored.append(
            (
                qkv_mat,
                out_mat,
                up_mat,
                down_mat,
                gathered,
                projected,
                logsum,
                mixture,
                first_sum,
                gathered_mid,
                hidden_in,
                hidden_out,
                second_sum,
            )
        )
    grad_stream = cotangent
    weight_grads = [None] * layers
    small_grads = [None] * layers
    for layer_index in reversed(range(layers)):
        (
            qkv_mat,
            out_mat,
            up_mat,
            down_mat,
            gathered,
            projected,
            logsum,
            mixture,
            first_sum,
            gathered_mid,
            hidden_in,
            hidden_out,
            second_sum,
        ) = stored[layer_index]
        qkv_mat, out_mat, up_mat, down_mat = (
            lax.all_gather(qkv_weight[layer_index].astype(jnp.bfloat16), "dp", axis=1, tiled=True),
            lax.all_gather(out_weight[layer_index].astype(jnp.bfloat16), "dp", axis=1, tiled=True),
            lax.all_gather(up_weight[layer_index].astype(jnp.bfloat16), "dp", axis=0, tiled=True),
            lax.all_gather(down_weight[layer_index].astype(jnp.bfloat16), "dp", axis=1, tiled=True),
        )
        shifts = shift_rows[layer_index]
        layer_gains = gain_rows[layer_index]
        grad_second, grad_gain_late, grad_shift_late = jax.vjp(
            normed, second_sum, layer_gains[1], shifts[5]
        )[1](grad_stream)
        grad_branch = collect(grad_second.astype(jnp.bfloat16))
        grad_down = jnp.einsum(
            "rf,rd->fd", hidden_out, grad_branch, preferred_element_type=jnp.float32
        )
        grad_hidden = jnp.einsum(
            "rd,fd->rf", grad_branch, down_mat, preferred_element_type=jnp.float32
        )
        grad_pre = (grad_hidden * gelu_slope(hidden_in)).astype(jnp.bfloat16)
        grad_up = jnp.einsum(
            "rd,rf->df", gathered_mid, grad_pre, preferred_element_type=jnp.float32
        )
        grad_mid = grad_second + reduce_rows(partial(project_back, grad_pre, up_mat), row_count)
        grad_first, grad_gain_early, grad_shift_early = jax.vjp(
            normed, first_sum, layer_gains[0], shifts[3]
        )[1](grad_mid)
        grad_attn = collect(grad_first.astype(jnp.bfloat16))
        grad_out = jnp.einsum("rc,rd->cd", mixture, grad_attn, preferred_element_type=jnp.float32)
        grad_mix = jnp.einsum(
            "rd,cd->rc", grad_attn, out_mat, preferred_element_type=jnp.float32
        ).astype(jnp.bfloat16)
        by_sequence = projected.reshape(seq_count, length, 3, head_cols)
        grad_proj = lax.map(
            attend_back,
            (
                by_sequence[:, :, 0],
                by_sequence[:, :, 1],
                by_sequence[:, :, 2],
                seg_ids,
                grad_mix.reshape(seq_count, length, head_cols),
                logsum,
            ),
        )
        grad_proj = grad_proj.reshape(seq_count * length, 3, head_cols)
        grad_qkv = jnp.einsum(
            "rd,rkc->kdc", gathered, grad_proj, preferred_element_type=jnp.float32
        )
        grad_stream = grad_first + reduce_rows(
            partial(project_triple, grad_proj, qkv_mat), row_count
        )
        proj_sums = jnp.sum(grad_proj.astype(jnp.float32), axis=0)
        zero_row = jnp.zeros((model_width,), jnp.float32)
        grad_query_shift = lax.dynamic_update_slice_in_dim(
            zero_row, proj_sums[0], tensor_rank * head_cols, 0
        )
        grad_value_shift = lax.dynamic_update_slice_in_dim(
            zero_row, proj_sums[2], tensor_rank * head_cols, 0
        )
        grad_up_shift = lax.dynamic_update_slice_in_dim(
            jnp.zeros((full_hidden,), jnp.float32),
            jnp.sum(grad_pre.astype(jnp.float32), axis=0),
            tensor_rank * hidden,
            0,
        )
        small_grads[layer_index] = (
            jnp.stack([grad_gain_early, grad_gain_late]),
            jnp.stack(
                [
                    grad_query_shift,
                    grad_value_shift,
                    jnp.sum(grad_first, axis=0),
                    grad_shift_early,
                    jnp.sum(grad_second, axis=0),
                    grad_shift_late,
                ]
            ),
            grad_up_shift,
        )
        weight_grads[layer_index] = (
            lax.psum_scatter(
                grad_qkv.astype(jnp.bfloat16), "dp", scatter_dimension=1, tiled=True
            ).astype(jnp.float32),
            lax.psum_scatter(
                grad_out.astype(jnp.bfloat16), "dp", scatter_dimension=1, tiled=True
            ).astype(jnp.float32),
            lax.psum_scatter(
                grad_up.astype(jnp.bfloat16), "dp", scatter_dimension=0, tiled=True
            ).astype(jnp.float32),
            lax.psum_scatter(
                grad_down.astype(jnp.bfloat16), "dp", scatter_dimension=1, tiled=True
            ).astype(jnp.float32),
        )
    qkv_stack = jnp.stack([weight_grads[layer_index][0] for layer_index in range(layers)])
    out_stack = jnp.stack([weight_grads[layer_index][1] for layer_index in range(layers)])
    up_stack = jnp.stack([weight_grads[layer_index][2] for layer_index in range(layers)])
    down_stack = jnp.stack([weight_grads[layer_index][3] for layer_index in range(layers)])
    gains_all = jnp.stack([small_grads[layer_index][0] for layer_index in range(layers)])
    shifts_all = jnp.stack([small_grads[layer_index][1] for layer_index in range(layers)])
    hidden_all = jnp.stack([small_grads[layer_index][2] for layer_index in range(layers)])
    gains_grad, biases_grad, ff_bias_grad = (
        lax.psum_scatter(gains_all, ("dp", "tensor"), scatter_dimension=2, tiled=True),
        lax.psum_scatter(shifts_all, ("dp", "tensor"), scatter_dimension=2, tiled=True),
        lax.psum_scatter(hidden_all, ("dp", "tensor"), scatter_dimension=1, tiled=True),
    )
    return (
        stream.astype(jnp.bfloat16),
        grad_stream,
        qkv_stack,
        out_stack,
        up_stack,
        down_stack,
        gains_grad,
        biases_grad,
        ff_bias_grad,
    )


def solution(mesh):
    placed = (
        P(("dp", "tensor"), None),
        P("dp", None),
        P(None, None, "dp", "tensor"),
        P(None, "tensor", "dp"),
        P(None, "dp", "tensor"),
        P(None, "tensor", "dp"),
        P(None, None, ("dp", "tensor")),
        P(None, None, ("dp", "tensor")),
        P(None, ("dp", "tensor")),
        P(("dp", "tensor"), None),
    )
    return jax.shard_map(
        on_device,
        mesh=mesh,
        in_specs=placed,
        out_specs=(
            P(("dp", "tensor"), None),
            P(("dp", "tensor"), None),
            P(None, None, "dp", "tensor"),
            P(None, "tensor", "dp"),
            P(None, "dp", "tensor"),
            P(None, "tensor", "dp"),
            P(None, None, ("dp", "tensor")),
            P(None, None, ("dp", "tensor")),
            P(None, ("dp", "tensor")),
        ),
        check_vma=False,
    )
```

profile of v0, /device:TPU:8, one launch (start us, length us, event | category | flops | bytes accessed | tf_op | source)
XLA Modules:
  0.0 2119.5 jit_solution(10846130051365599466)
XLA Ops:
  12.5 66.0 %all_gather.67 = f32[2,6,1024]{1,0,2:T(2,128)S(1)} all-gather(f32[2,6,32]{1,0,2:T(2,128)S(1)} %copy.99), channel_id=1, replica_groups=mesh['dp'=16,'tensor'=2] {'dp','tensor'}, dimensions={2}, use_global_device_ids=true | all-gather | bytes 50688 | tf_op jit(solution)/shard_map/all_gather | solution.py:124
  78.5 27.6 %fusion.141 = (f32[1,1,1024]{1,0,2:T(1,128)S(1)}, f32[1,1,1024]{1,0,2:T(1,128)S(1)}, f32[1,1,1024]{1,0,2:T(1,128)S(1)}, f32[1024]{0:T(1024)S(1)}, f32[1024]{0:T(...) fusion(f32[2,6,1024]{1,0,2:T(2,128)S(1)} %all_gather.67), kind=kLoop, calls=%fused_computation.290 | loop fusion | bytes 98304 | tf_op jit(solution)/shard_map/slice | solution.py:145
  146.3 69.6 %all_gather.69 = f32[2,2,1024]{1,0,2:T(2,128)S(1)} all-gather(f32[2,2,32]{1,0,2:T(2,128)S(1)} %copy.104), channel_id=1, replica_groups=mesh['dp'=16,'tensor'=2] {'dp','tensor'}, dimensions={2}, use_global_device_ids=true | all-gather | bytes 16896 | tf_op jit(solution)/shard_map/all_gather | solution.py:123
  215.9 26.9 %slice_reduce_fusion.1 = (f32[1024]{0:T(1024)}, f32[1024]{0:T(1024)}, f32[1024]{0:T(1024)S(1)}, f32[1024]{0:T(1024)S(1)}) fusion(f32[2,2,1024]{1,0,2:T(2,128)S(1)} %all_gather.69), kind=kLoop, calls=%fused_computation.222 | loop fusion | bytes 32768 | tf_op jit(solution)/shard_map/slice | solution.py:167
  249.2 66.1 %all_gather.72 = f32[2,4096]{1,0:T(2,128)S(1)} all-gather(f32[2,128]{1,0:T(2,128)S(1)} %copy-done.89), channel_id=1, replica_groups=mesh['dp'=16,'tensor'=2] {'dp','tensor'}, dimensions={1}, use_global_device_ids=true | all-gather | bytes 33792 | tf_op jit(solution)/shard_map/all_gather | solution.py:125
  315.9 25.8 %fusion.36 = (bf16[1024,2048]{1,0:T(8,128)(2,1)}, f32[1024,2048]{1,0:T(8,128)}) fusion(f32[2048]{0:T(1024)S(1)} %bitcast.432, bf16[1024,1024]{1,0:T(8,128)(2,1)} %all-gather.27.cloned.1.call-done, bf16[1,1024,2048]{2,1,0:T(8,128)(2,1)} %all-gather.45.cloned.1.call-done), kind=kOutput, calls=%fused_computation.80 | convolution fusion | flops 4433379328 | bytes 18882560 | tf_op jit(solution)/shard_map/dot_general | solution.py:163
  356.5 35.7 %reduce-scatter.26.cloned.1.call-done = bf16[512,1024]{1,0:T(8,128)(2,1)} async-done(((bf16[1024,1024]{1,0:T(8,128)(2,1)}), bf16[512,1024]{1,0:T(8,128)(2,1)}) %reduce-scatter.26.cloned.1.call-update) | async-done | bytes 1048592 | tf_op jit(solution)/shard_map/reduce_scatter | solution.py:34
  398.3 41.8 %all-gather.49.cloned.1.call-done = bf16[1,3,1024,512]{3,2,1,0:T(8,128)(2,1)} async-done(((bf16[1,3,64,512]{3,2,1,0:T(8,128)(2,1)}), bf16[1,3,1024,512]{3,2,1,0:T(8,128)(2,1)}) %all-gather.49.cloned.1.call-update) | async-done | bytes 3145744 | tf_op jit(solution)/shard_map/all_gather | solution.py:139
  440.1 33.5 %all-gather.29.cloned.1.call-done = bf16[1024,1024]{1,0:T(8,128)(2,1)} async-done(((bf16[512,1024]{1,0:T(8,128)(2,1)}), bf16[1024,1024]{1,0:T(8,128)(2,1)}) %all-gather.29.cloned.1.call-update) | async-done | bytes 2097168 | tf_op jit(solution)/shard_map/all_gather | solution.py:30
  517.8 31.0 %reduce-scatter.28.cloned.1.call-done = bf16[512,1024]{1,0:T(8,128)(2,1)} async-done(((bf16[1024,1024]{1,0:T(8,128)(2,1)}), bf16[512,1024]{1,0:T(8,128)(2,1)}) %reduce-scatter.28.cloned.1.call-update) | async-done | bytes 1048592 | tf_op jit(solution)/shard_map/reduce_scatter | solution.py:34
  554.4 48.2 %all-gather.53.cloned.1.call-done = bf16[1,1024,2048]{2,1,0:T(8,128)(2,1)} async-done(((bf16[1,64,2048]{2,1,0:T(8,128)(2,1)}), bf16[1,1024,2048]{2,1,0:T(8,128)(2,1)}) %all-gather.53.cloned.1.call-update) | async-done | bytes 4194320 | tf_op jit(solution)/shard_map/all_gather | solution.py:141
  602.6 33.7 %all-gather.31.cloned.1.call-done = bf16[1024,1024]{1,0:T(8,128)(2,1)} async-done(((bf16[512,1024]{1,0:T(8,128)(2,1)}), bf16[1024,1024]{1,0:T(8,128)(2,1)}) %all-gather.31.cloned.1.call-update) | async-done | bytes 2097168 | tf_op jit(solution)/shard_map/all_gather | solution.py:30
  661.9 27.4 %all-gather.55.cloned.1.call-done = bf16[1,2048,1024]{1,2,0:T(8,128)(2,1)} async-done(((bf16[1,2048,64]{1,2,0:T(8,128)(2,1)}), bf16[1,2048,1024]{1,2,0:T(8,128)(2,1)}) %all-gather.55.cloned.1.call-update) | async-done | bytes 4194320 | tf_op jit(solution)/shard_map/all_gather | solution.py:142
  698.7 30.4 %reduce-scatter.30.cloned.1.call-done = bf16[512,1024]{1,0:T(8,128)(2,1)} async-done(((bf16[1024,1024]{1,0:T(8,128)(2,1)}), bf16[512,1024]{1,0:T(8,128)(2,1)}) %reduce-scatter.30.cloned.1.call-update) | async-done | bytes 1048592 | tf_op jit(solution)/shard_map/reduce_scatter | solution.py:34
  737.6 33.0 %all-gather.33.cloned.1.call-done = bf16[1024,1024]{1,0:T(8,128)(2,1)} async-done(((bf16[512,1024]{1,0:T(8,128)(2,1)}), bf16[1024,1024]{1,0:T(8,128)(2,1)}) %all-gather.33.cloned.1.call-update) | async-done | bytes 2097168 | tf_op jit(solution)/shard_map/all_gather | solution.py:30
  789.7 31.9 %reduce-scatter.32.cloned.1.call-done = bf16[512,1024]{1,0:T(8,128)(2,1)} async-done(((bf16[1024,1024]{1,0:T(8,128)(2,1)}), bf16[512,1024]{1,0:T(8,128)(2,1)}) %reduce-scatter.32.cloned.1.call-update) | async-done | bytes 1048592 | tf_op jit(solution)/shard_map/reduce_scatter | solution.py:34
  829.1 33.0 %all-gather.35.cloned.1.call-done = bf16[1024,1024]{1,0:T(8,128)(2,1)} async-done(((bf16[512,1024]{1,0:T(8,128)(2,1)}), bf16[1024,1024]{1,0:T(8,128)(2,1)}) %all-gather.35.cloned.1.call-update) | async-done | bytes 2097168 | tf_op jit(solution)/shard_map/all_gather | solution.py:30
  867.9 31.9 %while.46 = (s32[]{:T(128)}, bf16[2,512,3,512]{1,3,2,0:T(8,128)(2,1)}, bf16[2,512,512]{1,2,0:T(8,128)(2,1)S(1)}, s32[2,512]{1,0:T(2,128)S(1)}, bf16[2,512,512]{1...) while((s32[]{:T(128)}, ...), condition=%wide.region_27.28_spmd, body=%wide.region_25.27_spmd.sunk | while | flops 1379921920 | bytes 102881448 | solution.py:236
  912.8 31.5 %reduce-scatter.34.cloned.1.call-done = bf16[512,1024]{1,0:T(8,128)(2,1)} async-done(((bf16[1024,1024]{1,0:T(8,128)(2,1)}), bf16[512,1024]{1,0:T(8,128)(2,1)}) %reduce-scatter.34.cloned.1.call-update) | async-done | bytes 1048592 | tf_op jit(solution)/shard_map/reduce_scatter | solution.py:34
  951.5 33.2 %all-gather.37.cloned.1.call-done = bf16[1024,1024]{1,0:T(8,128)(2,1)} async-done(((bf16[512,1024]{1,0:T(8,128)(2,1)}), bf16[1024,1024]{1,0:T(8,128)(2,1)}) %all-gather.37.cloned.1.call-update) | async-done | bytes 2097168 | tf_op jit(solution)/shard_map/all_gather | solution.py:30
  1003.4 31.9 %reduce-scatter.36.cloned.1.call-done = bf16[512,1024]{1,0:T(8,128)(2,1)} async-done(((bf16[1024,1024]{1,0:T(8,128)(2,1)}), bf16[512,1024]{1,0:T(8,128)(2,1)}) %reduce-scatter.36.cloned.1.call-update) | async-done | bytes 1048592 | tf_op jit(solution)/shard_map/reduce_scatter | solution.py:34
  1096.8 32.0 %while.47 = (s32[]{:T(128)}, bf16[2,512,3,512]{1,3,2,0:T(8,128)(2,1)}, bf16[2,512,512]{1,2,0:T(8,128)(2,1)S(1)}, s32[2,512]{1,0:T(2,128)S(1)}, bf16[2,512,512]{1...) while((s32[]{:T(128)}, ...), condition=%wide.region_36.37_spmd, body=%wide.region_34.36_spmd.sunk | while | flops 1379921920 | bytes 102881448 | solution.py:236
  1204.4 131.8 %reduce-scatter.52.cloned.1.call-done = f32[32,4]{1,0:T(8,128)} async-done(((f32[1024,4]{1,0:T(8,128)}), f32[32,4]{1,0:T(8,128)}) %reduce-scatter.52.cloned.1.call-update) | async-done | bytes 528
  1337.7 84.1 %reduce-scatter.50.cloned.1.call-done = bf16[2048,64]{0,1:T(8,128)(2,1)} async-done(((bf16[2048,1024]{0,1:T(8,128)(2,1)}), bf16[2048,64]{0,1:T(8,128)(2,1)}) %reduce-scatter.50.cloned.1.call-update) | async-done | bytes 262160 | tf_op jit(solution)/shard_map/reduce_scatter | solution.py:292
  1421.8 75.2 %reduce-scatter.48.cloned.1.call-done = bf16[2048,64]{0,1:T(8,128)(2,1)} async-done(((bf16[2048,1024]{0,1:T(8,128)(2,1)}), bf16[2048,64]{0,1:T(8,128)(2,1)}) %reduce-scatter.48.cloned.1.call-update) | async-done | bytes 262160 | tf_op jit(solution)/shard_map/reduce_scatter | solution.py:292
  1499.1 74.1 %reduce-scatter.46.cloned.1.call-done = bf16[64,2048]{1,0:T(8,128)(2,1)} async-done(((bf16[1024,2048]{1,0:T(8,128)(2,1)}), bf16[64,2048]{1,0:T(8,128)(2,1)}) %reduce-scatter.46.cloned.1.call-update) | async-done | bytes 262160 | tf_op jit(solution)/shard_map/reduce_scatter | solution.py:289
  1573.1 75.4 %reduce-scatter.44.cloned.1.call-done = bf16[64,2048]{1,0:T(8,128)(2,1)} async-done(((bf16[1024,2048]{1,0:T(8,128)(2,1)}), bf16[64,2048]{1,0:T(8,128)(2,1)}) %reduce-scatter.44.cloned.1.call-update) | async-done | bytes 262160 | tf_op jit(solution)/shard_map/reduce_scatter | solution.py:289
  1650.6 120.4 %reduce-scatter.54.cloned.1.call-done = f32[32,12]{1,0:T(8,128)} async-done(((f32[1024,12]{1,0:T(8,128)}), f32[32,12]{1,0:T(8,128)}) %reduce-scatter.54.cloned.1.call-update) | async-done | bytes 1552
  1772.4 68.7 %reduce-scatter.42.cloned.1.call-done = bf16[512,64]{0,1:T(8,128)(2,1)} async-done(((bf16[512,1024]{0,1:T(8,128)(2,1)}), bf16[512,64]{0,1:T(8,128)(2,1)}) %reduce-scatter.42.cloned.1.call-update) | async-done | bytes 65552 | tf_op jit(solution)/shard_map/reduce_scatter | solution.py:286
  1841.1 60.5 %reduce-scatter.40.cloned.1.call-done = bf16[512,64]{0,1:T(8,128)(2,1)} async-done(((bf16[512,1024]{0,1:T(8,128)(2,1)}), bf16[512,64]{0,1:T(8,128)(2,1)}) %reduce-scatter.40.cloned.1.call-update) | async-done | bytes 65552 | tf_op jit(solution)/shard_map/reduce_scatter | solution.py:286
  1903.2 171.3 %all-reduce.5.cloned.1.call-done = (bf16[3,1024,512]{2,0,1:T(4,128)(2,1)}, bf16[3,1024,512]{2,0,1:T(4,128)(2,1)}) async-done(((bf16[3,1024,512]{2,0,1:T(4,128)(2,1)}, bf16[3,1024,512]{2,0,1:T(4,128)(2,1)}), (bf16[3,1024,512]{2,0,1:T(4,128)(2,1)}, bf16[3,1024,512]{2,0,1:T(4,128)(2,1)})) %all-reduce.5.cloned.1.call-update) | async-done | bytes 6291472
  2078.1 31.3 %reduce-scatter.38.cloned.1.call-done = bf16[512,1024]{1,0:T(8,128)(2,1)} async-done(((bf16[1024,1024]{1,0:T(8,128)(2,1)}), bf16[512,1024]{1,0:T(8,128)(2,1)}) %reduce-scatter.38.cloned.1.call-update) | async-done | bytes 1048592 | tf_op jit(solution)/shard_map/reduce_scatter | solution.py:34
  (519 shorter events, 483.9 us)
Async XLA Ops:
  7.2 103.7 %all-gather.25.cloned.1.call-start = ((), (), s32[]{:S(2)}) async-start(), calls=%async_computation.17 | async-start | bytes 3145728 | tf_op jit(solution)/shard_map/all_gather | solution.py:30
  7.9 103.0 %all-gather.41.cloned.1.call-start = ((), (), s32[]{:S(2)}) async-start(), calls=%async_computation.39 | async-start | bytes 3342336 | tf_op jit(solution)/shard_map/all_gather | solution.py:139
  9.9 130.9 %all-gather.43.cloned.1.call-start = ((), (), s32[]{:S(2)}) async-start(), calls=%async_computation.40 | async-start | bytes 1114112 | tf_op jit(solution)/shard_map/all_gather | solution.py:140
  11.6 231.2 %reduce-scatter.24.cloned.1.call-start = ((), (), s32[]{:S(2)}) async-start(), calls=%async_computation.18 | async-start | bytes 3145728 | tf_op jit(solution)/shard_map/reduce_scatter | solution.py:34
  145.1 170.8 %all-gather.45.cloned.1.call-start = ((), (), s32[]{:S(2)}) async-start(), calls=%async_computation.41 | async-start | bytes 4456448 | tf_op jit(solution)/shard_map/all_gather | solution.py:141
  146.1 169.8 %all-gather.27.cloned.1.call-start = ((), (), s32[]{:S(2)}) async-start(), calls=%async_computation.19 | async-start | bytes 3145728 | tf_op jit(solution)/shard_map/all_gather | solution.py:30
  248.1 98.3 %all-gather.47.cloned.1.call-start = ((), (), s32[]{:S(2)}) async-start(), calls=%async_computation.42 | async-start | bytes 4456448 | tf_op jit(solution)/shard_map/all_gather | solution.py:142
  249.1 143.2 %reduce-scatter.26.cloned.1.call-start = ((), (), s32[]{:S(2)}) async-start(), calls=%async_computation.20 | async-start | bytes 3145728 | tf_op jit(solution)/shard_map/reduce_scatter | solution.py:34
  355.8 84.4 %all-gather.49.cloned.1.call-start = ((), (), s32[]{:S(2)}) async-start(), calls=%async_computation.43 | async-start | bytes 3342336 | tf_op jit(solution)/shard_map/all_gather | solution.py:139
  356.5 117.1 %all-gather.29.cloned.1.call-start = ((), (), s32[]{:S(2)}) async-start(), calls=%async_computation.21 | async-start | bytes 3145728 | tf_op jit(solution)/shard_map/all_gather | solution.py:30
  397.3 115.5 %all-gather.51.cloned.1.call-start = ((), (), s32[]{:S(2)}) async-start(), calls=%async_computation.44 | async-start | bytes 1114112 | tf_op jit(solution)/shard_map/all_gather | solution.py:140
  398.0 150.8 %reduce-scatter.28.cloned.1.call-start = ((), (), s32[]{:S(2)}) async-start(), calls=%async_computation.22 | async-start | bytes 3145728 | tf_op jit(solution)/shard_map/reduce_scatter | solution.py:34
  517.0 85.6 %all-gather.53.cloned.1.call-start = ((), (), s32[]{:S(2)}) async-start(), calls=%async_computation.45 | async-start | bytes 4456448 | tf_op jit(solution)/shard_map/all_gather | solution.py:141
  517.8 118.5 %all-gather.31.cloned.1.call-start = ((), (), s32[]{:S(2)}) async-start(), calls=%async_computation.23 | async-start | bytes 3145728 | tf_op jit(solution)/shard_map/all_gather | solution.py:30
  553.4 135.9 %all-gather.55.cloned.1.call-start = ((), (), s32[]{:S(2)}) async-start(), calls=%async_computation.46 | async-start | bytes 4456448 | tf_op jit(solution)/shard_map/all_gather | solution.py:142
  554.0 175.2 %reduce-scatter.30.cloned.1.call-start = ((), (), s32[]{:S(2)}) async-start(), calls=%async_computation.24 | async-start | bytes 3145728 | tf_op jit(solution)/shard_map/reduce_scatter | solution.py:34
  737.3 84.3 %reduce-scatter.32.cloned.1.call-start = ((), (), s32[]{:S(2)}) async-start(), calls=%async_computation.26 | async-start | bytes 3145728 | tf_op jit(solution)/shard_map/reduce_scatter | solution.py:34
  828.8 115.4 %reduce-scatter.34.cloned.1.call-start = ((), (), s32[]{:S(2)}) async-start(), calls=%async_computation.28 | async-start | bytes 3145728 | tf_op jit(solution)/shard_map/reduce_scatter | solution.py:34
  912.3 72.5 %all-gather.37.cloned.1.call-start = ((), (), s32[]{:S(2)}) async-start(), calls=%async_computation.29 | async-start | bytes 3145728 | tf_op jit(solution)/shard_map/all_gather | solution.py:30
  951.5 83.8 %reduce-scatter.36.cloned.1.call-start = ((), (), s32[]{:S(2)}) async-start(), calls=%async_computation.30 | async-start | bytes 3145728 | tf_op jit(solution)/shard_map/reduce_scatter | solution.py:34
  1003.3 86.8 %all-gather.39.cloned.1.call-start = ((), (), s32[]{:S(2)}) async-start(), calls=%async_computation.31 | async-start | bytes 3145728 | tf_op jit(solution)/shard_map/all_gather | solution.py:30
  1043.8 159.2 %reduce-scatter.56.cloned.1.call-start = ((), (), s32[]{:S(2)}) async-start(), calls=%async_computation.49 | async-start | bytes 2162688
  1046.1 290.2 %reduce-scatter.52.cloned.1.call-start = ((), (), s32[]{:S(2)}) async-start(), calls=%async_computation.47 | async-start | bytes 540672
  1048.1 373.7 %reduce-scatter.50.cloned.1.call-start = ((), (), s32[]{:S(2)}) async-start(), calls=%async_computation.38 | async-start | bytes 4456448 | tf_op jit(solution)/shard_map/reduce_scatter | solution.py:292
  1058.1 438.9 %reduce-scatter.48.cloned.1.call-start = ((), (), s32[]{:S(2)}) async-start(), calls=%async_computation.37 | async-start | bytes 4456448 | tf_op jit(solution)/shard_map/reduce_scatter | solution.py:292
  1068.0 505.2 %reduce-scatter.46.cloned.1.call-start = ((), (), s32[]{:S(2)}) async-start(), calls=%async_computation.36 | async-start | bytes 4456448 | tf_op jit(solution)/shard_map/reduce_scatter | solution.py:289
  1077.9 570.6 %reduce-scatter.44.cloned.1.call-start = ((), (), s32[]{:S(2)}) async-start(), calls=%async_computation.35 | async-start | bytes 4456448 | tf_op jit(solution)/shard_map/reduce_scatter | solution.py:289
  1089.9 681.1 %reduce-scatter.54.cloned.1.call-start = ((), (), s32[]{:S(2)}) async-start(), calls=%async_computation.48 | async-start | bytes 540672
  1133.4 707.7 %reduce-scatter.42.cloned.1.call-start = ((), (), s32[]{:S(2)}) async-start(), calls=%async_computation.34 | async-start | bytes 1114112 | tf_op jit(solution)/shard_map/reduce_scatter | solution.py:286
  1137.4 764.2 %reduce-scatter.40.cloned.1.call-start = ((), (), s32[]{:S(2)}) async-start(), calls=%async_computation.33 | async-start | bytes 1114112 | tf_op jit(solution)/shard_map/reduce_scatter | solution.py:286
  1142.1 932.5 %all-reduce.5.cloned.1.call-start = ((), (), s32[]{:S(2)}) async-start(), calls=%async_computation.50 | async-start | bytes 16777216
  1171.1 938.3 %reduce-scatter.38.cloned.1.call-start = ((), (), s32[]{:S(2)}) async-start(), calls=%async_computation.32 | async-start | bytes 3145728 | tf_op jit(solution)/shard_map/reduce_scatter | solution.py:34
  (105 other events, 5224.0 us)
Sparse Core Ops, SparseCore 0:
  9.6 44.4 all-gather.24
  56.8 45.8 all-gather.40
  105.4 35.3 all-gather.42
  145.3 46.8 reduce-scatter.23
  195.0 51.7 all-gather.44
  248.8 43.9 all-gather.26
  295.8 50.5 all-gather.46
  355.9 36.3 reduce-scatter.25
  394.5 45.5 all-gather.48
  475.8 36.9 all-gather.50
  517.1 31.6 reduce-scatter.27
  551.8 50.7 all-gather.52
  604.7 31.5 all-gather.30
  638.5 50.7 all-gather.54
  737.5 33.0 all-gather.32
  789.8 31.8 reduce-scatter.31
  828.9 33.1 all-gather.34
  912.4 31.8 reduce-scatter.33
  951.6 33.1 all-gather.36
  1003.4 31.8 reduce-scatter.35
  1043.9 33.1 all-gather.38
  1079.3 123.6 reduce-scatter.55
  1205.8 130.4 reduce-scatter.51
  1340.5 81.2 reduce-scatter.49
  1425.5 71.4 reduce-scatter.47
  1501.3 71.7 reduce-scatter.45
  1577.0 71.4 reduce-scatter.43
  1650.7 120.2 reduce-scatter.53
  1774.6 66.5 reduce-scatter.41
  1845.2 56.3 reduce-scatter.39
  1905.3 169.2 all-reduce.4
  2077.5 31.8 reduce-scatter.37
  (2 shorter events, 61.7 us)
where the time goes:
time: 2130 us; the launch traced here: 2120 us
  waiting for transfers between devices  1410 us (66%)
  matrix products  253 us (12%)
  blocking collectives  202 us (9%)
  local copies, waits for them, and re-layouts  158 us (7%)
  other arithmetic  73.7 us (3%)
    unnamed x38, waiting for transfers between devices  449 us
    reduce_scatter x8, waiting for transfers between devices, reduce_rows(): lax.psum_scatter(term_fn(jnp.int32(0), row_count * lax.axis_size('tensor'...  224 us
    all_gather x8, waiting for transfers between devices, collect(): return lax.all_gather(local_rows, 'tensor', axis=0, tiled=True)  166 us
    reduce_scatter x2, waiting for transfers between devices, on_device(): lax.psum_scatter(grad_down.astype(jnp.bfloat16), 'dp', scatter_dimension=...  159 us
    reduce_scatter x2, waiting for transfers between devices, on_device(): lax.psum_scatter(grad_up.astype(jnp.bfloat16), 'dp', scatter_dimension=0,...  149 us
    reduce_scatter x2, waiting for transfers between devices, on_device(): lax.psum_scatter(grad_out.astype(jnp.bfloat16), 'dp', scatter_dimension=1...  129 us
    all_gather x1, blocking collectives, on_device(): lax.all_gather(norm_gains, ('dp', 'tensor'), axis=2, tiled=True)  69.6 us
    all_gather x1, blocking collectives, on_device(): lax.all_gather(ff_bias, ('dp', 'tensor'), axis=1, tiled=True)  66.1 us
  transfers between devices with their start and end apart: 34, of which 28 were waited for; matrix products, arithmetic and copies ran while one was open for 15% of the time, Pallas kernels for 0%

commit v1 on v0

v1 whole, which is shorter than its diff:
```python
from functools import partial

import jax
import jax.numpy as jnp
import numpy as np
from jax import lax
from jax.experimental import pallas as pl
from jax.experimental.pallas import tpu as pltpu
from jax.sharding import Mesh
from jax.sharding import PartitionSpec as P

HD = 64
EPSILON = 1e-06
HALF_ROOT = 0.7071067811865476
INV_ROOT_TAU = 0.3989422804014327
BF = jnp.bfloat16
F32 = jnp.float32
RANKS = ("dp", "thi", "tlo")
SPREAD = ("thi", "tlo", "dp")


def norm_parts(summed):
    centre = summed - jnp.mean(summed, axis=-1, keepdims=True)
    spread = jnp.mean(centre * centre, axis=-1, keepdims=True)
    rate = lax.rsqrt(spread + EPSILON)
    return centre * rate, rate


def norm_back(grad, unit, rate, gain):
    scaled = grad * gain
    return rate * (
        scaled
        - jnp.mean(scaled, axis=-1, keepdims=True)
        - unit * jnp.mean(scaled * unit, axis=-1, keepdims=True)
    )


def gelu_slope(hidden_in):
    return (
        0.5 * (1.0 + lax.erf(hidden_in * HALF_ROOT))
        + hidden_in * jnp.exp(-0.5 * hidden_in * hidden_in) * INV_ROOT_TAU
    )


def dot(a, b):
    return jnp.dot(a, b, preferred_element_type=F32)


def dot_nt(a, b):
    return lax.dot_general(a, b, (((1,), (1,)), ((), ())), preferred_element_type=F32)


def dot_tn(a, b):
    return lax.dot_general(a, b, (((0,), (0,)), ((), ())), preferred_element_type=F32)


def attend_kernel(q_ref, k_ref, v_ref, segq_ref, segk_ref, out_ref):
    same = segq_ref[0] == segk_ref[0]
    outs = []
    for half in range(q_ref.shape[1] // HD):
        cols = slice(half * HD, half * HD + HD)
        q = (q_ref[:, cols].astype(F32) * HD ** (-0.5)).astype(BF)
        scores = jnp.where(same, dot_nt(q, k_ref[:, cols]), -jnp.inf)
        top = jnp.max(scores, axis=-1, keepdims=True)
        weights = jnp.exp(scores - top)
        total = jnp.sum(weights, axis=-1, keepdims=True)
        probs = (weights * (1.0 / total)).astype(BF)
        outs.append(dot(probs, v_ref[:, cols]))
    out_ref[...] = jnp.concatenate(outs, axis=1).astype(BF)


def attend_back_kernel(q_ref, k_ref, v_ref, grad_ref, segq_ref, segk_ref, dq_ref, dk_ref, dv_ref):
    same = segk_ref[0] == segq_ref[0]
    dqs, dks, dvs = [], [], []
    for half in range(q_ref.shape[1] // HD):
        cols = slice(half * HD, half * HD + HD)
        q = (q_ref[:, cols].astype(F32) * HD ** (-0.5)).astype(BF)
        k, v, grad = k_ref[:, cols], v_ref[:, cols], grad_ref[:, cols]
        scores = jnp.where(same, dot_nt(k, q), -jnp.inf)
        top = jnp.max(scores, axis=0, keepdims=True)
        weights = jnp.exp(scores - top)
        probs = weights * (1.0 / jnp.sum(weights, axis=0, keepdims=True))
        dvs.append(dot(probs.astype(BF), grad))
        grad_probs = dot_nt(v, grad)
        inner = jnp.sum(grad_probs * probs, axis=0, keepdims=True)
        grad_scores = (probs * (grad_probs - inner)).astype(BF)
        dks.append(dot(grad_scores, q))
        dqs.append(dot_tn(grad_scores, k) * HD ** (-0.5))
    dq_ref[...] = jnp.concatenate(dqs, axis=1).astype(dq_ref.dtype)
    dk_ref[...] = jnp.concatenate(dks, axis=1).astype(dk_ref.dtype)
    dv_ref[...] = jnp.concatenate(dvs, axis=1).astype(dv_ref.dtype)


def pair_width(cols):
    return 128 if cols % 128 == 0 else cols


def attend(q, k, v, offsets, cols, seg_q, seg_k):
    sets = seg_q.shape[0]
    rows, keys = q.shape[0] // sets, k.shape[0] // sets
    wide = pair_width(cols)
    spec = lambda n, off: pl.BlockSpec((n, wide), lambda s, j, off=off: (s, off // wide + j))
    heads = cols // HD
    return pl.pallas_call(
        attend_kernel,
        grid=(sets, cols // wide),
        in_specs=[
            spec(rows, offsets[0]),
            spec(keys, offsets[1]),
            spec(keys, offsets[2]),
            pl.BlockSpec((1, rows, 1), lambda s, j: (s, 0, 0)),
            pl.BlockSpec((1, 1, keys), lambda s, j: (s, 0, 0)),
        ],
        out_specs=spec(rows, 0),
        out_shape=jax.ShapeDtypeStruct((q.shape[0], cols), BF),
        cost_estimate=pl.CostEstimate(
            flops=4 * heads * sets * rows * keys * HD * 4,
            bytes_accessed=8 * q.shape[0] * cols,
            transcendentals=heads * sets * rows * keys,
        ),
        name="attend",
    )(q, k, v, seg_q[:, :, None], seg_k[:, None, :])


def attend_back(q, k, v, offsets, cols, grad, seg_q, seg_k, kv_type):
    sets = seg_q.shape[0]
    rows, keys = q.shape[0] // sets, k.shape[0] // sets
    wide = pair_width(cols)
    spec = lambda n, off: pl.BlockSpec((n, wide), lambda s, j, off=off: (s, off // wide + j))
    heads = cols // HD
    return pl.pallas_call(
        attend_back_kernel,
        grid=(sets, cols // wide),
        in_specs=[
            spec(rows, offsets[0]),
            spec(keys, offsets[1]),
            spec(keys, offsets[2]),
            spec(rows, 0),
            pl.BlockSpec((1, 1, rows), lambda s, j: (s, 0, 0)),
            pl.BlockSpec((1, keys, 1), lambda s, j: (s, 0, 0)),
        ],
        out_specs=[spec(rows, 0), spec(keys, 0), spec(keys, 0)],
        out_shape=[
            jax.ShapeDtypeStruct((q.shape[0], cols), BF),
            jax.ShapeDtypeStruct((k.shape[0], cols), kv_type),
            jax.ShapeDtypeStruct((k.shape[0], cols), kv_type),
        ],
        cost_estimate=pl.CostEstimate(
            flops=10 * heads * sets * rows * keys * HD * 4,
            bytes_accessed=14 * q.shape[0] * cols,
            transcendentals=heads * sets * rows * keys,
        ),
        name="attend_back",
    )(q, k, v, grad, seg_q[:, None, :], seg_k[:, :, None])


def swap(value, mask):
    count = lax.axis_size("dp") * lax.axis_size("thi") * lax.axis_size("tlo")
    return lax.ppermute(value, RANKS, [(i, i ^ mask) for i in range(count)])


def gather_small(row):
    count = lax.axis_size("dp") * lax.axis_size("thi") * lax.axis_size("tlo")
    held, mask = row[None], 1
    while mask < count:
        held = jnp.concatenate([held, swap(held, mask)], axis=0)
        mask *= 2
    return jnp.take(held, jnp.arange(count) ^ lax.axis_index(RANKS), axis=0)


def scatter_small(parts):
    count = parts.shape[0]
    held, mask = jnp.take(parts, jnp.arange(count) ^ lax.axis_index(RANKS), axis=0), count // 2
    while mask:
        held = held[:mask] + swap(held[mask:], mask)
        mask //= 2
    return held[0]


def gather_weights(shard):
    whole = lax.all_gather(shard, SPREAD, axis=0, tiled=True)
    parts = lax.axis_size("thi") * lax.axis_size("tlo")
    return whole.reshape(parts, whole.shape[0] // parts, whole.shape[1])


def scatter_grads(parts):
    return lax.psum_scatter(
        jnp.concatenate(parts, axis=0), SPREAD, scatter_dimension=0, tiled=True
    ).astype(F32)


def on_device(
    inputs,
    seg_ids,
    qkv_weight,
    out_weight,
    up_weight,
    down_weight,
    norm_gains,
    row_biases,
    ff_bias,
    cotangent,
):
    blocks = lax.axis_size("thi") * lax.axis_size("tlo")
    sharers = lax.axis_size("tlo")
    rows, width = inputs.shape
    layers = qkv_weight.shape[0]
    head_cols = qkv_weight.shape[3]
    hidden = up_weight.shape[2]
    length = seg_ids.shape[1]
    sets = max(1, rows // length)
    T = range(blocks)

    seg_k = lax.dynamic_slice_in_dim(seg_ids, lax.axis_index("thi") * sets, sets)
    seg_q = seg_k
    if sharers > 1:
        seg_q = lax.dynamic_slice_in_dim(seg_k, lax.axis_index("tlo") * rows, rows, axis=1)

    shards = [
        (
            jnp.concatenate([qkv_weight[l, k] for k in range(3)], axis=1).astype(BF),
            jnp.concatenate(
                [out_weight[l].T, up_weight[l], down_weight[l].T], axis=1
            ).astype(BF),
        )
        for l in range(layers)
    ]
    gathered = [[None, None] for _ in range(layers)]
    small = gather_small(
        jnp.concatenate([norm_gains.reshape(-1), row_biases.reshape(-1), ff_bias.reshape(-1)])
    )
    devices = small.shape[0]
    cuts = np.cumsum([norm_gains.size, row_biases.size])
    spread_out = lambda piece, like: jnp.moveaxis(
        piece.reshape((devices,) + like.shape), 0, -2
    ).reshape(like.shape[:-1] + (devices * like.shape[-1],))
    gain_rows = spread_out(small[:, : cuts[0]], norm_gains)
    shift_rows = spread_out(small[:, cuts[0] : cuts[1]], row_biases)
    up_shifts = spread_out(small[:, cuts[1] :], ff_bias)

    weights = []
    for l in range(layers):
        if l == 0:
            qkv = gather_weights(shards[l][0])
            rest = gather_weights(shards[l][1])
        else:
            both = gather_weights(jnp.concatenate(shards[l], axis=1))
            qkv, rest = both[:, :, : 3 * head_cols], both[:, :, 3 * head_cols :]
        out = rest[:, :, :head_cols]
        up = rest[:, :, head_cols : head_cols + hidden]
        down = rest[:, :, head_cols + hidden :]
        weights.append((qkv, out, up, down))

    stream = inputs.astype(F32)
    stored = []
    for l in range(layers):
        qkv, out, up, down = weights[l]
        shifts, gains = shift_rows[l], gain_rows[l]
        low = stream.astype(BF)
        projected, kept_keys, mixture = [], [], []
        for t in T:
            shift = jnp.concatenate(
                [
                    shifts[0, t * head_cols : (t + 1) * head_cols],
                    jnp.zeros((head_cols,), F32),
                    shifts[1, t * head_cols : (t + 1) * head_cols],
                ]
            )
            mine = (dot(low, qkv[t]) + shift).astype(BF)
            projected.append(mine)
            if sharers > 1:
                kv = lax.all_gather(mine[:, head_cols:], "tlo", axis=0, tiled=True)
                offsets = (0, 0, head_cols)
            else:
                kv, offsets = mine, (0, head_cols, 2 * head_cols)
            kept_keys.append(kv)
            mixture.append(attend(mine, kv, kv, offsets, head_cols, seg_q, seg_k))
        attended = sum(dot_nt(mixture[t], out[t]) for t in T)
        unit_early, rate_early = norm_parts(stream + (attended + shifts[2]))
        mid = unit_early * gains[0] + shifts[3]
        mid_low = mid.astype(BF)
        hidden_in = [
            dot(mid_low, up[t]) + up_shifts[l, t * hidden : (t + 1) * hidden] for t in T
        ]
        hidden_out = [jax.nn.gelu(h, approximate=False).astype(BF) for h in hidden_in]
        branch = sum(dot_nt(hidden_out[t], down[t]) for t in T)
        unit_late, rate_late = norm_parts(mid + (branch + shifts[4]))
        stored.append(
            (
                low,
                projected,
                kept_keys,
                offsets,
                mixture,
                unit_early,
                rate_early,
                mid_low,
                hidden_in,
                hidden_out,
                unit_late,
                rate_late,
            )
        )
        stream = unit_late * gains[1] + shifts[5]

    grad_stream = cotangent
    mlp_parts, attn_parts = [None] * layers, [None] * layers
    small_grads = [None] * layers
    over_rows = lambda value: jnp.sum(value.astype(F32), axis=0)
    for l in reversed(range(layers)):
        qkv, out, up, down = weights[l]
        gains = gain_rows[l]
        (
            low,
            projected,
            kept_keys,
            offsets,
            mixture,
            unit_early,
            rate_early,
            mid_low,
            hidden_in,
            hidden_out,
            unit_late,
            rate_late,
        ) = stored[l]
        grad_second = norm_back(grad_stream, unit_late, rate_late, gains[1])
        gain_late, shift_late = over_rows(grad_stream * unit_late), over_rows(grad_stream)
        second_low = grad_second.astype(BF)
        grad_down = [dot_tn(second_low, hidden_out[t]).astype(BF) for t in T]
        grad_pre = [
            (dot(second_low, down[t]) * gelu_slope(hidden_in[t])).astype(BF) for t in T
        ]
        grad_up = [dot_tn(mid_low, grad_pre[t]).astype(BF) for t in T]
        mlp_parts[l] = [jnp.concatenate([grad_up[t], grad_down[t]], axis=1) for t in T]
        grad_mid = grad_second + sum(dot_nt(grad_pre[t], up[t]) for t in T)
        grad_first = norm_back(grad_mid, unit_early, rate_early, gains[0])
        gain_early, shift_early = over_rows(grad_mid * unit_early), over_rows(grad_mid)
        first_low = grad_first.astype(BF)
        grad_out = [dot_tn(first_low, mixture[t]).astype(BF) for t in T]
        grad_proj = []
        for t in T:
            grad_mix = dot(first_low, out[t]).astype(BF)
            dq, dk, dv = attend_back(
                projected[t],
                kept_keys[t],
                kept_keys[t],
                offsets,
                head_cols,
                grad_mix,
                seg_q,
                seg_k,
                F32 if sharers > 1 else BF,
            )
            if sharers > 1:
                dk = lax.psum_scatter(dk, "tlo", scatter_dimension=0, tiled=True).astype(BF)
                dv = lax.psum_scatter(dv, "tlo", scatter_dimension=0, tiled=True).astype(BF)
            grad_proj.append((dq, dk, dv))
        grad_qkv = [
            jnp.concatenate([dot_tn(low, part).astype(BF) for part in grad_proj[t]], axis=1)
            for t in T
        ]
        attn_parts[l] = [jnp.concatenate([grad_qkv[t], grad_out[t]], axis=1) for t in T]
        grad_stream = grad_first + sum(
            dot_nt(grad_proj[t][k], qkv[t][:, k * head_cols : (k + 1) * head_cols])
            for t in T
            for k in range(3)
        )
        small_grads[l] = (
            jnp.stack([gain_early, gain_late]),
            jnp.stack(
                [
                    jnp.concatenate([over_rows(grad_proj[t][0]) for t in T]),
                    jnp.concatenate([over_rows(grad_proj[t][2]) for t in T]),
                    over_rows(grad_first),
                    shift_early,
                    over_rows(grad_second),
                    shift_late,
                ]
            ),
            jnp.concatenate([over_rows(grad_pre[t]) for t in T]),
        )
    mlp_done, attn_done = [None] * layers, [None] * layers
    for l in reversed(range(layers)):
        mlp_done[l] = scatter_grads(mlp_parts[l])
        attn_done[l] = scatter_grads(attn_parts[l])
    fold = lambda whole: jnp.moveaxis(
        whole.reshape(whole.shape[:-1] + (devices, whole.shape[-1] // devices)), -2, 0
    ).reshape(devices, -1)
    stacked = [jnp.stack([small_grads[l][i] for l in range(layers)]) for i in range(3)]
    summed = scatter_small(jnp.concatenate([fold(whole) for whole in stacked], axis=1))
    return (
        stream.astype(BF),
        grad_stream,
        jnp.stack(
            [
                jnp.stack(
                    [attn_done[l][:, k * head_cols : (k + 1) * head_cols] for k in range(3)]
                )
                for l in range(layers)
            ]
        ),
        jnp.stack([attn_done[l][:, 3 * head_cols :].T for l in range(layers)]),
        jnp.stack([mlp_done[l][:, :hidden] for l in range(layers)]),
        jnp.stack([mlp_done[l][:, hidden:].T for l in range(layers)]),
        summed[: cuts[0]].reshape(norm_gains.shape),
        summed[cuts[0] : cuts[1]].reshape(row_biases.shape),
        summed[cuts[1] :].reshape(ff_bias.shape),
    )


def solution(mesh):
    def whole(*args):
        inputs, seg_ids = args[:2]
        depth, blocks = mesh.shape["dp"], mesh.shape["tensor"]
        rows = inputs.shape[0] // (depth * blocks)
        sharers = max(1, seg_ids.shape[1] // rows)
        inner = Mesh(mesh.devices.reshape(depth, blocks // sharers, sharers), RANKS)
        tensor = ("thi", "tlo")
        row_wise = P(RANKS, None)
        weight_specs = (
            P(None, None, "dp", tensor),
            P(None, tensor, "dp"),
            P(None, "dp", tensor),
            P(None, tensor, "dp"),
            P(None, None, RANKS),
            P(None, None, RANKS),
            P(None, RANKS),
        )
        return jax.shard_map(
            on_device,
            mesh=inner,
            in_specs=(row_wise, P("dp", None)) + weight_specs + (row_wise,),
            out_specs=(row_wise, row_wise) + weight_specs,
            check_vma=False,
        )(*args)

    return whole
```

time: 2130 us -> 1290 us (0.61)
  waiting for transfers between devices: 1410 us -> 578 us
  other arithmetic: 73.7 us -> 316 us
  blocking collectives: 202 us -> 0 us
  local copies, waits for them, and re-layouts: 158 us -> 46.8 us
  Pallas kernels: 0 us -> 96.4 us
  matrix products: 253 us -> 214 us
    unnamed x38 -> x9, waiting for transfers between devices: 449 us -> 0.14 us
    reduce_scatter x14 -> x2, waiting for transfers between devices: 662 us -> 306 us  [scatter_grads(): lax.psum_scatter(jnp.concatenate(parts, axis=0), SPREAD, scatter_dimensio...]
    concatenate x0 -> x18, other arithmetic: none -> 290 us  [the longest x4 289 us: scatter_grads(): jnp.concatenate(parts, axis=0)]
    all_gather x3 -> x0, blocking collectives: 202 us -> none  [the longest x1 69.6 us: on_device(): lax.all_gather(norm_gains, ('dp', 'tensor'), axis=2, tiled=True)]
    pallas_call x0 -> x8, Pallas kernels: none -> 96.4 us  [the longest x4 49.8 us: attend_back(): pl.pallas_call(attend_back_kernel, grid=(sets, cols // wide), in_specs=[s...]
    slice x9 -> x18, local copies, waits for them, and re-layouts: 60.8 us -> 1.32 us  [the longest x1 0.57 us: on_device(): stream = unit_late * gains[1] + shifts[5]]
    all_gather x16 -> x3, waiting for transfers between devices: 301 us -> 255 us  [gather_weights(): whole = lax.all_gather(shard, SPREAD, axis=0, tiled=True)]
    dot_general x52 -> x64, matrix products: 253 us -> 214 us  [the longest x16 107 us: dot(): return jnp.dot(a, b, preferred_element_type=F32)]
  transfers between devices with their start and end apart: 34 -> 17, of which waited for: 28 -> 15; matrix products, arithmetic and copies ran while one was open for 15% -> 30% of each run, Pallas kernels for 0% -> 4%
where the time goes in v1:
time: 1290 us; the launch traced here: 1280 us
  waiting for transfers between devices  578 us (45%)
  other arithmetic  316 us (24%)
  matrix products  214 us (17%)
  Pallas kernels  96.4 us (7%)
  local copies, waits for them, and re-layouts  46.8 us (4%)
  between operations  16.6 us (1%)
    reduce_scatter x2, waiting for transfers between devices, scatter_grads(): lax.psum_scatter(jnp.concatenate(parts, axis=0), SPREAD, scatter_dimensio...  306 us
    concatenate x4, other arithmetic, scatter_grads(): jnp.concatenate(parts, axis=0)  289 us
    all_gather x3, waiting for transfers between devices, gather_weights(): whole = lax.all_gather(shard, SPREAD, axis=0, tiled=True)  255 us
    dot_general x16, matrix products, dot(): return jnp.dot(a, b, preferred_element_type=F32)  107 us
    dot_general x24, matrix products, dot_nt(): lax.dot_general(a, b, (((1,), (1,)), ((), ())), preferred_element_type=F32)  56.8 us
    dot_general x24, matrix products, dot_tn(): lax.dot_general(a, b, (((0,), (0,)), ((), ())), preferred_element_type=F32)  51 us
    pallas_call x4, Pallas kernels, attend_back(): pl.pallas_call(attend_back_kernel, grid=(sets, cols // wide), in_specs=[s...  49.8 us
    pallas_call x4, Pallas kernels, attend(): pl.pallas_call(attend_kernel, grid=(sets, cols // wide), in_specs=[spec(r...  46.7 us
  transfers between devices with their start and end apart: 17, of which 15 were waited for; matrix products, arithmetic and copies ran while one was open for 30% of the time, Pallas kernels for 4%

profile of v1, /device:TPU:8, one launch (start us, length us, event | category | flops | bytes accessed | tf_op | source)
XLA Modules:
  0.0 1279.9 jit_solution(4877159760008336204)
XLA Ops:
  36.8 46.3 %all-gather.4.cloned.1.call-done = bf16[2048,1536]{1,0:T(8,128)(2,1)} async-done(((bf16[64,1536]{1,0:T(8,128)(2,1)}), bf16[2048,1536]{1,0:T(8,128)(2,1)}) %all-gather.4.cloned.1.call-update) | async-done | bytes 6291472 | tf_op jit(solution)/shard_map/all_gather | solution.py:181
  88.0 11.8 attend.5
  99.7 4.9 fusion.93.q_ref.k_ref.v_ref
  104.7 11.6 attend.4
  116.3 92.0 %all-gather.6.cloned.1.call-done = bf16[2048,4608]{1,0:T(8,128)(2,1)} async-done(((bf16[64,4608]{1,0:T(8,128)(2,1)}), bf16[2048,4608]{1,0:T(8,128)(2,1)}) %all-gather.6.cloned.1.call-update) | async-done | bytes 18874384 | tf_op jit(solution)/shard_map/all_gather | solution.py:181
  213.5 15.3 %fusion.2 = (bf16[512,2048]{1,0:T(8,128)(2,1)S(1)}, f32[512,2048]{1,0:T(8,128)}) fusion(f32[2048]{0:T(1024)S(1)} %bitcast.375, bf16[512,1024]{1,0:T(8,128)(2,1)S(1)} %fusion.96, bf16[2,1024,4608]{2,1,0:T(8,128)(2,1)} %bitcast.346), kind=kOutput, calls=%fused_computation.16 | convolution fusion | flops 2216689664 | bytes 11542528 | tf_op jit(solution)/shard_map/dot_general | solution.py:46
  231.3 12.6 fusion.5
  247.4 116.7 %all-gather.8.cloned.1.call-done = bf16[2048,6144]{1,0:T(8,128)(2,1)} async-done(((bf16[64,6144]{1,0:T(8,128)(2,1)}), bf16[2048,6144]{1,0:T(8,128)(2,1)}) %all-gather.8.cloned.1.call-update) | async-done | bytes 25165840 | tf_op jit(solution)/shard_map/all_gather | solution.py:181
  368.9 11.6 attend.7
  380.5 4.9 fusion.82.q_ref.k_ref.v_ref
  385.4 11.6 attend.6
  402.2 13.3 %fusion.11 = (bf16[512,2048]{1,0:T(8,128)(2,1)S(1)}, f32[512,2048]{1,0:T(8,128)S(1)}) fusion(f32[2048]{0:T(1024)S(1)} %bitcast.379, bf16[512,1024]{1,0:T(8,128)(2,1)S(1)} %fusion.98, bf16[2,1024,6144]{2,1,0:T(8,128)(2,1)} %bitcast.330), kind=kOutput, calls=%fused_computation.25 | convolution fusion | flops 2216689664 | bytes 11542528 | tf_op jit(solution)/shard_map/dot_general | solution.py:46
  415.6 13.5 %fusion.8 = (bf16[512,2048]{1,0:T(8,128)(2,1)S(1)}, f32[512,2048]{1,0:T(8,128)S(1)}) fusion(f32[2048]{0:T(1024)S(1)} %bitcast.377, bf16[512,1024]{1,0:T(8,128)(2,1)S(1)} %fusion.98, bf16[2,1024,6144]{2,1,0:T(8,128)(2,1)} %bitcast.331), kind=kOutput, calls=%fused_computation.22 | convolution fusion | flops 2216689664 | bytes 11542528 | tf_op jit(solution)/shard_map/dot_general | solution.py:46
  429.1 5.3 fusion.75
  434.5 5.2 fusion.150
  444.1 6.4 convert_reduce_fusion
  450.5 6.7 convert_reduce_fusion.1
  457.2 5.3 fusion.72
  462.6 6.1 multiply_reduce_fusion.1
  479.1 12.3 attend_back.4
  491.5 12.4 attend_back.5
  511.2 71.9 %maximum_maximum_fusion.3 = bf16[2048,2048]{0,1:T(8,128)(2,1)} fusion(bf16[1024,512]{0,1:T(8,128)(2,1)S(1)} %copy-done.21, bf16[1024,512]{0,1:T(8,128)(2,1)S(1)} %convolution_convert_fusion.9, bf16[1024,512]{0,1:T(8,128)(2,1)S(1)} %convolution_convert_fusion.10, bf16[1024,512]{0,1:T(8,128)(2,1)S(1)} %convolution_convert_fusion.11, ...), kind=kLoop, calls=%fused_computation.5 | loop fusion | flops 67108864 | bytes 16777216 | tf_op jit(solution)/shard_map/concatenate | solution.py:188
  583.1 12.3 copy.60
  606.0 6.8 convert_reduce_fusion.3
  630.8 12.7 attend_back.6
  651.6 12.3 attend_back.7
  669.4 71.9 %maximum_maximum_fusion.2 = bf16[2048,2048]{0,1:T(8,128)(2,1)} fusion(bf16[1024,512]{0,1:T(8,128)(2,1)S(1)} %copy-done.19, bf16[1024,512]{0,1:T(8,128)(2,1)S(1)} %fusion.104, bf16[1024,512]{0,1:T(8,128)(2,1)S(1)} %fusion.103, bf16[1024,512]{0,1:T(8,128)(2,1)S(1)} %fusion.102, bf16[1024,512]{0,1:T(8,128)(2,1)S(1)} %copy-done.20, ...), kind=kLoop, calls=%fused_computation.4 | loop fusion | flops 67108864 | bytes 16777216 | tf_op jit(solution)/shard_map/concatenate | solution.py:188
  741.3 12.3 copy.58
  765.7 72.4 %maximum_maximum_fusion = bf16[2048,4096]{1,0:T(8,128)(2,1)} fusion(bf16[1024,2048]{1,0:T(8,128)(2,1)S(1)} %convolution_convert_fusion.4, bf16[1024,2048]{1,0:T(8,128)(2,1)S(1)} %convolution_convert_fusion.5, bf16[1024,2048]{1,0:T(8,128)(2,1)S(1)} %convolution_convert_fusion.6, bf16[1024,2048]{1,0:T(8,128)(2,1)S(1)} %convolution_convert_fusion.7), kind=kLoop, calls=%fused_computation.2 | loop fusion | flops 67108864 | bytes 33554432 | tf_op jit(solution)/shard_map/concatenate | solution.py:188
  850.2 72.4 %maximum_maximum_fusion.1 = bf16[2048,4096]{1,0:T(8,128)(2,1)} fusion(bf16[1024,2048]{1,0:T(8,128)(2,1)S(1)} %convolution_convert_fusion, bf16[1024,2048]{1,0:T(8,128)(2,1)S(1)} %convolution_convert_fusion.1, bf16[1024,2048]{1,0:T(8,128)(2,1)S(1)} %convolution_convert_fusion.2, bf16[1024,2048]{1,0:T(8,128)(2,1)S(1)} %convolution_convert_fusion.3), kind=kLoop, calls=%fused_computation.3 | loop fusion | flops 67108864 | bytes 33554432 | tf_op jit(solution)/shard_map/concatenate | solution.py:188
  962.3 121.0 %reduce-scatter.9.cloned.1.call-done = bf16[64,4096]{1,0:T(8,128)(2,1)} async-done(((bf16[2048,4096]{1,0:T(8,128)(2,1)}), bf16[64,4096]{1,0:T(8,128)(2,1)}) %reduce-scatter.9.cloned.1.call-update) | async-done | bytes 524304 | tf_op jit(solution)/shard_map/reduce_scatter | solution.py:187
  1084.5 184.9 %reduce-scatter.11.cloned.1.call-done = bf16[64,4096]{1,0:T(8,128)(2,1)} async-done(((bf16[2048,4096]{1,0:T(8,128)(2,1)}), bf16[64,4096]{1,0:T(8,128)(2,1)}) %reduce-scatter.11.cloned.1.call-update) | async-done | bytes 524304 | tf_op jit(solution)/shard_map/reduce_scatter | solution.py:187
  (466 shorter events, 186.3 us)
Async XLA Ops:
  7.2 75.9 %all-gather.4.cloned.1.call-start = ((), (), s32[]{:S(2)}) async-start(), calls=%async_computation.4 | async-start | bytes 6488064 | tf_op jit(solution)/shard_map/all_gather | solution.py:181
  9.2 199.1 %all-gather.6.cloned.1.call-start = ((), (), s32[]{:S(2)}) async-start(), calls=%async_computation.5 | async-start | bytes 19464192 | tf_op jit(solution)/shard_map/all_gather | solution.py:181
  11.8 71.3 %copy-start.33 = (bf16[512,1024]{1,0:T(8,128)(2,1)S(1)}, bf16[512,1024]{1,0:T(8,128)(2,1)}, u32[]{:S(2)}) copy-start(bf16[512,1024]{1,0:T(8,128)(2,1)} %param.12) | copy-start | bytes 3145732
  12.7 351.5 %all-gather.8.cloned.1.call-start = ((), (), s32[]{:S(2)}) async-start(), calls=%async_computation.6 | async-start | bytes 25952256 | tf_op jit(solution)/shard_map/all_gather | solution.py:181
  13.7 943.3 %reduce-scatter.15.cloned.1.call-start = ((), (), s32[]{:S(2)}) async-start(), calls=%async_computation.10 | async-start | bytes 8650752
  14.0 3.7 collective-permute-start
  17.7 1.2 collective-permute-start.1
  18.9 3.8 collective-permute-start.2
  22.7 3.9 collective-permute-start.3
  26.6 5.5 collective-permute-start.4
  34.6 209.3 %copy-start.47 = (f32[1024]{0:T(1024)}, f32[1024]{0:T(1024)S(1)}, u32[]{:S(2)}) copy-start(f32[1024]{0:T(1024)S(1)} %mul.316) | copy-start | bytes 12292
  36.8 176.7 %copy-start.63 = (f32[1,2048]{1,0:T(1,128)}, f32[1,2048]{1,0:T(1,128)S(1)}, u32[]{:S(2)}) copy-start(f32[1,2048]{1,0:T(1,128)S(1)} %get-tuple-element.120) | copy-start | bytes 24580
  36.8 194.5 %copy-start.61 = (f32[1,2048]{1,0:T(1,128)}, f32[1,2048]{1,0:T(1,128)S(1)}, u32[]{:S(2)}) copy-start(f32[1,2048]{1,0:T(1,128)S(1)} %get-tuple-element.119) | copy-start | bytes 24580
  104.7 105.8 %copy-start.45 = (bf16[512,512]{1,0:T(8,128)(2,1)S(1)}, bf16[512,512]{1,0:T(8,128)(2,1)}, u32[]{:S(2)}) copy-start(bf16[512,512]{1,0:T(8,128)(2,1)} %attend.5) | copy-start | bytes 1572868
  212.7 31.3 %copy-start = (f32[512,1024]{1,0:T(8,128)}, f32[512,1024]{1,0:T(8,128)S(1)}, u32[]{:S(2)}) copy-start(f32[512,1024]{1,0:T(8,128)S(1)} %get-tuple-element.136) | copy-start | bytes 6291460
  212.7 31.3 %copy-start.50 = (f32[512]{0:T(512)}, f32[512]{0:T(512)S(1)}, u32[]{:S(2)}) copy-start(f32[512]{0:T(512)S(1)} %broadcast_multiply_fusion.11) | copy-start | bytes 6148
  213.0 30.9 %copy-start.52 = (f32[512]{0:T(512)}, f32[512]{0:T(512)S(1)}, u32[]{:S(2)}) copy-start(f32[512]{0:T(512)S(1)} %add_rsqrt_fusion.3) | copy-start | bytes 6148
  213.0 15.8 %slice-start.2 = ((s8[18874368]{0:T(1024)(128)(4,1)}), s8[4194304]{0:T(1024)(128)(4,1)S(1)}, s32[]{:S(2)}) async-start(s8[18874368]{0:T(1024)(128)(4,1)} %bitcast.348), calls=%async_computation.13 | async-start | bytes 8388608
  213.5 17.8 %copy-start.27 = (bf16[512,1024]{1,0:T(8,128)(2,1)}, bf16[512,1024]{1,0:T(8,128)(2,1)S(1)}, u32[]{:S(2)}) copy-start(bf16[512,1024]{1,0:T(8,128)(2,1)S(1)} %fusion.96) | copy-start | bytes 3145732
  213.5 15.4 %slice-start.3 = ((s8[18874368]{0:T(1024)(128)(4,1)}), s8[4194304]{0:T(1024)(128)(4,1)S(1)}, s32[]{:S(2)}) async-start(s8[18874368]{0:T(1024)(128)(4,1)} %bitcast.348), calls=%async_computation.14 | async-start | bytes 8388608
  213.5 15.4 %slice-start.4 = ((s8[18874368]{0:T(1024)(128)(4,1)}), s8[4194304]{0:T(1024)(128)(4,1)S(1)}, s32[]{:S(2)}) async-start(s8[18874368]{0:T(1024)(128)(4,1)} %bitcast.348), calls=%async_computation.15 | async-start | bytes 8388608
  213.5 15.4 %slice-start.5 = ((s8[18874368]{0:T(1024)(128)(4,1)}), s8[4194304]{0:T(1024)(128)(4,1)S(1)}, s32[]{:S(2)}) async-start(s8[18874368]{0:T(1024)(128)(4,1)} %bitcast.348), calls=%async_computation.16 | async-start | bytes 8388608
  247.4 133.1 %copy-start.31 = (bf16[512,1024]{1,0:T(8,128)(2,1)}, bf16[512,1024]{1,0:T(8,128)(2,1)S(1)}, u32[]{:S(2)}) copy-start(bf16[512,1024]{1,0:T(8,128)(2,1)S(1)} %fusion.97) | copy-start | bytes 3145732
  415.5 18.9 %copy-start.80 = (bf16[512,2048]{1,0:T(8,128)(2,1)}, bf16[512,2048]{1,0:T(8,128)(2,1)S(1)}, u32[]{:S(2)}) copy-start(bf16[512,2048]{1,0:T(8,128)(2,1)S(1)} %get-tuple-element.147) | copy-start | bytes 6291460
  595.5 362.9 %reduce-scatter.13.cloned.1.call-start = ((), (), s32[]{:S(2)}) async-start(), calls=%async_computation.9 | async-start | bytes 8650752
  753.7 329.6 %reduce-scatter.9.cloned.1.call-start = ((), (), s32[]{:S(2)}) async-start(), calls=%async_computation.7 | async-start | bytes 17301504 | tf_op jit(solution)/shard_map/reduce_scatter | solution.py:187
  838.1 431.3 %reduce-scatter.11.cloned.1.call-start = ((), (), s32[]{:S(2)}) async-start(), calls=%async_computation.8 | async-start | bytes 17301504 | tf_op jit(solution)/shard_map/reduce_scatter | solution.py:187
  933.8 7.9 collective-permute-start.5
  941.7 3.9 collective-permute-start.6
  945.6 4.5 collective-permute-start.7
  950.1 1.2 collective-permute-start.8
  951.4 3.7 collective-permute-start.9
  (88 other events, 451.8 us)
Sparse Core Ops, SparseCore 0:
  11.5 71.5 all-gather.3
  86.6 121.7 all-gather.5
  211.8 152.2 all-gather.7
  595.6 139.0 reduce-scatter.14
  753.8 138.6 reduce-scatter.12
  894.6 188.6 reduce-scatter.8
  1085.6 183.8 reduce-scatter.10

commit v2 on v1

v2 whole, which is shorter than its diff:
```python
from functools import partial

import jax
import jax.numpy as jnp
import numpy as np
from jax import lax
from jax.experimental import pallas as pl
from jax.experimental.pallas import tpu as pltpu
from jax.sharding import Mesh
from jax.sharding import PartitionSpec as P

HD = 64
EPSILON = 1e-06
HALF_ROOT = 0.7071067811865476
INV_ROOT_TAU = 0.3989422804014327
BF = jnp.bfloat16
F32 = jnp.float32
RANKS = ("dp", "thi", "tlo")
SPREAD = ("thi", "tlo", "dp")


def norm_parts(summed):
    centre = summed - jnp.mean(summed, axis=-1, keepdims=True)
    spread = jnp.mean(centre * centre, axis=-1, keepdims=True)
    rate = lax.rsqrt(spread + EPSILON)
    return centre * rate, rate


def norm_back(grad, unit, rate, gain):
    scaled = grad * gain
    return rate * (
        scaled
        - jnp.mean(scaled, axis=-1, keepdims=True)
        - unit * jnp.mean(scaled * unit, axis=-1, keepdims=True)
    )


def dot(a, b):
    return jnp.dot(a, b, preferred_element_type=F32)


def dot_nt(a, b):
    return lax.dot_general(a, b, (((1,), (1,)), ((), ())), preferred_element_type=F32)


def dot_tn(a, b):
    return lax.dot_general(a, b, (((0,), (0,)), ((), ())), preferred_element_type=F32)


def attend_kernel(q_ref, k_ref, v_ref, segq_ref, segk_ref, out_ref):
    same = segk_ref[0] == segq_ref[0]
    outs = []
    for half in range(q_ref.shape[1] // HD):
        cols = slice(half * HD, half * HD + HD)
        q = (q_ref[:, cols].astype(F32) * HD ** (-0.5)).astype(BF)
        scores = jnp.where(same, dot_nt(k_ref[:, cols], q), -jnp.inf)
        top = jnp.max(scores, axis=0, keepdims=True)
        weights = jnp.exp(scores - top)
        total = jnp.sum(weights, axis=0, keepdims=True)
        probs = (weights * (1.0 / total)).astype(BF)
        outs.append(dot_tn(probs, v_ref[:, cols]))
    out_ref[...] = jnp.concatenate(outs, axis=1).astype(BF)


def attend_back_kernel(q_ref, k_ref, v_ref, grad_ref, segq_ref, segk_ref, *out_refs):
    same = segk_ref[0] == segq_ref[0]
    found = [], [], []
    for half in range(q_ref.shape[1] // HD):
        cols = slice(half * HD, half * HD + HD)
        q = (q_ref[:, cols].astype(F32) * HD ** (-0.5)).astype(BF)
        k, v, grad = k_ref[:, cols], v_ref[:, cols], grad_ref[:, cols]
        scores = jnp.where(same, dot_nt(k, q), -jnp.inf)
        top = jnp.max(scores, axis=0, keepdims=True)
        weights = jnp.exp(scores - top)
        probs = weights * (1.0 / jnp.sum(weights, axis=0, keepdims=True))
        grad_probs = dot_nt(v, grad)
        inner = jnp.sum(grad_probs * probs, axis=0, keepdims=True)
        grad_scores = (probs * (grad_probs - inner)).astype(BF)
        found[0].append(dot_tn(grad_scores, k) * HD ** (-0.5))
        found[1].append(dot(grad_scores, q))
        found[2].append(dot(probs.astype(BF), grad))
    for i in range(3):
        target = out_refs[0].at[i] if len(out_refs) == 1 else out_refs[i]
        target[...] = jnp.concatenate(found[i], axis=1).astype(target.dtype)


def attention_specs(rows, keys, cols):
    wide = 128 if cols % 128 == 0 else cols
    pairs = cols // wide
    part = lambda n, k: pl.BlockSpec(
        (n, wide), lambda s, j: (s, (j // pairs * 3 + k) * pairs + j % pairs)
    )
    plain = lambda n: pl.BlockSpec((n, wide), lambda s, j: (s, j))
    segs = [
        pl.BlockSpec((1, 1, rows), lambda s, j: (s, 0, 0)),
        pl.BlockSpec((1, keys, 1), lambda s, j: (s, 0, 0)),
    ]
    return wide, pairs, [part(rows, 0), part(keys, 1), part(keys, 2)], plain, segs


def attend(q, kv, cols, seg_q, seg_k):
    sets, parts = seg_q.shape[0], q.shape[1] // (3 * cols)
    rows, keys = q.shape[0] // sets, kv.shape[0] // sets
    _, pairs, specs, plain, segs = attention_specs(rows, keys, cols)
    work = parts * cols // HD * sets * rows * keys
    return pl.pallas_call(
        attend_kernel,
        grid=(sets, parts * pairs),
        in_specs=specs + segs,
        out_specs=plain(rows),
        out_shape=jax.ShapeDtypeStruct((q.shape[0], parts * cols), BF),
        cost_estimate=pl.CostEstimate(
            flops=16 * work * HD, bytes_accessed=2 * q.size * 2, transcendentals=work
        ),
        name="attend",
    )(q, kv, kv, seg_q[:, None, :], seg_k[:, :, None])


def attend_back(q, kv, cols, grad, seg_q, seg_k):
    sets, parts = seg_q.shape[0], q.shape[1] // (3 * cols)
    rows, keys = q.shape[0] // sets, kv.shape[0] // sets
    wide, pairs, specs, plain, segs = attention_specs(rows, keys, cols)
    work = parts * cols // HD * sets * rows * keys
    if rows == keys:
        out_specs = pl.BlockSpec((3, rows, wide), lambda s, j: (0, s, j))
        out_shape = jax.ShapeDtypeStruct((3, q.shape[0], parts * cols), BF)
    else:
        out_specs = [plain(rows), plain(keys), plain(keys)]
        out_shape = [
            jax.ShapeDtypeStruct((q.shape[0], parts * cols), BF),
            jax.ShapeDtypeStruct((kv.shape[0], parts * cols), F32),
            jax.ShapeDtypeStruct((kv.shape[0], parts * cols), F32),
        ]
    return pl.pallas_call(
        attend_back_kernel,
        grid=(sets, parts * pairs),
        in_specs=specs + [plain(rows)] + segs,
        out_specs=out_specs,
        out_shape=out_shape,
        cost_estimate=pl.CostEstimate(
            flops=40 * work * HD, bytes_accessed=4 * q.size * 2, transcendentals=work
        ),
        name="attend_back",
    )(q, kv, kv, grad, seg_q[:, None, :], seg_k[:, :, None])


def tile(most, *sizes):
    for size in (1024, 768, 512, 384, 256, 128):
        if size <= most and all(n % size == 0 for n in sizes):
            return size
    raise ValueError("width")


def cost(flops, *arrays):
    return pl.CostEstimate(
        flops=flops,
        bytes_accessed=sum(a.size * a.dtype.itemsize for a in arrays),
        transcendentals=0,
    )


def times_weight(which, x, weight, cols, finish, extras, out_types, name):
    rows, parts, count = x.shape[0], len(weight), len(weight[0])
    bn = tile(1024, cols, *[v[3] for w in weight for v in w])
    per = cols // bn

    def spec(t, view):
        _, block, height, first = view
        local = lambda j: first // bn + jnp.clip(j - t * per, 0, per - 1)
        if block is None:
            return pl.BlockSpec((height, bn), lambda j, _: (0, local(j)))
        return pl.BlockSpec((height, bn), lambda j, names: (names[block], local(j)))

    def kernel(which_ref, x_ref, *refs):
        step = pl.program_id(0)
        more = refs[parts * count : parts * count + len(extras)]
        outs = refs[parts * count + len(extras) :]
        for t in range(parts):

            @pl.when((step >= t * per) & (step < t * per + per))
            def _(t=t):
                total, first = None, 0
                for ref in refs[t * count : (t + 1) * count]:
                    height = ref.shape[0]
                    part = dot(x_ref[:, first : first + height], ref[...])
                    total = part if total is None else total + part
                    first += height
                for ref, out in zip(outs, finish(total, *[e[...] for e in more])):
                    ref[...] = out.astype(ref.dtype)

    return pl.pallas_call(
        kernel,
        grid_spec=pltpu.PrefetchScalarGridSpec(
            num_scalar_prefetch=1,
            grid=(parts * per,),
            in_specs=[pl.BlockSpec(x.shape, lambda j, _: (0, 0))]
            + [spec(t, v) for t in range(parts) for v in weight[t]]
            + [pl.BlockSpec((e.shape[0], bn), lambda j, _: (0, j)) for e in extras],
            out_specs=[pl.BlockSpec((rows, bn), lambda j, _: (0, j)) for _ in out_types],
        ),
        out_shape=[jax.ShapeDtypeStruct((rows, parts * cols), t) for t in out_types],
        cost_estimate=cost(2 * x.size * cols * parts, x, x),
        name=name,
    )(which, x, *[v[0] for w in weight for v in w], *extras)


def times_transposed(which, right, weight, name):
    parts = len(weight)
    stack, rows, each = right.shape[0], right.shape[1], right.shape[2] // parts
    bn = tile(1024, each, *[v[3] for w in weight for v in w])
    per = each // bn
    heights = [v[2] for v in weight[0]]
    width = sum(heights)

    def spec(view):
        _, block, height, first = view
        if block is None:
            return pl.BlockSpec((height, bn), lambda j, _: (0, first // bn + j))
        return pl.BlockSpec((height, bn), lambda j, names: (names[block], first // bn + j))

    def kernel(which_ref, *refs):
        out_ref = refs[-1]
        begin = pl.program_id(0) == 0
        place = 0
        for b, height in enumerate(heights):
            cols = slice(place, place + height)
            total = sum(
                dot_nt(refs[t][...], refs[parts + t * len(heights) + b][...])
                for t in range(parts)
            )
            if stack * per == 1:
                out_ref[:, cols] = total
            else:

                @pl.when(begin)
                def _():
                    out_ref[:, cols] = total

                @pl.when(jnp.logical_not(begin))
                def _():
                    out_ref[:, cols] += total

            place += height

    return pl.pallas_call(
        kernel,
        grid_spec=pltpu.PrefetchScalarGridSpec(
            num_scalar_prefetch=1,
            grid=(stack * per,),
            in_specs=[
                pl.BlockSpec(
                    (None, rows, bn), lambda j, _, t=t: (j // per, 0, t * per + j % per)
                )
                for t in range(parts)
            ]
            + [spec(v) for w in weight for v in w],
            out_specs=pl.BlockSpec((rows, width), lambda j, _: (0, 0)),
        ),
        out_shape=jax.ShapeDtypeStruct((rows, width), F32),
        cost_estimate=cost(2 * rows * width * stack * each * parts, right),
        name=name,
    )(which, *[right] * parts, *[v[0] for w in weight for v in w])


def weight_grads(pairs, parts, section, sections, add=None, blocks=1, name="weight_grads"):
    rows, width = pairs[0][0].shape
    height = width // sections
    bn = tile(1024, *[right.shape[2] // parts for _, right in pairs])
    counts = [right.shape[0] * right.shape[2] // parts // bn for _, right in pairs]
    starts = [sum(counts[:i]) for i in range(len(pairs))]
    columns = sum(counts) * bn
    low = height // blocks

    def kernel(*refs):
        step = pl.program_id(0)
        turned = refs[-len(pairs) :]
        at = len(pairs) * (1 + parts)
        add_ref = refs[at] if add is not None else None
        outs = refs[at + (add is not None) : -len(pairs)]
        for i in range(len(pairs)):
            base = i * (1 + parts)

            @pl.when(step == starts[i])
            def _(i=i, base=base):
                turned[i][...] = refs[base][...].T

            @pl.when((step >= starts[i]) & (step < starts[i] + counts[i]))
            def _(i=i, base=base):
                for t in range(parts):
                    value = dot(turned[i][...], refs[base + 1 + t][...])
                    if add_ref is not None:
                        value += add_ref[t].astype(F32)
                    value = value.astype(BF)
                    if blocks == 1:
                        outs[0][t] = value
                    else:
                        for b in range(blocks):
                            outs[b * parts + t][...] = value[b * low : (b + 1) * low]

    in_specs, operands = [], []
    for i, (left, right) in enumerate(pairs):
        in_specs.append(pl.BlockSpec((rows, height), lambda j: (0, section)))
        operands.append(left)
        per = right.shape[2] // parts // bn
        for t in range(parts):

            def where(j, i=i, t=t, per=per):
                local = jnp.clip(j - starts[i], 0, counts[i] - 1)
                return local // per, 0, t * per + local % per

            in_specs.append(pl.BlockSpec((None, rows, bn), where))
            operands.append(right)
    if add is not None:
        in_specs.append(pl.BlockSpec((parts, height, bn), lambda j: (0, 0, j)))
        operands.append(add)
    if blocks == 1:
        out_specs = pl.BlockSpec((parts, height, bn), lambda j: (0, 0, j))
        out_shape = jax.ShapeDtypeStruct((parts, height, columns), BF)
    else:
        out_specs = [pl.BlockSpec((low, bn), lambda j: (0, j))] * (blocks * parts)
        out_shape = [jax.ShapeDtypeStruct((low, columns), BF)] * (blocks * parts)
    found = pl.pallas_call(
        kernel,
        grid=(sum(counts),),
        in_specs=in_specs,
        out_specs=out_specs,
        out_shape=out_shape,
        scratch_shapes=[pltpu.VMEM((height, rows), BF) for _ in pairs],
        cost_estimate=cost(2 * height * rows * columns * parts, *[p[1] for p in pairs]),
        name=name,
    )(*operands)
    if blocks == 1:
        return found
    return [[found[b * parts + t] for t in range(parts)] for b in range(blocks)]


def three_parts(value):
    first = lax.reduce_precision(value, 8, 7)
    second = lax.reduce_precision(value - first, 8, 7)
    return [part.astype(BF) for part in (first, second, value - first - second)]


def pack_small(row, height):
    flat = jnp.concatenate(three_parts(row))
    columns = -(-flat.shape[0] // (128 * height)) * 128
    return jnp.pad(flat, (0, height * columns - flat.shape[0])).reshape(height, columns)


def unpack_small(packed, size, height):
    depth = lax.axis_size("dp")
    flat = packed.reshape(-1, depth, height * packed.shape[1])[:, :, : 3 * size]
    parts = jnp.sum(flat.reshape(-1, depth, 3, size).astype(F32), axis=2)
    return jnp.swapaxes(parts, 0, 1).reshape(-1, size)


def swap(value, mask):
    count = lax.axis_size("dp") * lax.axis_size("thi") * lax.axis_size("tlo")
    return lax.ppermute(value, RANKS, [(i, i ^ mask) for i in range(count)])


def relative_small(parts):
    return jnp.take(parts, jnp.arange(parts.shape[0]) ^ lax.axis_index(RANKS), axis=0)


def scatter_small(held, until):
    mask = held.shape[0] // 2
    while mask >= until:
        held = held[:mask] + swap(held[mask:], mask)
        mask //= 2
    return held


def over_dp(value, mask):
    count = lax.axis_size("dp")
    return lax.ppermute(value, "dp", [(i, i ^ mask) for i in range(count)])


def over_tensor(value, mask):
    count = lax.axis_size("thi") * lax.axis_size("tlo")
    return lax.ppermute(value, ("thi", "tlo"), [(i, i ^ mask) for i in range(count)])


def tensor_size():
    return lax.axis_size("thi") * lax.axis_size("tlo")


def hold(*trees):
    return lax.optimization_barrier(trees)


def gather_far(shard):
    rest = lax.axis_size("dp") // 4
    return jnp.concatenate([shard] + [over_dp(shard, 4 * m) for m in range(1, rest)], axis=0)


def gather_sides(own):
    return over_dp(own, 2), [over_tensor(own, m) for m in range(1, tensor_size())]


def gather_corners(own, sides):
    across, near = sides
    half = own.shape[0] // 2
    far = [
        jnp.concatenate([over_dp(block[:half], 2), over_tensor(across[half:], m + 1)], axis=0)
        for m, block in enumerate(near)
    ]
    return [[own] + near, [across] + far]


def gather_core(here):
    return [here, [[over_dp(block, 1) for block in line] for line in here]]


def block_views(blocks, first):
    return [
        [(line[t], None, line[t].shape[0], first) for half in blocks for line in half]
        for t in range(len(blocks[0][0]))
    ]


def wide(value):
    return value.astype(F32)


def scatter_corners(line):
    half = line[0][0].shape[0] // 2
    return (
        [over_dp(block[:half], 2) for block in line[1][1:]],
        [over_tensor(block[half:], m + 1) for m, block in enumerate(line[1][1:])],
    )


def scatter_sides(line, corners):
    near, across = line[0][1:], line[1][0]
    half = across.shape[0] // 2
    tops, bottoms = corners
    near = [
        jnp.concatenate([(wide(a[:half]) + wide(b)).astype(BF), a[half:]], axis=0)
        for a, b in zip(near, tops)
    ]
    if bottoms:
        low = (wide(across[half:]) + sum(wide(b) for b in bottoms)).astype(BF)
        across = jnp.concatenate([across[:half], low], axis=0)
    return [over_dp(across, 2)] + [over_tensor(block, m + 1) for m, block in enumerate(near)]


def scatter_far(line, sides):
    own = line[0][0]
    rest = lax.axis_size("dp") // 4
    height = own.shape[0] // rest
    piece = lambda m: sum(
        (wide(v[m * height : (m + 1) * height]) for v in sides),
        wide(own[m * height : (m + 1) * height]),
    )
    return [piece(0)] + [over_dp(piece(m).astype(BF), 4 * m) for m in range(1, rest)]


def scatter_end(addends):
    return sum(wide(v) for v in addends)


def relative_blocks():
    depth = lax.axis_size("dp")
    rest = depth // 4
    own = lax.axis_index("dp")
    place = np.arange(depth)
    core, second, far = place // (2 * rest), place // rest % 2, place % rest
    order = jnp.asarray(far * 4 + second * 2 + core) ^ own
    mask = jnp.arange(depth) ^ own
    places = ((mask & 1) * 2 + (mask >> 1 & 1)) * rest + (mask >> 2)
    return order, places


def reorder(rows, order):
    cut = rows.reshape(rows.shape[:-1] + (order.shape[0], -1))
    return jnp.take(cut, order, axis=-2).reshape(rows.shape)


def selection(order, width):
    each = width // order.shape[0]
    source = (order[:, None] * each + jnp.arange(each)[None]).reshape(-1)
    return (jnp.arange(width)[:, None] == source[None, :]).astype(BF)


def select_wide(rows, chooser):
    return sum(dot(part, chooser) for part in three_parts(rows))


def on_device(
    inputs,
    seg_ids,
    qkv_weight,
    out_weight,
    up_weight,
    down_weight,
    norm_gains,
    row_biases,
    ff_bias,
    cotangent,
):
    blocks = tensor_size()
    sharers = lax.axis_size("tlo")
    rows, width = inputs.shape
    layers = qkv_weight.shape[0]
    head_cols = qkv_weight.shape[3]
    hidden = up_weight.shape[2]
    length = seg_ids.shape[1]
    sets = max(1, rows // length)
    T = range(blocks)

    seg_k = lax.dynamic_slice_in_dim(seg_ids, lax.axis_index("thi") * sets, sets)
    seg_q = seg_k
    if sharers > 1:
        seg_q = lax.dynamic_slice_in_dim(seg_k, lax.axis_index("tlo") * rows, rows, axis=1)

    order, places = relative_blocks()
    pick, unpick = selection(order, width), selection(places, width)
    own_t = lax.axis_index(("thi", "tlo"))
    same_t = jnp.arange(blocks, dtype=jnp.int32)
    relative_t = (same_t ^ own_t).astype(jnp.int32)

    join = lambda *parts: jnp.concatenate(parts, axis=1).astype(BF)
    qkv_of = lambda l: [qkv_weight[l, k] for k in range(3)]
    spread = lambda shard: lax.all_gather(shard, SPREAD, axis=0, tiled=True)
    views = lambda whole, first: [[(whole, t, width, first)] for t in T]
    row = jnp.concatenate([norm_gains.reshape(-1), row_biases.reshape(-1), ff_bias.reshape(-1)])
    height = qkv_weight.shape[2]
    first_whole = spread(jnp.concatenate([join(*qkv_of(0)), pack_small(row, height)], axis=1))
    small = unpack_small(first_whole[:, 3 * head_cols :], row.shape[0], height)
    mlp_views = [None] * layers
    for l in range(1, layers):
        mlp = spread(join(up_weight[l], down_weight[l].T))
        mlp_views[l] = views(mlp, 0), views(mlp, hidden)
    mid_own = gather_far(join(up_weight[0], out_weight[0].T))
    down_shard = join(down_weight[0].T)
    mid_own, down_shard = hold(mid_own, down_shard)
    mid_sides = gather_sides(mid_own)
    down_own = gather_far(down_shard)
    mid_here = gather_corners(mid_own, mid_sides)
    mid_blocks = gather_core(mid_here)
    down_own, mid_here = hold(down_own, mid_here)
    down_sides = gather_sides(down_own)
    later_shards = [join(*qkv_of(l), out_weight[l].T) for l in range(1, layers)]

    devices = small.shape[0]
    cuts = np.cumsum([norm_gains.size, row_biases.size])
    spread_out = lambda piece, like: jnp.moveaxis(
        piece.reshape((devices,) + like.shape), 0, -2
    ).reshape(like.shape[:-1] + (devices * like.shape[-1],))
    gain_rows = spread_out(small[:, : cuts[0]], norm_gains)
    shift_rows = spread_out(small[:, cuts[0] : cuts[1]], row_biases)
    up_shifts = spread_out(small[:, cuts[1] :], ff_bias)

    def vectors(l):
        gains, shifts, up_shift = gain_rows[l], shift_rows[l], up_shifts[l]
        heads, wide = reorder(shifts[:2], relative_t), shifts[2:]
        if l == 0:
            gains, wide = reorder(gains, order), reorder(wide, order)
            up_shift = reorder(up_shift, relative_t)
        else:
            gains = jnp.concatenate([reorder(gains[:1], order), gains[1:]])
            wide = jnp.concatenate([reorder(wide[:2], order), wide[2:]])
        heads = heads.reshape(2, blocks, head_cols)
        qkv_shift = jnp.stack([heads[0], jnp.zeros_like(heads[0]), heads[1]], axis=1)
        return gains, qkv_shift.reshape(1, -1), wide, up_shift[None]

    add_shift = lambda value, shift: (value + shift,)

    def enter(value, shift):
        value = value + shift
        upto = 0.5 * (1.0 + lax.erf(value * HALF_ROOT))
        return value * upto, upto + value * jnp.exp(-0.5 * value * value) * INV_ROOT_TAU

    def leave(value, slope):
        return (value * slope.astype(F32),)

    gather_keys = (
        (lambda v: lax.all_gather(v, "tlo", axis=0, tiled=True)) if sharers > 1 else (lambda v: v)
    )
    stored = []
    stream = dot(inputs, pick)
    for l in range(layers):
        gains, qkv_shift, shifts, up_shift = vectors(l)
        if l > 1:
            stream = select_wide(stream, pick)
        if l == 0:
            qkv, low = views(first_whole, 0), inputs
        else:
            qkv, out = attn_views[l]
            up, down = mlp_views[l]
            low = stream.astype(BF)
        (projected,) = times_weight(
            relative_t, low, qkv, 3 * head_cols, add_shift, [qkv_shift], [BF], "project"
        )
        if l == 0:
            projected, down_sides = hold(projected, down_sides)
            down_here = gather_corners(down_own, down_sides)
        keys = gather_keys(projected)
        mixture = attend(projected, keys, head_cols, seg_q, seg_k)
        if l == 0:
            mixture, down_here, later_shards = hold(mixture, down_here, later_shards)
            later_own = [gather_far(s) for s in later_shards]
            up, out = block_views(mid_blocks, 0), block_views(mid_blocks, hidden)
            down = block_views(gather_core(down_here), 0)
        attended = times_transposed(relative_t, mixture[None], out, "attended")
        unit_early, rate_early = norm_parts(stream + (attended + shifts[0]))
        mid = unit_early * gains[0] + shifts[1]
        if l == 0:
            mid, later_own = hold(mid, later_own)
            later_sides = [gather_sides(own) for own in later_own]
        else:
            mid = select_wide(mid, unpick)
        mid_low = mid.astype(BF)
        hidden_out, slopes = times_weight(
            same_t, mid_low, up, hidden, enter, [up_shift], [BF, BF], "enter"
        )
        if l == 0:
            hidden_out, later_sides = hold(hidden_out, later_sides)
            later_here = [gather_corners(o, s) for o, s in zip(later_own, later_sides)]
        branch = times_transposed(same_t, hidden_out[None], down, "branch")
        if l == 0:
            branch, later_here = hold(branch, later_here)
            attn_views = [None]
            for got in [gather_core(here) for here in later_here]:
                attn_views.append((block_views(got, 0), block_views(got, 3 * head_cols)))
        unit_late, rate_late = norm_parts(mid + (branch + shifts[2]))
        stored.append(
            (
                qkv,
                out,
                up,
                down,
                gains,
                low,
                projected,
                keys,
                mixture,
                unit_early,
                rate_early,
                mid_low,
                slopes,
                hidden_out,
                unit_late,
                rate_late,
            )
        )
        stream = unit_late * gains[1] + shifts[3]
    if layers == 1:
        stream = select_wide(stream, unpick)

    grad_stream = cotangent if layers > 1 else select_wide(cotangent, pick)
    mlp_done, attn_done = [None] * layers, [None] * layers
    small_grads = [None] * layers
    over_rows = lambda value: jnp.sum(value.astype(F32), axis=0)
    fold = lambda whole: jnp.moveaxis(
        whole.reshape(whole.shape[:-1] + (devices, whole.shape[-1] // devices)), -2, 0
    ).reshape(devices, -1)
    flying = None
    for l in reversed(range(layers)):
        (
            qkv,
            out,
            up,
            down,
            gains,
            low,
            projected,
            keys,
            mixture,
            unit_early,
            rate_early,
            mid_low,
            slopes,
            hidden_out,
            unit_late,
            rate_late,
        ) = stored[l]
        if 0 < l < layers - 1:
            grad_stream = select_wide(grad_stream, unpick)
        grad_second = norm_back(grad_stream, unit_late, rate_late, gains[1])
        gain_late, shift_late = over_rows(grad_stream * unit_late), over_rows(grad_stream)
        second_low = grad_second.astype(BF)
        (grad_pre,) = times_weight(same_t, second_low, down, hidden, leave, [slopes], [BF], "leave")
        mlp_pairs = [(mid_low, grad_pre[None]), (second_low, hidden_out[None])]
        if l == 0:
            if flying is not None:
                line, corners = flying
                grad_pre, corners = hold(grad_pre, corners)
                sides = scatter_sides(line, corners)
            mlp_send = weight_grads(mlp_pairs, blocks, 1, 2, name="mlp_send")
            mlp_send, grad_pre = hold(mlp_send, grad_pre)
            mlp_came = over_dp(mlp_send, 1)
        else:
            whole = weight_grads(mlp_pairs, blocks, 0, 1, name="mlp_grads")
            whole, grad_pre = hold(whole, grad_pre)
            mlp_done[l] = lax.psum_scatter(
                whole.reshape(-1, whole.shape[2]), SPREAD, scatter_dimension=0, tiled=True
            ).astype(F32)
        grad_mid = grad_second + times_transposed(same_t, grad_pre[None], up, "grad_mid")
        if l > 0:
            grad_mid = select_wide(grad_mid, pick)
        grad_first = norm_back(grad_mid, unit_early, rate_early, gains[0])
        gain_early, shift_early = over_rows(grad_mid * unit_early), over_rows(grad_mid)
        first_low = grad_first.astype(BF)
        if l == 0:
            first_low, mlp_came = hold(first_low, mlp_came)
            mlp_line = weight_grads(
                mlp_pairs, blocks, 0, 2, add=mlp_came, blocks=2, name="mlp_keep"
            )
            if flying is not None:
                first_low, mlp_line, sides = hold(first_low, mlp_line, sides)
                addends = scatter_far(line, sides)
            else:
                first_low, mlp_line = hold(first_low, mlp_line)
            mlp_corners = scatter_corners(mlp_line)
        (grad_mix,) = times_weight(
            relative_t, first_low, out, head_cols, lambda v: (v,), [], [BF], "grad_mix"
        )
        grad_proj = attend_back(projected, keys, head_cols, grad_mix, seg_q, seg_k)
        if sharers > 1:
            grad_proj = jnp.stack(
                [grad_proj[0]]
                + [
                    lax.psum_scatter(v, "tlo", scatter_dimension=0, tiled=True).astype(BF)
                    for v in grad_proj[1:]
                ]
            )
        left = dot(low, pick).astype(BF) if l == 0 else low
        attn_pairs = [(left, grad_proj), (first_low, mixture[None])]
        attn_send = weight_grads(attn_pairs, blocks, 1, 2, name="attn_send")
        if l == 0:
            if flying is not None:
                attn_send, addends = hold(attn_send, addends)
                attn_done[l + 1] = scatter_end(addends)
            attn_send, grad_proj, mlp_corners = hold(attn_send, grad_proj, mlp_corners)
            mlp_sides = scatter_sides(mlp_line, mlp_corners)
        else:
            attn_send, grad_proj = hold(attn_send, grad_proj)
        attn_came = over_dp(attn_send, 1)
        back = times_transposed(relative_t, grad_proj, qkv, "grad_stream")
        back, attn_came = hold(back, attn_came)
        attn_line = weight_grads(
            attn_pairs, blocks, 0, 2, add=attn_came, blocks=2, name="attn_keep"
        )
        heads_grad = jnp.stack([over_rows(grad_proj[0]), over_rows(grad_proj[2])])
        wide_grad = jnp.stack(
            [over_rows(grad_first), shift_early, over_rows(grad_second), shift_late]
        )
        gains_grad = jnp.stack([gain_early, gain_late])
        ups_grad = over_rows(grad_pre)
        heads_grad = reorder(heads_grad, relative_t)
        if l == 0:
            ups_grad = reorder(ups_grad, relative_t)
            wide_grad, gains_grad = reorder(wide_grad, places), reorder(gains_grad, places)
        else:
            wide_grad = jnp.concatenate([reorder(wide_grad[:2], places), wide_grad[2:]])
            gains_grad = jnp.concatenate([reorder(gains_grad[:1], places), gains_grad[1:]])
        small_grads[l] = gains_grad, jnp.concatenate([heads_grad, wide_grad]), ups_grad
        if l == 0:
            smalls = [jnp.stack([small_grads[n][i] for n in range(layers)]) for i in range(3)]
            small_sums = relative_small(
                jnp.concatenate([fold(whole) for whole in smalls], axis=1)
            )
            attn_line, mlp_sides, back, small_sums = hold(attn_line, mlp_sides, back, small_sums)
            mlp_addends = scatter_far(mlp_line, mlp_sides)
            attn_corners = scatter_corners(attn_line)
            attn_corners, mlp_addends = hold(attn_corners, mlp_addends)
            attn_sides = scatter_sides(attn_line, attn_corners)
            small_sums = scatter_small(small_sums, 2 * blocks)
            attn_sides, small_sums = hold(attn_sides, small_sums)
            attn_done[l] = scatter_end(scatter_far(attn_line, attn_sides))
            mlp_done[l] = scatter_end(mlp_addends)
            summed = scatter_small(small_sums, 1)[0]
            input_grad = select_wide(grad_first, unpick) + back
        else:
            attn_line, back = hold(attn_line, back)
            flying = attn_line, scatter_corners(attn_line)
            grad_stream = grad_first + back

    return (
        stream.astype(BF),
        input_grad,
        jnp.stack(
            [
                jnp.stack(
                    [attn_done[l][:, k * head_cols : (k + 1) * head_cols] for k in range(3)]
                )
                for l in range(layers)
            ]
        ),
        jnp.stack([attn_done[l][:, 3 * head_cols :].T for l in range(layers)]),
        jnp.stack([mlp_done[l][:, :hidden] for l in range(layers)]),
        jnp.stack([mlp_done[l][:, hidden:].T for l in range(layers)]),
        summed[: cuts[0]].reshape(norm_gains.shape),
        summed[cuts[0] : cuts[1]].reshape(row_biases.shape),
        summed[cuts[1] :].reshape(ff_bias.shape),
    )


def solution(mesh):
    def whole(*args):
        inputs, seg_ids = args[:2]
        depth, blocks = mesh.shape["dp"], mesh.shape["tensor"]
        rows = inputs.shape[0] // (depth * blocks)
        sharers = max(1, seg_ids.shape[1] // rows)
        inner = Mesh(mesh.devices.reshape(depth, blocks // sharers, sharers), RANKS)
        tensor = ("thi", "tlo")
        row_wise = P(RANKS, None)
        weight_specs = (
            P(None, None, "dp", tensor),
            P(None, tensor, "dp"),
            P(None, "dp", tensor),
            P(None, tensor, "dp"),
            P(None, None, RANKS),
            P(None, None, RANKS),
            P(None, RANKS),
        )
        return jax.shard_map(
            on_device,
            mesh=inner,
            in_specs=(row_wise, P("dp", None)) + weight_specs + (row_wise,),
            out_specs=(row_wise, row_wise) + weight_specs,
            check_vma=False,
        )(*args)

    return whole
```

time: 1290 us -> 851 us (0.66)
  waiting for transfers between devices: 578 us -> 281 us
  other arithmetic: 316 us -> 87.7 us
  Pallas kernels: 96.4 us -> 304 us
  matrix products: 214 us -> 27.7 us
  starting transfers between devices: 11.3 us -> 64.3 us
  local copies, waits for them, and re-layouts: 46.8 us -> 63.8 us
    reduce_scatter x2 -> x1, waiting for transfers between devices: 306 us -> 0.01 us  [on_device(): lax.psum_scatter(whole.reshape(-1, whole.shape[2]), SPREAD, scatter_dimen...]
    concatenate x18 -> x16, other arithmetic: 290 us -> 13.4 us  [the longest x3 3.55 us: gather_far(): jnp.concatenate([shard] + [over_dp(shard, 4 * m) for m in range(1, rest)]...]
    all_gather x3 -> x2, waiting for transfers between devices: 255 us -> 0.01 us  [on_device(): spread = lambda shard: lax.all_gather(shard, SPREAD, axis=0, tiled=True)]
    ppermute x0 -> x57, waiting for transfers between devices: none -> 250 us  [the longest x45 182 us: over_dp(): return lax.ppermute(value, 'dp', [(i, i ^ mask) for i in range(count)])]
    pallas_call x8 -> x27, Pallas kernels: 96.4 us -> 304 us  [the longest x8 84.8 us: times_transposed(): pl.pallas_call(kernel, grid_spec=pltpu.PrefetchScalarGridSpec(num_scalar_...]
    dot_general x48 -> x0, matrix products: 108 us -> none  [the longest x24 56.8 us: dot_nt(): lax.dot_general(a, b, (((1,), (1,)), ((), ())), preferred_element_type=F32)]
    dot_general x16 -> x10, matrix products: 107 us -> 27.7 us  [dot(): return jnp.dot(a, b, preferred_element_type=F32)]
    ppermute x0 -> x57, starting transfers between devices: none -> 56.3 us  [the longest x45 41.5 us: over_dp(): return lax.ppermute(value, 'dp', [(i, i ^ mask) for i in range(count)])]
  transfers between devices with their start and end apart: 17 -> 65, of which waited for: 15 -> 27; matrix products, arithmetic and copies ran while one was open for 30% -> 17% of each run, Pallas kernels for 4% -> 29%
where the time goes in v2:
time: 851 us; the launch traced here: 845 us
  Pallas kernels  304 us (36%)
  waiting for transfers between devices  281 us (33%)
  other arithmetic  87.7 us (10%)
  starting transfers between devices  64.3 us (8%)
  local copies, waits for them, and re-layouts  63.8 us (7%)
  matrix products  27.7 us (3%)
  between operations  15.6 us (2%)
    ppermute x45, waiting for transfers between devices, over_dp(): return lax.ppermute(value, 'dp', [(i, i ^ mask) for i in range(count)])  182 us
    pallas_call x8, Pallas kernels, times_transposed(): pl.pallas_call(kernel, grid_spec=pltpu.PrefetchScalarGridSpec(num_scalar_...  84.8 us
    pallas_call x8, Pallas kernels, times_weight(): pl.pallas_call(kernel, grid_spec=pltpu.PrefetchScalarGridSpec(num_scalar_...  75.3 us
    pallas_call x7, Pallas kernels, weight_grads(): pl.pallas_call(kernel, grid=(sum(counts),), in_specs=in_specs, out_specs=...  71 us
    ppermute x12, waiting for transfers between devices, over_tensor(): lax.ppermute(value, ('thi', 'tlo'), [(i, i ^ mask) for i in range(count)])  68.4 us
    pallas_call x2, Pallas kernels, attend_back(): pl.pallas_call(attend_back_kernel, grid=(sets, parts * pairs), in_specs=s...  45.9 us
    ppermute x45, starting transfers between devices, over_dp(): return lax.ppermute(value, 'dp', [(i, i ^ mask) for i in range(count)])  41.5 us
    ppermute x5, waiting for transfers between devices, swap(): return lax.ppermute(value, RANKS, [(i, i ^ mask) for i in range(count)])  30.9 us
  transfers between devices with their start and end apart: 65, of which 27 were waited for; matrix products, arithmetic and copies ran while one was open for 17% of the time, Pallas kernels for 29%

profile of v2, /device:TPU:8, one launch (start us, length us, event | category | flops | bytes accessed | tf_op | source)
XLA Modules:
  0.0 844.6 jit_solution(13973576971675764616)
XLA Ops:
  16.5 11.6 %collective-permute-done = bf16[64,2560]{1,0:T(8,128)(2,1)S(1)} collective-permute-done((bf16[64,2560]{1,0:T(8,128)(2,1)S(1)}, bf16[64,2560]{1,0:T(8,128)(2,1)S(1)}, u32[]{:S(2)}, u32[]{:S(2)}) %collective-permute-start) | collective-permute-done | bytes 327712 | tf_op jit(solution)/shard_map/ppermute | solution.py:375
  28.1 13.7 %collective-permute-done.1 = bf16[64,2560]{1,0:T(8,128)(2,1)S(1)} collective-permute-done((bf16[64,2560]{1,0:T(8,128)(2,1)S(1)}, bf16[64,2560]{1,0:T(8,128)(2,1)S(1)}, u32[]{:S(2)}, u32[]{:S(2)}) %collective-permute-start.1) | collective-permute-done | bytes 327712 | tf_op jit(solution)/shard_map/ppermute | solution.py:375
  58.7 26.4 %collective-permute-done.6.refs_6_.refs_4_ = bf16[256,2560]{1,0:T(8,128)(2,1)S(1)} collective-permute-done((bf16[256,2560]{1,0:T(8,128)(2,1)S(1)}, bf16[256,2560]{1,0:T(8,128)(2,1)S(1)}, u32[]{:S(2)}, u32[]{:S(2)}) %collective-permute-start.6) | collective-permute-done | bytes 1310752 | tf_op jit(solution)/shard_map/ppermute | solution.py:380
  101.0 15.3 %collective-permute-done.4 = bf16[64,2048]{1,0:T(8,128)(2,1)} collective-permute-done((bf16[64,2048]{1,0:T(8,128)(2,1)S(1)}, bf16[64,2048]{1,0:T(8,128)(2,1)}, u32[]{:S(2)}, u32[]{:S(2)}) %collective-permute-start.4) | collective-permute-done | bytes 262176 | tf_op jit(solution)/shard_map/ppermute | solution.py:375
  135.9 8.8 %project.2.q_ref.k_ref.v_ref = bf16[512,3072]{1,0:T(8,128)(2,1)} custom-call(s32[2]{0:T(128)} %iota_xor_fusion.which_ref, bf16[512,1024]{1,0:T(8,128)(2,1)} %x_ref.1, bf16[2048,1664]{1,0:T(8,128)(2,1)} %all-gather.3.cloned.1.call-done.refs_0_.refs_1_.refs_2_.refs_3_, bf16[2048,1664]{1,0:T(8,128)(2,1)} %all-gather.3.cloned.1.call-done.refs_0_.refs_1_.refs_2_.refs_3_, ...), custom_call_target="tpu_custom_call" | custom-call | flops 3221225472 | bytes 2097152 | tf_op jit(solution)/shard_map/project/pallas_call | solution.py:191
  166.1 8.8 %collective-permute-done.12 = bf16[128,2048]{1,0:T(8,128)(2,1)} collective-permute-done((bf16[128,2048]{1,0:T(8,128)(2,1)S(1)}, bf16[128,2048]{1,0:T(8,128)(2,1)}, u32[]{:S(2)}, u32[]{:S(2)}) %collective-permute-start.12) | collective-permute-done | bytes 524320 | tf_op jit(solution)/shard_map/ppermute | solution.py:375
  177.8 13.3 %attend.2 = bf16[512,1024]{1,0:T(8,128)(2,1)} custom-call(bf16[512,3072]{1,0:T(8,128)(2,1)} %project.2.q_ref.k_ref.v_ref, bf16[512,3072]{1,0:T(8,128)(2,1)} %project.2.q_ref.k_ref.v_ref, bf16[512,3072]{1,0:T(8,128)(2,1)} %project.2.q_ref.k_ref.v_ref, s32[1,1,512]{2,1,0:T(1,128)} %get-tuple-element.336.segq_ref, s32[1,512,1]{2,1,0:T(8,128)} %copy.76.segk_ref), custom_call_target="tpu_custom_call" | custom-call | flops 4294967296 | bytes 6291456 | tf_op jit(solution)/shard_map/attend/pallas_call | solution.py:106
  206.4 9.9 %collective-permute-done.19 = bf16[64,2048]{1,0:T(8,128)(2,1)S(1)} collective-permute-done((bf16[64,2048]{1,0:T(8,128)(2,1)S(1)}, bf16[64,2048]{1,0:T(8,128)(2,1)S(1)}, u32[]{:S(2)}, u32[]{:S(2)}) %collective-permute-start.19) | collective-permute-done | bytes 262176 | tf_op jit(solution)/shard_map/ppermute | solution.py:375
  217.0 18.4 %collective-permute-done.20 = bf16[64,2048]{1,0:T(8,128)(2,1)} collective-permute-done((bf16[64,2048]{1,0:T(8,128)(2,1)S(1)}, bf16[64,2048]{1,0:T(8,128)(2,1)}, u32[]{:S(2)}, u32[]{:S(2)}) %collective-permute-start.20) | collective-permute-done | bytes 262176 | tf_op jit(solution)/shard_map/ppermute | solution.py:375
  240.0 11.6 %collective-permute-done.21.refs_1_.refs_3_ = bf16[256,2048]{1,0:T(8,128)(2,1)} collective-permute-done((bf16[256,2048]{1,0:T(8,128)(2,1)S(1)}, bf16[256,2048]{1,0:T(8,128)(2,1)}, u32[]{:S(2)}, u32[]{:S(2)}) %collective-permute-start.21) | collective-permute-done | bytes 1048608 | tf_op jit(solution)/shard_map/ppermute | solution.py:375
  261.7 13.3 %enter.2 = (bf16[512,4096]{1,0:T(8,128)(2,1)}, bf16[512,4096]{1,0:T(8,128)(2,1)}) custom-call(s32[2]{0:T(128)} %iota.43.which_ref, bf16[512,1024]{1,0:T(8,128)(2,1)} %convert_element_type.332.x_ref.refs_0_, bf16[256,2560]{1,0:T(8,128)(2,1)} %copy-done.8, bf16[256,2560]{1,0:T(8,128)(2,1)} %collective-permute-done.7.refs_3_.refs_1_, ...), custom_call_target="tpu_custom_call" | custom-call | flops 4294967296 | bytes 2097152 | tf_op jit(solution)/shard_map/enter/pallas_call | solution.py:191
  279.4 15.5 %branch.2 = f32[512,1024]{1,0:T(8,128)} custom-call(s32[2]{0:T(128)} %iota.42.which_ref, bf16[1,512,4096]{2,1,0:T(8,128)(2,1)} %bitcast.170, bf16[1,512,4096]{2,1,0:T(8,128)(2,1)} %bitcast.171, bf16[256,2048]{1,0:T(8,128)(2,1)} %pad_maximum_fusion.3.refs_2_.refs_0_, bf16[256,2048]{1,0:T(8,128)(2,1)} %collective-permute-done.10.refs_3_.refs_1_, ...), custom_call_target="tpu_custom_call" | custom-call | flops 4294967296 | bytes 4194304 | tf_op jit(solution)/shard_map/branch/pallas_call | solution.py:245
  312.3 13.7 %attend.3 = bf16[512,1024]{1,0:T(8,128)(2,1)} custom-call(bf16[512,3072]{1,0:T(8,128)(2,1)} %project.3.q_ref.k_ref.v_ref, bf16[512,3072]{1,0:T(8,128)(2,1)} %project.3.q_ref.k_ref.v_ref, bf16[512,3072]{1,0:T(8,128)(2,1)} %project.3.q_ref.k_ref.v_ref, s32[1,1,512]{2,1,0:T(1,128)} %get-tuple-element.336.segq_ref, s32[1,512,1]{2,1,0:T(8,128)} %copy.76.segk_ref), custom_call_target="tpu_custom_call" | custom-call | flops 4294967296 | bytes 6291456 | tf_op jit(solution)/shard_map/attend/pallas_call | solution.py:106
  341.0 13.0 %enter.3 = (bf16[512,4096]{1,0:T(8,128)(2,1)}, bf16[512,4096]{1,0:T(8,128)(2,1)}) custom-call(s32[2]{0:T(128)} %iota.46.which_ref, bf16[512,1024]{1,0:T(8,128)(2,1)} %get-tuple-element.350.x_ref.refs_0_, bf16[2048,4096]{1,0:T(8,128)(2,1)} %all-gather.5.cloned.1.call-done.refs_0_.refs_1_.refs_2_.refs_3_, ...), custom_call_target="tpu_custom_call" | custom-call | flops 4294967296 | bytes 2097152 | tf_op jit(solution)/shard_map/enter/pallas_call | solution.py:191
  354.5 10.1 %branch.3 = f32[512,1024]{1,0:T(8,128)} custom-call(s32[2]{0:T(128)} %iota.45.which_ref, bf16[1,512,4096]{2,1,0:T(8,128)(2,1)} %bitcast.176, bf16[1,512,4096]{2,1,0:T(8,128)(2,1)} %bitcast.177, bf16[2048,4096]{1,0:T(8,128)(2,1)} %all-gather.5.cloned.1.call-done.refs_0_.refs_1_.refs_2_.refs_3_, ...), custom_call_target="tpu_custom_call" | custom-call | flops 4294967296 | bytes 4194304 | tf_op jit(solution)/shard_map/branch/pallas_call | solution.py:245
  374.6 10.7 %leave.2 = bf16[512,4096]{1,0:T(8,128)(2,1)} custom-call(s32[2]{0:T(128)} %iota.48.which_ref, bf16[512,1024]{1,0:T(8,128)(2,1)} %convert_element_type.339.x_ref.refs_3_, bf16[2048,4096]{1,0:T(8,128)(2,1)} %all-gather.5.cloned.1.call-done.refs_0_.refs_1_.refs_2_.refs_3_, bf16[2048,4096]{1,0:T(8,128)(2,1)} %all-gather.5.cloned.1.call-done.refs_0_.refs_1_.refs_2_.refs_3_, ...), custom_call_target="tpu_custom_call" | custom-call | flops 4294967296 | bytes 2097152 | tf_op jit(solution)/shard_map/leave/pallas_call | solution.py:191
  385.3 15.7 %mlp_grads.1 = bf16[2,1024,4096]{2,1,0:T(8,128)(2,1)} custom-call(bf16[512,1024]{1,0:T(8,128)(2,1)} %get-tuple-element.350.x_ref.refs_0_, bf16[1,512,4096]{2,1,0:T(8,128)(2,1)} %bitcast.166, bf16[1,512,4096]{2,1,0:T(8,128)(2,1)} %bitcast.167, bf16[512,1024]{1,0:T(8,128)(2,1)} %convert_element_type.339.x_ref.refs_3_, bf16[1,512,4096]{2,1,0:T(8,128)(2,1)} %bitcast.178, ...), custom_call_target="tpu_custom_call" | custom-call | flops 8589934592 | bytes 8388608 | tf_op jit(solution)/shard_map/mlp_grads/pallas_call | solution.py:322
  401.5 10.4 %grad_mid.2 = f32[512,1024]{1,0:T(8,128)} custom-call(s32[2]{0:T(128)} %iota.47.which_ref, bf16[1,512,4096]{2,1,0:T(8,128)(2,1)} %bitcast.168, bf16[1,512,4096]{2,1,0:T(8,128)(2,1)} %bitcast.169, bf16[2048,4096]{1,0:T(8,128)(2,1)} %all-gather.5.cloned.1.call-done.refs_0_.refs_1_.refs_2_.refs_3_, ...), custom_call_target="tpu_custom_call" | custom-call | flops 4294967296 | bytes 4194304 | tf_op jit(solution)/shard_map/grad_mid/pallas_call | solution.py:245
  430.9 22.9 %attend_back.2.refs_1_.refs_2_.refs_0_ = bf16[3,512,1024]{2,1,0:T(8,128)(2,1)} custom-call(bf16[512,3072]{1,0:T(8,128)(2,1)} %project.3.q_ref.k_ref.v_ref, bf16[512,3072]{1,0:T(8,128)(2,1)} %project.3.q_ref.k_ref.v_ref, bf16[512,3072]{1,0:T(8,128)(2,1)} %project.3.q_ref.k_ref.v_ref, bf16[512,1024]{1,0:T(8,128)(2,1)} %grad_mix.2.grad_ref, ...), custom_call_target="tpu_custom_call" | custom-call | flops 10737418240 | bytes 12582912 | tf_op jit(solution)/shard_map/attend_back/pallas_call | solution.py:134
  461.1 13.2 %grad_stream.2 = f32[512,1024]{1,0:T(8,128)} custom-call(s32[2]{0:T(128)} %iota_xor_fusion.which_ref, bf16[3,512,1024]{2,1,0:T(8,128)(2,1)} %attend_back.2.refs_1_.refs_2_.refs_0_, bf16[3,512,1024]{2,1,0:T(8,128)(2,1)} %attend_back.2.refs_1_.refs_2_.refs_0_, bf16[256,2048]{1,0:T(8,128)(2,1)} %copy-done.6, ...), custom_call_target="tpu_custom_call" | custom-call | flops 3221225472 | bytes 3145728 | tf_op jit(solution)/shard_map/grad_stream/pallas_call | solution.py:245
  474.3 8.9 %attn_keep.2 = (bf16[256,2048]{1,0:T(8,128)(2,1)}, bf16[256,2048]{1,0:T(8,128)(2,1)}, bf16[256,2048]{1,0:T(8,128)(2,1)}, bf16[256,2048]{1,0:T(8,128)(2,1)}) custom-call(bf16[512,1024]{1,0:T(8,128)(2,1)} %fusion.23.x_ref.refs_0_, bf16[3,512,1024]{2,1,0:T(8,128)(2,1)} %attend_back.2.refs_1_.refs_2_.refs_0_, ...), custom_call_target="tpu_custom_call" | custom-call | flops 2147483648 | bytes 4194304 | tf_op jit(solution)/shard_map/attn_keep/pallas_call | solution.py:322
  493.6 11.2 %leave.3 = bf16[512,4096]{1,0:T(8,128)(2,1)} custom-call(s32[2]{0:T(128)} %iota.50.which_ref, bf16[512,1024]{1,0:T(8,128)(2,1)} %convert_element_type.344.x_ref.refs_3_, bf16[256,2048]{1,0:T(8,128)(2,1)} %pad_maximum_fusion.3.refs_2_.refs_0_, bf16[256,2048]{1,0:T(8,128)(2,1)} %collective-permute-done.10.refs_3_.refs_1_, ...), custom_call_target="tpu_custom_call" | custom-call | flops 4294967296 | bytes 2097152 | tf_op jit(solution)/shard_map/leave/pallas_call | solution.py:191
  504.8 10.8 %mlp_send.1 = bf16[2,512,4096]{2,1,0:T(8,128)(2,1)} custom-call(bf16[512,1024]{1,0:T(8,128)(2,1)} %convert_element_type.332.x_ref.refs_0_, bf16[1,512,4096]{2,1,0:T(8,128)(2,1)} %bitcast.160, bf16[1,512,4096]{2,1,0:T(8,128)(2,1)} %bitcast.161, bf16[512,1024]{1,0:T(8,128)(2,1)} %convert_element_type.344.x_ref.refs_3_, bf16[1,512,4096]{2,1,0:T(8,128)(2,1)} %bitcast.172, ...), custom_call_target="tpu_custom_call" | custom-call | flops 4294967296 | bytes 8388608 | tf_op jit(solution)/shard_map/mlp_send/pallas_call | solution.py:322
  528.7 15.7 %grad_mid.3 = f32[512,1024]{1,0:T(8,128)} custom-call(s32[2]{0:T(128)} %iota.49.which_ref, bf16[1,512,4096]{2,1,0:T(8,128)(2,1)} %bitcast.162, bf16[1,512,4096]{2,1,0:T(8,128)(2,1)} %bitcast.163, bf16[256,2560]{1,0:T(8,128)(2,1)} %copy-done.8, bf16[256,2560]{1,0:T(8,128)(2,1)} %collective-permute-done.7.refs_3_.refs_1_, ...), custom_call_target="tpu_custom_call" | custom-call | flops 4294967296 | bytes 4194304 | tf_op jit(solution)/shard_map/grad_mid/pallas_call | solution.py:245
  572.2 12.2 %mlp_keep.1 = (bf16[256,4096]{1,0:T(8,128)(2,1)}, bf16[256,4096]{1,0:T(8,128)(2,1)}, bf16[256,4096]{1,0:T(8,128)(2,1)}, bf16[256,4096]{1,0:T(8,128)(2,1)}) custom-call(bf16[512,1024]{1,0:T(8,128)(2,1)} %convert_element_type.332.x_ref.refs_0_, bf16[1,512,4096]{2,1,0:T(8,128)(2,1)} %bitcast.164, bf16[1,512,4096]{2,1,0:T(8,128)(2,1)} %bitcast.165, ...), custom_call_target="tpu_custom_call" | custom-call | flops 4294967296 | bytes 8388608 | tf_op jit(solution)/shard_map/mlp_keep/pallas_call | solution.py:322
  584.4 23.9 %collective-permute-done.37 = bf16[256,2048]{1,0:T(8,128)(2,1)} collective-permute-done((bf16[256,2048]{1,0:T(8,128)(2,1)}, bf16[256,2048]{1,0:T(8,128)(2,1)}, u32[]{:S(2)}, u32[]{:S(2)}) %collective-permute-start.37) | collective-permute-done | bytes 1048608 | tf_op jit(solution)/shard_map/ppermute | solution.py:375
  624.8 23.0 %attend_back.3.refs_1_.refs_2_.refs_0_ = bf16[3,512,1024]{2,1,0:T(8,128)(2,1)} custom-call(bf16[512,3072]{1,0:T(8,128)(2,1)} %project.2.q_ref.k_ref.v_ref, bf16[512,3072]{1,0:T(8,128)(2,1)} %project.2.q_ref.k_ref.v_ref, bf16[512,3072]{1,0:T(8,128)(2,1)} %project.2.q_ref.k_ref.v_ref, bf16[512,1024]{1,0:T(8,128)(2,1)} %grad_mix.3.grad_ref, ...), custom_call_target="tpu_custom_call" | custom-call | flops 10737418240 | bytes 12582912 | tf_op jit(solution)/shard_map/attend_back/pallas_call | solution.py:134
  686.6 8.7 %attn_keep.3 = (bf16[256,2048]{1,0:T(8,128)(2,1)}, bf16[256,2048]{1,0:T(8,128)(2,1)}, bf16[256,2048]{1,0:T(8,128)(2,1)}, bf16[256,2048]{1,0:T(8,128)(2,1)}) custom-call(bf16[512,1024]{1,0:T(8,128)(2,1)} %get-tuple-element.353.refs_0_, bf16[3,512,1024]{2,1,0:T(8,128)(2,1)} %attend_back.3.refs_1_.refs_2_.refs_0_, ...), custom_call_target="tpu_custom_call" | custom-call | flops 2147483648 | bytes 4194304 | tf_op jit(solution)/shard_map/attn_keep/pallas_call | solution.py:322
  695.3 20.8 %collective-permute-done.46 = bf16[256,4096]{1,0:T(8,128)(2,1)} collective-permute-done((bf16[256,4096]{1,0:T(8,128)(2,1)}, bf16[256,4096]{1,0:T(8,128)(2,1)}, u32[]{:S(2)}, u32[]{:S(2)}) %collective-permute-start.46) | collective-permute-done | bytes 2097184 | tf_op jit(solution)/shard_map/ppermute | solution.py:380
  735.7 29.8 %collective-permute-done.55 = f32[8,768]{1,0:T(8,128)S(1)} collective-permute-done((f32[8,768]{1,0:T(8,128)S(1)}, f32[8,768]{1,0:T(8,128)S(1)}, u32[]{:S(2)}, u32[]{:S(2)}) %collective-permute-start.55) | collective-permute-done | bytes 24608 | tf_op jit(solution)/shard_map/ppermute | solution.py:358
  781.3 19.8 %collective-permute-done.53 = bf16[256,2048]{1,0:T(8,128)(2,1)S(1)} collective-permute-done((bf16[256,2048]{1,0:T(8,128)(2,1)S(1)}, bf16[256,2048]{1,0:T(8,128)(2,1)S(1)}, u32[]{:S(2)}, u32[]{:S(2)}) %collective-permute-start.53) | collective-permute-done | bytes 1048608 | tf_op jit(solution)/shard_map/ppermute | solution.py:380
  814.4 9.5 %collective-permute-done.58 = bf16[64,2048]{1,0:T(8,128)(2,1)} collective-permute-done((bf16[64,2048]{1,0:T(8,128)(2,1)S(1)}, bf16[64,2048]{1,0:T(8,128)(2,1)}, u32[]{:S(2)}, u32[]{:S(2)}) %collective-permute-start.58) | collective-permute-done | bytes 262176 | tf_op jit(solution)/shard_map/ppermute | solution.py:375
  (556 shorter events, 358.3 us)
Async XLA Ops:
  7.2 122.7 %all-gather.3.cloned.1.call-start = ((), (), s32[]{:S(2)}) async-start(), calls=%async_computation.1 | async-start | bytes 7028736 | tf_op jit(solution)/shard_map/all_gather | solution.py:524
  11.6 328.9 %all-gather.5.cloned.1.call-start = ((), (), s32[]{:S(2)}) async-start(), calls=%async_computation.2 | async-start | bytes 17301504 | tf_op jit(solution)/shard_map/all_gather | solution.py:524
  12.8 821.7 %reduce-scatter.2.cloned.1.call-start = ((), (), s32[]{:S(2)}) async-start(), calls=%async_computation.3 | async-start | bytes 17301504 | tf_op jit(solution)/shard_map/reduce_scatter | solution.py:696
  13.0 28.8 %collective-permute-start.1 = (bf16[64,2560]{1,0:T(8,128)(2,1)S(1)}, bf16[64,2560]{1,0:T(8,128)(2,1)S(1)}, u32[]{:S(2)}, u32[]{:S(2)}) collective-permute-start(bf16[64,2560]{1,0:T(8,128)(2,1)S(1)} %pad_maximum_fusion.15), channel_id=1, source_target_pairs={{0,16},{2,18},{4,20},{6,22},{8,24},{10,26},{12,28},{14,30},{16,0},... | collective-permute-start | bytes 983048 | tf_op jit(solution)/shard_map/ppermute | solution.py:375
  16.0 33.3 %collective-permute-start.2 = (bf16[64,2560]{1,0:T(8,128)(2,1)S(1)}, bf16[64,2560]{1,0:T(8,128)(2,1)S(1)}, u32[]{:S(2)}, u32[]{:S(2)}) collective-permute-start(bf16[64,2560]{1,0:T(8,128)(2,1)S(1)} %pad_maximum_fusion.15), channel_id=1, source_target_pairs={{0,24},{2,26},{4,28},{6,30},{8,16},{10,18},{12,20},{14,22},{16,8},... | collective-permute-start | bytes 983048 | tf_op jit(solution)/shard_map/ppermute | solution.py:375
  49.4 35.6 %collective-permute-start.6 = (bf16[256,2560]{1,0:T(8,128)(2,1)S(1)}, bf16[256,2560]{1,0:T(8,128)(2,1)S(1)}, u32[]{:S(2)}, u32[]{:S(2)}) collective-permute-start(bf16[256,2560]{1,0:T(8,128)(2,1)S(1)} %pad_maximum_fusion.2.refs_2_.refs_0_), channel_id=1, source_target_pairs={{0,1},{1,0},{2,3},{3,2},{4,5},{5,4},{6,7},{7,6},{8,9},{9,8},{10,11... | collective-permute-start | bytes 3932168 | tf_op jit(solution)/shard_map/ppermute | solution.py:380
  51.5 46.3 %collective-permute-start.7 = (bf16[256,2560]{1,0:T(8,128)(2,1)S(1)}, bf16[256,2560]{1,0:T(8,128)(2,1)}, u32[]{:S(2)}, u32[]{:S(2)}) collective-permute-start(bf16[256,2560]{1,0:T(8,128)(2,1)S(1)} %pad_maximum_fusion.2.refs_2_.refs_0_), channel_id=1, source_target_pairs={{0,4},{2,6},{4,0},{6,2},{8,12},{10,14},{12,8},{14,10},{16,20},{18,... | collective-permute-start | bytes 3932168 | tf_op jit(solution)/shard_map/ppermute | solution.py:375
  86.0 38.0 %collective-permute-start.8 = (bf16[128,2560]{1,0:T(8,128)(2,1)}, bf16[128,2560]{1,0:T(8,128)(2,1)S(1)}, u32[]{:S(2)}, u32[]{:S(2)}) collective-permute-start(bf16[128,2560]{1,0:T(8,128)(2,1)} %slice.621), channel_id=1, source_target_pairs={{0,4},{2,6},{4,0},{6,2},{8,12},{10,14},{12,8},{14,10},{16,20},{18,... | collective-permute-start | bytes 1966088 | tf_op jit(solution)/shard_map/ppermute | solution.py:375
  90.7 31.1 %collective-permute-start.5 = (bf16[64,2048]{1,0:T(8,128)(2,1)S(1)}, bf16[64,2048]{1,0:T(8,128)(2,1)}, u32[]{:S(2)}, u32[]{:S(2)}) collective-permute-start(bf16[64,2048]{1,0:T(8,128)(2,1)S(1)} %get-tuple-element.105), channel_id=1, source_target_pairs={{0,24},{2,26},{4,28},{6,30},{8,16},{10,18},{12,20},{14,22},{16,8},... | collective-permute-start | bytes 786440 | tf_op jit(solution)/shard_map/ppermute | solution.py:375
  158.5 34.8 %collective-permute-start.14 = (bf16[256,2560]{1,0:T(8,128)(2,1)S(1)}, bf16[256,2560]{1,0:T(8,128)(2,1)}, u32[]{:S(2)}, u32[]{:S(2)}) collective-permute-start(bf16[256,2560]{1,0:T(8,128)(2,1)S(1)} %pad_maximum_fusion.2.refs_2_.refs_0_), channel_id=1, source_target_pairs={{0,2},{2,0},{4,6},{6,4},{8,10},{10,8},{12,14},{14,12},{16,18},{18,... | collective-permute-start | bytes 3932168 | tf_op jit(solution)/shard_map/ppermute | solution.py:375
  158.5 35.4 %collective-permute-start.15 = (bf16[256,2560]{1,0:T(8,128)(2,1)}, bf16[256,2560]{1,0:T(8,128)(2,1)}, u32[]{:S(2)}, u32[]{:S(2)}) collective-permute-start(bf16[256,2560]{1,0:T(8,128)(2,1)} %collective-permute-done.7.refs_3_.refs_1_), channel_id=1, source_target_pairs={{0,2},{2,0},{4,6},{6,4},{8,10},{10,8},{12,14},{14,12},{16,18},{18,... | collective-permute-start | bytes 3932168 | tf_op jit(solution)/shard_map/ppermute | solution.py:375
  159.0 37.7 %collective-permute-start.16 = (bf16[256,2560]{1,0:T(8,128)(2,1)S(1)}, bf16[256,2560]{1,0:T(8,128)(2,1)}, u32[]{:S(2)}, u32[]{:S(2)}) collective-permute-start(bf16[256,2560]{1,0:T(8,128)(2,1)S(1)} %collective-permute-done.6.refs_6_.refs_4_), channel_id=1, source_target_pairs={{0,2},{2,0},{4,6},{6,4},{8,10},{10,8},{12,14},{14,12},{16,18},{18,... | collective-permute-start | bytes 3932168 | tf_op jit(solution)/shard_map/ppermute | solution.py:375
  159.0 37.7 %collective-permute-start.17 = (bf16[256,2560]{1,0:T(8,128)(2,1)}, bf16[256,2560]{1,0:T(8,128)(2,1)}, u32[]{:S(2)}, u32[]{:S(2)}) collective-permute-start(bf16[256,2560]{1,0:T(8,128)(2,1)} %constant_dynamic-update-slice_fusion.refs_7_.refs_5_), channel_id=1, source_target_pairs={{0,2},{2,0},{4,6},{6,4},{8,10},{10,8},{12,14},{14,12},{16,18},{18,... | collective-permute-start | bytes 3932168 | tf_op jit(solution)/shard_map/ppermute | solution.py:375
  193.9 41.5 %collective-permute-start.20 = (bf16[64,2048]{1,0:T(8,128)(2,1)S(1)}, bf16[64,2048]{1,0:T(8,128)(2,1)}, u32[]{:S(2)}, u32[]{:S(2)}) collective-permute-start(bf16[64,2048]{1,0:T(8,128)(2,1)S(1)} %copy-done.41), channel_id=1, source_target_pairs={{0,24},{2,26},{4,28},{6,30},{8,16},{10,18},{12,20},{14,22},{16,8},... | collective-permute-start | bytes 786440 | tf_op jit(solution)/shard_map/ppermute | solution.py:375
  238.9 39.2 %collective-permute-start.23 = (bf16[256,2048]{1,0:T(8,128)(2,1)}, bf16[256,2048]{1,0:T(8,128)(2,1)}, u32[]{:S(2)}, u32[]{:S(2)}) collective-permute-start(bf16[256,2048]{1,0:T(8,128)(2,1)} %pad_maximum_fusion.3.refs_2_.refs_0_), channel_id=1, source_target_pairs={{0,2},{2,0},{4,6},{6,4},{8,10},{10,8},{12,14},{14,12},{16,18},{18,... | collective-permute-start | bytes 3145736 | tf_op jit(solution)/shard_map/ppermute | solution.py:375
  239.0 39.8 %collective-permute-start.24 = (bf16[256,2048]{1,0:T(8,128)(2,1)}, bf16[256,2048]{1,0:T(8,128)(2,1)}, u32[]{:S(2)}, u32[]{:S(2)}) collective-permute-start(bf16[256,2048]{1,0:T(8,128)(2,1)} %collective-permute-done.10.refs_3_.refs_1_), channel_id=1, source_target_pairs={{0,2},{2,0},{4,6},{6,4},{8,10},{10,8},{12,14},{14,12},{16,18},{18,... | collective-permute-start | bytes 3145736 | tf_op jit(solution)/shard_map/ppermute | solution.py:375
  239.5 39.3 %collective-permute-start.25 = (bf16[256,2048]{1,0:T(8,128)(2,1)}, bf16[256,2048]{1,0:T(8,128)(2,1)}, u32[]{:S(2)}, u32[]{:S(2)}) collective-permute-start(bf16[256,2048]{1,0:T(8,128)(2,1)} %collective-permute-done.11.refs_6_.refs_4_), channel_id=1, source_target_pairs={{0,2},{2,0},{4,6},{6,4},{8,10},{10,8},{12,14},{14,12},{16,18},{18,... | collective-permute-start | bytes 3145736 | tf_op jit(solution)/shard_map/ppermute | solution.py:375
  239.6 39.3 %collective-permute-start.26 = (bf16[256,2048]{1,0:T(8,128)(2,1)}, bf16[256,2048]{1,0:T(8,128)(2,1)}, u32[]{:S(2)}, u32[]{:S(2)}) collective-permute-start(bf16[256,2048]{1,0:T(8,128)(2,1)} %pad_maximum_fusion.4.refs_7_.refs_5_), channel_id=1, source_target_pairs={{0,2},{2,0},{4,6},{6,4},{8,10},{10,8},{12,14},{14,12},{16,18},{18,... | collective-permute-start | bytes 3145736 | tf_op jit(solution)/shard_map/ppermute | solution.py:375
  518.6 53.6 %collective-permute-start.36 = (bf16[2,512,4096]{2,1,0:T(8,128)(2,1)}, bf16[2,512,4096]{2,1,0:T(8,128)(2,1)}, u32[]{:S(2)}, u32[]{:S(2)}) collective-permute-start(bf16[2,512,4096]{2,1,0:T(8,128)(2,1)} %mlp_send.1), channel_id=1, source_target_pairs={{0,2},{2,0},{4,6},{6,4},{8,10},{10,8},{12,14},{14,12},{16,18},{18,... | collective-permute-start | bytes 25165832 | tf_op jit(solution)/shard_map/ppermute | solution.py:375
  559.5 48.8 %collective-permute-start.37 = (bf16[256,2048]{1,0:T(8,128)(2,1)}, bf16[256,2048]{1,0:T(8,128)(2,1)}, u32[]{:S(2)}, u32[]{:S(2)}) collective-permute-start(bf16[256,2048]{1,0:T(8,128)(2,1)} %pad_maximum_fusion.7), channel_id=1, source_target_pairs={{0,4},{2,6},{4,0},{6,2},{8,12},{10,14},{12,8},{14,10},{16,20},{18,... | collective-permute-start | bytes 3145736 | tf_op jit(solution)/shard_map/ppermute | solution.py:375
  611.4 46.4 %collective-permute-start.39 = (bf16[64,2048]{1,0:T(8,128)(2,1)}, bf16[64,2048]{1,0:T(8,128)(2,1)S(1)}, u32[]{:S(2)}, u32[]{:S(2)}) collective-permute-start(bf16[64,2048]{1,0:T(8,128)(2,1)} %get-tuple-element.293), channel_id=1, source_target_pairs={{0,8},{2,10},{4,12},{6,14},{8,0},{10,2},{12,4},{14,6},{16,24},{18,... | collective-permute-start | bytes 786440 | tf_op jit(solution)/shard_map/ppermute | solution.py:375
  611.4 46.4 %collective-permute-start.40 = (bf16[64,2048]{1,0:T(8,128)(2,1)}, bf16[64,2048]{1,0:T(8,128)(2,1)}, u32[]{:S(2)}, u32[]{:S(2)}) collective-permute-start(bf16[64,2048]{1,0:T(8,128)(2,1)} %get-tuple-element.292), channel_id=1, source_target_pairs={{0,16},{2,18},{4,20},{6,22},{8,24},{10,26},{12,28},{14,30},{16,0},... | collective-permute-start | bytes 786440 | tf_op jit(solution)/shard_map/ppermute | solution.py:375
  615.1 42.7 %collective-permute-start.41 = (bf16[64,2048]{1,0:T(8,128)(2,1)}, bf16[64,2048]{1,0:T(8,128)(2,1)}, u32[]{:S(2)}, u32[]{:S(2)}) collective-permute-start(bf16[64,2048]{1,0:T(8,128)(2,1)} %get-tuple-element.291), channel_id=1, source_target_pairs={{0,24},{2,26},{4,28},{6,30},{8,16},{10,18},{12,20},{14,22},{16,8},... | collective-permute-start | bytes 786440 | tf_op jit(solution)/shard_map/ppermute | solution.py:375
  616.6 47.8 %collective-permute-start.42 = (bf16[128,4096]{1,0:T(8,128)(2,1)}, bf16[128,4096]{1,0:T(8,128)(2,1)}, u32[]{:S(2)}, u32[]{:S(2)}) collective-permute-start(bf16[128,4096]{1,0:T(8,128)(2,1)} %get-tuple-element.297), channel_id=1, source_target_pairs={{0,4},{2,6},{4,0},{6,2},{8,12},{10,14},{12,8},{14,10},{16,20},{18,... | collective-permute-start | bytes 3145736 | tf_op jit(solution)/shard_map/ppermute | solution.py:375
  617.6 46.7 %collective-permute-start.43 = (bf16[128,4096]{1,0:T(8,128)(2,1)}, bf16[128,4096]{1,0:T(8,128)(2,1)}, u32[]{:S(2)}, u32[]{:S(2)}) collective-permute-start(bf16[128,4096]{1,0:T(8,128)(2,1)} %get-tuple-element.296), channel_id=1, source_target_pairs={{0,1},{1,0},{2,3},{3,2},{4,5},{5,4},{6,7},{7,6},{8,9},{9,8},{10,11... | collective-permute-start | bytes 3145736 | tf_op jit(solution)/shard_map/ppermute | solution.py:380
  667.8 48.4 %collective-permute-start.46 = (bf16[256,4096]{1,0:T(8,128)(2,1)}, bf16[256,4096]{1,0:T(8,128)(2,1)}, u32[]{:S(2)}, u32[]{:S(2)}) collective-permute-start(bf16[256,4096]{1,0:T(8,128)(2,1)} %pad_maximum_fusion.1), channel_id=1, source_target_pairs={{0,1},{1,0},{2,3},{3,2},{4,5},{5,4},{6,7},{7,6},{8,9},{9,8},{10,11... | collective-permute-start | bytes 6291464 | tf_op jit(solution)/shard_map/ppermute | solution.py:380
  672.2 48.4 %collective-permute-start.45 = (bf16[256,4096]{1,0:T(8,128)(2,1)}, bf16[256,4096]{1,0:T(8,128)(2,1)}, u32[]{:S(2)}, u32[]{:S(2)}) collective-permute-start(bf16[256,4096]{1,0:T(8,128)(2,1)} %pad_maximum_fusion), channel_id=1, source_target_pairs={{0,4},{2,6},{4,0},{6,2},{8,12},{10,14},{12,8},{14,10},{16,20},{18,... | collective-permute-start | bytes 6291464 | tf_op jit(solution)/shard_map/ppermute | solution.py:375
  729.2 40.8 %collective-permute-start.49 = (bf16[64,4096]{1,0:T(8,128)(2,1)S(1)}, bf16[64,4096]{1,0:T(8,128)(2,1)S(1)}, u32[]{:S(2)}, u32[]{:S(2)}) collective-permute-start(bf16[64,4096]{1,0:T(8,128)(2,1)S(1)} %get-tuple-element.286), channel_id=1, source_target_pairs={{0,8},{2,10},{4,12},{6,14},{8,0},{10,2},{12,4},{14,6},{16,24},{18,... | collective-permute-start | bytes 1572872 | tf_op jit(solution)/shard_map/ppermute | solution.py:375
  729.3 42.3 %collective-permute-start.50 = (bf16[64,4096]{1,0:T(8,128)(2,1)S(1)}, bf16[64,4096]{1,0:T(8,128)(2,1)S(1)}, u32[]{:S(2)}, u32[]{:S(2)}) collective-permute-start(bf16[64,4096]{1,0:T(8,128)(2,1)S(1)} %get-tuple-element.285), channel_id=1, source_target_pairs={{0,16},{2,18},{4,20},{6,22},{8,24},{10,26},{12,28},{14,30},{16,0},... | collective-permute-start | bytes 1572872 | tf_op jit(solution)/shard_map/ppermute | solution.py:375
  730.9 46.6 %collective-permute-start.51 = (bf16[64,4096]{1,0:T(8,128)(2,1)S(1)}, bf16[64,4096]{1,0:T(8,128)(2,1)S(1)}, u32[]{:S(2)}, u32[]{:S(2)}) collective-permute-start(bf16[64,4096]{1,0:T(8,128)(2,1)S(1)} %get-tuple-element.284), channel_id=1, source_target_pairs={{0,24},{2,26},{4,28},{6,30},{8,16},{10,18},{12,20},{14,22},{16,8},... | collective-permute-start | bytes 1572872 | tf_op jit(solution)/shard_map/ppermute | solution.py:375
  732.8 32.8 %collective-permute-start.55 = (f32[8,768]{1,0:T(8,128)S(1)}, f32[8,768]{1,0:T(8,128)S(1)}, u32[]{:S(2)}, u32[]{:S(2)}) collective-permute-start(f32[8,768]{1,0:T(8,128)S(1)} %slice.652), channel_id=1, source_target_pairs={{0,8},{1,9},{2,10},{3,11},{4,12},{5,13},{6,14},{7,15},{8,0},{9,1},... | collective-permute-start | bytes 73736 | tf_op jit(solution)/shard_map/ppermute | solution.py:358
  733.9 43.5 %collective-permute-start.47 = (bf16[128,2048]{1,0:T(8,128)(2,1)S(1)}, bf16[128,2048]{1,0:T(8,128)(2,1)S(1)}, u32[]{:S(2)}, u32[]{:S(2)}) collective-permute-start(bf16[128,2048]{1,0:T(8,128)(2,1)S(1)} %get-tuple-element.303), channel_id=1, source_target_pairs={{0,4},{2,6},{4,0},{6,2},{8,12},{10,14},{12,8},{14,10},{16,20},{18,... | collective-permute-start | bytes 1572872 | tf_op jit(solution)/shard_map/ppermute | solution.py:375
  (106 other events, 1923.9 us)
Sparse Core Ops, SparseCore 0:
  11.7 105.2 all-gather.2
  120.4 144.3 all-gather.4
  420.7 236.8 reduce-scatter.1

commit v3 on v2

--- a/solution.py
+++ b/solution.py
@@ -138,7 +138,7 @@
         out_specs=out_specs,
         out_shape=out_shape,
         cost_estimate=pl.CostEstimate(
-            flops=40 * work * HD, bytes_accessed=4 * q.size * 2, transcendentals=work
+            flops=5 * work * HD, bytes_accessed=q.size, transcendentals=work // 8
         ),
         name="attend_back",
     )(q, kv, kv, grad, seg_q[:, None, :], seg_k[:, :, None])
@@ -151,10 +151,11 @@
     raise ValueError("width")
 
 
-def cost(flops, *arrays):
+def cost(name, flops, *arrays):
+    short = 1 if name in ("project", "attended", "enter", "branch") else 8
     return pl.CostEstimate(
-        flops=flops,
-        bytes_accessed=sum(a.size * a.dtype.itemsize for a in arrays),
+        flops=flops // short,
+        bytes_accessed=sum(a.size * a.dtype.itemsize for a in arrays) // short,
         transcendentals=0,
     )
 
@@ -199,7 +200,7 @@
             out_specs=[pl.BlockSpec((rows, bn), lambda j, _: (0, j)) for _ in out_types],
         ),
         out_shape=[jax.ShapeDtypeStruct((rows, parts * cols), t) for t in out_types],
-        cost_estimate=cost(2 * x.size * cols * parts, x, x),
+        cost_estimate=cost(name, 2 * x.size * cols * parts, x, x),
         name=name,
     )(which, x, *[v[0] for w in weight for v in w], *extras)
 
@@ -257,7 +258,7 @@
             out_specs=pl.BlockSpec((rows, width), lambda j, _: (0, 0)),
         ),
         out_shape=jax.ShapeDtypeStruct((rows, width), F32),
-        cost_estimate=cost(2 * rows * width * stack * each * parts, right),
+        cost_estimate=cost(name, 2 * rows * width * stack * each * parts, right),
         name=name,
     )(which, *[right] * parts, *[v[0] for w in weight for v in w])
 
@@ -326,7 +327,7 @@
         out_specs=out_specs,
         out_shape=out_shape,
         scratch_shapes=[pltpu.VMEM((height, rows), BF) for _ in pairs],
-        cost_estimate=cost(2 * height * rows * columns * parts, *[p[1] for p in pairs]),
+        cost_estimate=cost(name, 2 * height * rows * columns * parts, *[p[1] for p in pairs]),
         name=name,
     )(*operands)
     if blocks == 1:
@@ -386,6 +387,10 @@
 
 def hold(*trees):
     return lax.optimization_barrier(trees)
+
+
+def after(tree, *others):
+    return lax.optimization_barrier((tree, others))[0]
 
 
 def gather_far(shard):
@@ -430,7 +435,7 @@
     )
 
 
-def scatter_sides(line, corners):
+def scatter_sum(line, corners):
     near, across = line[0][1:], line[1][0]
     half = across.shape[0] // 2
     tops, bottoms = corners
@@ -441,10 +446,14 @@
     if bottoms:
         low = (wide(across[half:]) + sum(wide(b) for b in bottoms)).astype(BF)
         across = jnp.concatenate([across[:half], low], axis=0)
-    return [over_dp(across, 2)] + [over_tensor(block, m + 1) for m, block in enumerate(near)]
-
-
-def scatter_far(line, sides):
+    return [across] + near
+
+
+def scatter_sides(sums):
+    return [over_dp(sums[0], 2)] + [over_tensor(v, m + 1) for m, v in enumerate(sums[1:])]
+
+
+def scatter_pieces(line, sides):
     own = line[0][0]
     rest = lax.axis_size("dp") // 4
     height = own.shape[0] // rest
@@ -452,7 +461,11 @@
         (wide(v[m * height : (m + 1) * height]) for v in sides),
         wide(own[m * height : (m + 1) * height]),
     )
-    return [piece(0)] + [over_dp(piece(m).astype(BF), 4 * m) for m in range(1, rest)]
+    return [piece(0)] + [piece(m).astype(BF) for m in range(1, rest)]
+
+
+def scatter_far(pieces):
+    return [pieces[0]] + [over_dp(piece, 4 * m) for m, piece in enumerate(pieces) if m]
 
 
 def scatter_end(addends):
@@ -516,8 +529,7 @@
     order, places = relative_blocks()
     pick, unpick = selection(order, width), selection(places, width)
     own_t = lax.axis_index(("thi", "tlo"))
-    same_t = jnp.arange(blocks, dtype=jnp.int32)
-    relative_t = (same_t ^ own_t).astype(jnp.int32)
+    relative_t = (jnp.arange(blocks, dtype=jnp.int32) ^ own_t).astype(jnp.int32)
 
     join = lambda *parts: jnp.concatenate(parts, axis=1).astype(BF)
     qkv_of = lambda l: [qkv_weight[l, k] for k in range(3)]
@@ -527,10 +539,11 @@
     height = qkv_weight.shape[2]
     first_whole = spread(jnp.concatenate([join(*qkv_of(0)), pack_small(row, height)], axis=1))
     small = unpack_small(first_whole[:, 3 * head_cols :], row.shape[0], height)
-    mlp_views = [None] * layers
+    later_views = [None]
     for l in range(1, layers):
-        mlp = spread(join(up_weight[l], down_weight[l].T))
-        mlp_views[l] = views(mlp, 0), views(mlp, hidden)
+        whole = spread(join(*qkv_of(l), out_weight[l].T, up_weight[l], down_weight[l].T))
+        firsts = (0, 3 * head_cols, 4 * head_cols, 4 * head_cols + hidden)
+        later_views.append([views(whole, first) for first in firsts])
     mid_own = gather_far(join(up_weight[0], out_weight[0].T))
     down_shard = join(down_weight[0].T)
     mid_own, down_shard = hold(mid_own, down_shard)
@@ -540,7 +553,6 @@
     mid_blocks = gather_core(mid_here)
     down_own, mid_here = hold(down_own, mid_here)
     down_sides = gather_sides(down_own)
-    later_shards = [join(*qkv_of(l), out_weight[l].T) for l in range(1, layers)]
 
     devices = small.shape[0]
     cuts = np.cumsum([norm_gains.size, row_biases.size])
@@ -554,12 +566,9 @@
     def vectors(l):
         gains, shifts, up_shift = gain_rows[l], shift_rows[l], up_shifts[l]
         heads, wide = reorder(shifts[:2], relative_t), shifts[2:]
+        up_shift = reorder(up_shift, relative_t)
         if l == 0:
             gains, wide = reorder(gains, order), reorder(wide, order)
-            up_shift = reorder(up_shift, relative_t)
-        else:
-            gains = jnp.concatenate([reorder(gains[:1], order), gains[1:]])
-            wide = jnp.concatenate([reorder(wide[:2], order), wide[2:]])
         heads = heads.reshape(2, blocks, head_cols)
         qkv_shift = jnp.stack([heads[0], jnp.zeros_like(heads[0]), heads[1]], axis=1)
         return gains, qkv_shift.reshape(1, -1), wide, up_shift[None]
@@ -581,13 +590,12 @@
     stream = dot(inputs, pick)
     for l in range(layers):
         gains, qkv_shift, shifts, up_shift = vectors(l)
-        if l > 1:
-            stream = select_wide(stream, pick)
+        if l == 1:
+            stream = select_wide(stream, unpick)
         if l == 0:
             qkv, low = views(first_whole, 0), inputs
         else:
-            qkv, out = attn_views[l]
-            up, down = mlp_views[l]
+            qkv, out, up, down = later_views[l]
             low = stream.astype(BF)
         (projected,) = times_weight(
             relative_t, low, qkv, 3 * head_cols, add_shift, [qkv_shift], [BF], "project"
@@ -598,31 +606,17 @@
         keys = gather_keys(projected)
         mixture = attend(projected, keys, head_cols, seg_q, seg_k)
         if l == 0:
-            mixture, down_here, later_shards = hold(mixture, down_here, later_shards)
-            later_own = [gather_far(s) for s in later_shards]
+            mixture, down_here = hold(mixture, down_here)
             up, out = block_views(mid_blocks, 0), block_views(mid_blocks, hidden)
             down = block_views(gather_core(down_here), 0)
         attended = times_transposed(relative_t, mixture[None], out, "attended")
         unit_early, rate_early = norm_parts(stream + (attended + shifts[0]))
         mid = unit_early * gains[0] + shifts[1]
-        if l == 0:
-            mid, later_own = hold(mid, later_own)
-            later_sides = [gather_sides(own) for own in later_own]
-        else:
-            mid = select_wide(mid, unpick)
         mid_low = mid.astype(BF)
         hidden_out, slopes = times_weight(
-            same_t, mid_low, up, hidden, enter, [up_shift], [BF, BF], "enter"
+            relative_t, mid_low, up, hidden, enter, [up_shift], [BF, BF], "enter"
         )
-        if l == 0:
-            hidden_out, later_sides = hold(hidden_out, later_sides)
-            later_here = [gather_corners(o, s) for o, s in zip(later_own, later_sides)]
-        branch = times_transposed(same_t, hidden_out[None], down, "branch")
-        if l == 0:
-            branch, later_here = hold(branch, later_here)
-            attn_views = [None]
-            for got in [gather_core(here) for here in later_here]:
-                attn_views.append((block_views(got, 0), block_views(got, 3 * head_cols)))
+        branch = times_transposed(relative_t, hidden_out[None], down, "branch")
         unit_late, rate_late = norm_parts(mid + (branch + shifts[2]))
         stored.append(
             (
@@ -648,7 +642,7 @@
     if layers == 1:
         stream = select_wide(stream, unpick)
 
-    grad_stream = cotangent if layers > 1 else select_wide(cotangent, pick)
+    grad_stream = cotangent
     mlp_done, attn_done = [None] * layers, [None] * layers
     small_grads = [None] * layers
     over_rows = lambda value: jnp.sum(value.astype(F32), axis=0)
@@ -675,47 +669,47 @@
             unit_late,
             rate_late,
         ) = stored[l]
-        if 0 < l < layers - 1:
-            grad_stream = select_wide(grad_stream, unpick)
+        if l == 0:
+            grad_stream = select_wide(grad_stream, pick)
         grad_second = norm_back(grad_stream, unit_late, rate_late, gains[1])
         gain_late, shift_late = over_rows(grad_stream * unit_late), over_rows(grad_stream)
         second_low = grad_second.astype(BF)
-        (grad_pre,) = times_weight(same_t, second_low, down, hidden, leave, [slopes], [BF], "leave")
-        mlp_pairs = [(mid_low, grad_pre[None]), (second_low, hidden_out[None])]
-        if l == 0:
-            if flying is not None:
-                line, corners = flying
-                grad_pre, corners = hold(grad_pre, corners)
-                sides = scatter_sides(line, corners)
-            mlp_send = weight_grads(mlp_pairs, blocks, 1, 2, name="mlp_send")
-            mlp_send, grad_pre = hold(mlp_send, grad_pre)
-            mlp_came = over_dp(mlp_send, 1)
-        else:
-            whole = weight_grads(mlp_pairs, blocks, 0, 1, name="mlp_grads")
-            whole, grad_pre = hold(whole, grad_pre)
-            mlp_done[l] = lax.psum_scatter(
-                whole.reshape(-1, whole.shape[2]), SPREAD, scatter_dimension=0, tiled=True
-            ).astype(F32)
-        grad_mid = grad_second + times_transposed(same_t, grad_pre[None], up, "grad_mid")
-        if l > 0:
-            grad_mid = select_wide(grad_mid, pick)
+        (grad_pre,) = times_weight(relative_t, second_low, down, hidden, leave, [slopes], [BF], "leave")
+        if flying is not None:
+            line, corners, other_line, other_sides = flying
+            grad_pre, corners, other_sides = hold(grad_pre, corners, other_sides)
+            sums = scatter_sum(line, corners)
+            pieces = scatter_pieces(other_line, other_sides)
+            grad_pre, sums, pieces = hold(grad_pre, sums, pieces)
+            sides, other_addends = scatter_sides(sums), scatter_far(pieces)
+        turned = (lambda v: v) if l == 0 else (lambda v: dot(v, pick).astype(BF))
+        mlp_pairs = [(turned(mid_low), grad_pre[None]), (turned(second_low), hidden_out[None])]
+        mlp_send = weight_grads(mlp_pairs, blocks, 1, 2, name="mlp_send")
+        mlp_send, grad_pre = hold(mlp_send, grad_pre)
+        mlp_came = over_dp(mlp_send, 1)
+        back = times_transposed(relative_t, grad_pre[None], up, "grad_mid")
+        mlp_line = weight_grads(
+            mlp_pairs, blocks, 0, 2, add=after(mlp_came, back), blocks=2, name="mlp_keep"
+        )
+        mlp_line, back = hold(mlp_line, back)
+        mlp_corners = scatter_corners(mlp_line)
+        grad_mid = grad_second + back
         grad_first = norm_back(grad_mid, unit_early, rate_early, gains[0])
         gain_early, shift_early = over_rows(grad_mid * unit_early), over_rows(grad_mid)
         first_low = grad_first.astype(BF)
-        if l == 0:
-            first_low, mlp_came = hold(first_low, mlp_came)
-            mlp_line = weight_grads(
-                mlp_pairs, blocks, 0, 2, add=mlp_came, blocks=2, name="mlp_keep"
-            )
-            if flying is not None:
-                first_low, mlp_line, sides = hold(first_low, mlp_line, sides)
-                addends = scatter_far(line, sides)
-            else:
-                first_low, mlp_line = hold(first_low, mlp_line)
-            mlp_corners = scatter_corners(mlp_line)
+        if flying is not None:
+            first_low, sides, other_addends = hold(first_low, sides, other_addends)
+            pieces = scatter_pieces(line, sides)
+            mlp_done[l + 1] = scatter_end(other_addends)
+            first_low, pieces = hold(first_low, pieces)
+            addends = scatter_far(pieces)
         (grad_mix,) = times_weight(
             relative_t, first_low, out, head_cols, lambda v: (v,), [], [BF], "grad_mix"
         )
+        grad_mix, mlp_corners = hold(grad_mix, mlp_corners)
+        mlp_sums = scatter_sum(mlp_line, mlp_corners)
+        grad_mix, mlp_sums = hold(grad_mix, mlp_sums)
+        mlp_sides = scatter_sides(mlp_sums)
         grad_proj = attend_back(projected, keys, head_cols, grad_mix, seg_q, seg_k)
         if sharers > 1:
             grad_proj = jnp.stack(
@@ -725,15 +719,17 @@
                     for v in grad_proj[1:]
                 ]
             )
-        left = dot(low, pick).astype(BF) if l == 0 else low
-        attn_pairs = [(left, grad_proj), (first_low, mixture[None])]
+        left = dot(low, pick).astype(BF)
+        attn_pairs = [(left, grad_proj), (turned(first_low), mixture[None])]
         attn_send = weight_grads(attn_pairs, blocks, 1, 2, name="attn_send")
+        if flying is not None:
+            attn_send, addends = hold(attn_send, addends)
+            attn_done[l + 1] = scatter_end(addends)
         if l == 0:
-            if flying is not None:
-                attn_send, addends = hold(attn_send, addends)
-                attn_done[l + 1] = scatter_end(addends)
-            attn_send, grad_proj, mlp_corners = hold(attn_send, grad_proj, mlp_corners)
-            mlp_sides = scatter_sides(mlp_line, mlp_corners)
+            attn_send, grad_proj, mlp_sides = hold(attn_send, grad_proj, mlp_sides)
+            mlp_pieces = scatter_pieces(mlp_line, mlp_sides)
+            attn_send, grad_proj, mlp_pieces = hold(attn_send, grad_proj, mlp_pieces)
+            mlp_addends = scatter_far(mlp_pieces)
         else:
             attn_send, grad_proj = hold(attn_send, grad_proj)
         attn_came = over_dp(attn_send, 1)
@@ -742,39 +738,47 @@
         attn_line = weight_grads(
             attn_pairs, blocks, 0, 2, add=attn_came, blocks=2, name="attn_keep"
         )
-        heads_grad = jnp.stack([over_rows(grad_proj[0]), over_rows(grad_proj[2])])
         wide_grad = jnp.stack(
             [over_rows(grad_first), shift_early, over_rows(grad_second), shift_late]
         )
         gains_grad = jnp.stack([gain_early, gain_late])
-        ups_grad = over_rows(grad_pre)
-        heads_grad = reorder(heads_grad, relative_t)
         if l == 0:
-            ups_grad = reorder(ups_grad, relative_t)
             wide_grad, gains_grad = reorder(wide_grad, places), reorder(gains_grad, places)
-        else:
-            wide_grad = jnp.concatenate([reorder(wide_grad[:2], places), wide_grad[2:]])
-            gains_grad = jnp.concatenate([reorder(gains_grad[:1], places), gains_grad[1:]])
-        small_grads[l] = gains_grad, jnp.concatenate([heads_grad, wide_grad]), ups_grad
+        small_grads[l] = gains_grad, wide_grad, grad_proj, grad_pre
         if l == 0:
-            smalls = [jnp.stack([small_grads[n][i] for n in range(layers)]) for i in range(3)]
+            attn_line, back = hold(attn_line, back)
+            attn_corners = scatter_corners(attn_line)
+            held = after(small_grads, attn_line)
+            heads_grads = [jnp.stack([over_rows(h[2][0]), over_rows(h[2][2])]) for h in held]
+            smalls = (
+                jnp.stack([h[0] for h in held]),
+                jnp.concatenate(
+                    [
+                        reorder(jnp.stack(heads_grads), relative_t),
+                        jnp.stack([h[1] for h in held]),
+                    ],
+                    axis=1,
+                ),
+                reorder(jnp.stack([over_rows(h[3]) for h in held]), relative_t),
+            )
             small_sums = relative_small(
                 jnp.concatenate([fold(whole) for whole in smalls], axis=1)
             )
-            attn_line, mlp_sides, back, small_sums = hold(attn_line, mlp_sides, back, small_sums)
-            mlp_addends = scatter_far(mlp_line, mlp_sides)
-            attn_corners = scatter_corners(attn_line)
-            attn_corners, mlp_addends = hold(attn_corners, mlp_addends)
-            attn_sides = scatter_sides(attn_line, attn_corners)
-            small_sums = scatter_small(small_sums, 2 * blocks)
+            attn_sums = scatter_sum(*after((attn_line, attn_corners), small_sums))
+            attn_sides = scatter_sides(attn_sums)
+            mlp_addends, small_sums = after((mlp_addends, small_sums), attn_sums)
+            mlp_done[l] = scatter_end(mlp_addends)
+            small_sums = scatter_small(after(small_sums, mlp_done[l]), 4 * blocks)
             attn_sides, small_sums = hold(attn_sides, small_sums)
-            attn_done[l] = scatter_end(scatter_far(attn_line, attn_sides))
-            mlp_done[l] = scatter_end(mlp_addends)
+            attn_pieces = scatter_pieces(attn_line, attn_sides)
+            attn_pieces, small_sums = hold(attn_pieces, small_sums)
+            attn_addends = scatter_far(attn_pieces)
             summed = scatter_small(small_sums, 1)[0]
-            input_grad = select_wide(grad_first, unpick) + back
+            attn_done[l] = scatter_end(after(attn_addends, summed))
+            input_grad = select_wide(after(grad_first, attn_line), unpick) + back
         else:
             attn_line, back = hold(attn_line, back)
-            flying = attn_line, scatter_corners(attn_line)
+            flying = attn_line, scatter_corners(attn_line), mlp_line, mlp_sides
             grad_stream = grad_first + back
 
     return (

time: 851 us -> 796 us (0.935)
  waiting for transfers between devices: 281 us -> 219 us
    ppermute x45 -> x42, waiting for transfers between devices: 182 us -> 135 us  [over_dp(): return lax.ppermute(value, 'dp', [(i, i ^ mask) for i in range(count)])]
    all_gather x2, waiting for transfers between devices: 0.01 us -> 26.1 us  [on_device(): spread = lambda shard: lax.all_gather(shard, SPREAD, axis=0, tiled=True)]
    ppermute x5, waiting for transfers between devices: 30.9 us -> 5.35 us  [swap(): return lax.ppermute(value, RANKS, [(i, i ^ mask) for i in range(count)])]
    ppermute x12, waiting for transfers between devices: 68.4 us -> 52.8 us  [over_tensor(): lax.ppermute(value, ('thi', 'tlo'), [(i, i ^ mask) for i in range(count)])]
    pallas_call x7 -> x8, Pallas kernels: 71 us -> 78.1 us  [weight_grads(): pl.pallas_call(kernel, grid=(sum(counts),), in_specs=in_specs, out_specs=...]
    convert_element_type x11 -> x12, other arithmetic: 16.5 us -> 23.4 us  [the longest x4 11.9 us: scatter_pieces(): return [piece(0)] + [piece(m).astype(BF) for m in range(1, rest)]]
    dot_general x10 -> x14, matrix products: 27.7 us -> 30.5 us  [dot(): return jnp.dot(a, b, preferred_element_type=F32)]
    ppermute x45 -> x42, starting transfers between devices: 41.5 us -> 39.4 us  [over_dp(): return lax.ppermute(value, 'dp', [(i, i ^ mask) for i in range(count)])]
  transfers between devices with their start and end apart: 65 -> 61, of which waited for: 27 -> 31; matrix products, arithmetic and copies ran while one was open for 17% -> 16% of each run, Pallas kernels for 29% -> 23%
where the time goes in v3:
time: 796 us; the launch traced here: 789 us
  Pallas kernels  306 us (38%)
  waiting for transfers between devices  219 us (28%)
  other arithmetic  92.6 us (12%)
  local copies, waits for them, and re-layouts  65.7 us (8%)
  starting transfers between devices  59.4 us (7%)
  matrix products  30.5 us (4%)
  between operations  16.1 us (2%)
    ppermute x42, waiting for transfers between devices, over_dp(): return lax.ppermute(value, 'dp', [(i, i ^ mask) for i in range(count)])  135 us
    pallas_call x8, Pallas kernels, times_transposed(): pl.pallas_call(kernel, grid_spec=pltpu.PrefetchScalarGridSpec(num_scalar_...  79.5 us
    pallas_call x8, Pallas kernels, weight_grads(): pl.pallas_call(kernel, grid=(sum(counts),), in_specs=in_specs, out_specs=...  78.1 us
    pallas_call x8, Pallas kernels, times_weight(): pl.pallas_call(kernel, grid_spec=pltpu.PrefetchScalarGridSpec(num_scalar_...  75.5 us
    ppermute x12, waiting for transfers between devices, over_tensor(): lax.ppermute(value, ('thi', 'tlo'), [(i, i ^ mask) for i in range(count)])  52.8 us
    pallas_call x2, Pallas kernels, attend_back(): pl.pallas_call(attend_back_kernel, grid=(sets, parts * pairs), in_specs=s...  45.9 us
    ppermute x42, starting transfers between devices, over_dp(): return lax.ppermute(value, 'dp', [(i, i ^ mask) for i in range(count)])  39.4 us
    dot_general x14, matrix products, dot(): return jnp.dot(a, b, preferred_element_type=F32)  30.5 us
  transfers between devices with their start and end apart: 61, of which 31 were waited for; matrix products, arithmetic and copies ran while one was open for 16% of the time, Pallas kernels for 23%

profile of v3, /device:TPU:8, one launch (start us, length us, event | category | flops | bytes accessed | tf_op | source)
XLA Modules:
  0.0 788.8 jit_solution(8225539900540277954)
XLA Ops:
  18.8 24.4 %collective-permute-done.2 = bf16[64,2560]{1,0:T(8,128)(2,1)S(1)} collective-permute-done((bf16[64,2560]{1,0:T(8,128)(2,1)S(1)}, bf16[64,2560]{1,0:T(8,128)(2,1)S(1)}, u32[]{:S(2)}, u32[]{:S(2)}) %collective-permute-start.2) | collective-permute-done | bytes 327712 | tf_op jit(solution)/shard_map/ppermute | solution.py:376
  58.3 31.7 %collective-permute-done.6.refs_6_.refs_4_ = bf16[256,2560]{1,0:T(8,128)(2,1)S(1)} collective-permute-done((bf16[256,2560]{1,0:T(8,128)(2,1)S(1)}, bf16[256,2560]{1,0:T(8,128)(2,1)S(1)}, u32[]{:S(2)}, u32[]{:S(2)}) %collective-permute-start.6) | collective-permute-done | bytes 1310752 | tf_op jit(solution)/shard_map/ppermute | solution.py:381
  103.4 14.8 %collective-permute-done.5 = bf16[64,2048]{1,0:T(8,128)(2,1)} collective-permute-done((bf16[64,2048]{1,0:T(8,128)(2,1)S(1)}, bf16[64,2048]{1,0:T(8,128)(2,1)}, u32[]{:S(2)}, u32[]{:S(2)}) %collective-permute-start.5) | collective-permute-done | bytes 262176 | tf_op jit(solution)/shard_map/ppermute | solution.py:376
  139.3 8.8 %project.2.q_ref.k_ref.v_ref = bf16[512,3072]{1,0:T(8,128)(2,1)} custom-call(s32[2]{0:T(128)} %iota_xor_fusion.which_ref, bf16[512,1024]{1,0:T(8,128)(2,1)} %x_ref.1, bf16[2048,1664]{1,0:T(8,128)(2,1)} %all-gather.3.cloned.1.call-done.refs_0_.refs_1_.refs_2_.refs_3_, bf16[2048,1664]{1,0:T(8,128)(2,1)} %all-gather.3.cloned.1.call-done.refs_0_.refs_1_.refs_2_.refs_3_, ...), custom_call_target="tpu_custom_call" | custom-call | flops 3221225472 | bytes 2097152 | tf_op jit(solution)/shard_map/project/pallas_call | solution.py:192
  148.1 9.2 %collective-permute-done.10.refs_3_.refs_1_ = bf16[256,2048]{1,0:T(8,128)(2,1)} collective-permute-done((bf16[256,2048]{1,0:T(8,128)(2,1)}, bf16[256,2048]{1,0:T(8,128)(2,1)}, u32[]{:S(2)}, u32[]{:S(2)}) %collective-permute-start.10) | collective-permute-done | bytes 1048608 | tf_op jit(solution)/shard_map/ppermute | solution.py:376
  170.8 13.6 %collective-permute-done.13 = bf16[128,2048]{1,0:T(8,128)(2,1)} collective-permute-done((bf16[128,2048]{1,0:T(8,128)(2,1)}, bf16[128,2048]{1,0:T(8,128)(2,1)}, u32[]{:S(2)}, u32[]{:S(2)}) %collective-permute-start.13) | collective-permute-done | bytes 524320 | tf_op jit(solution)/shard_map/ppermute | solution.py:381
  187.4 13.3 %attend.2 = bf16[512,1024]{1,0:T(8,128)(2,1)} custom-call(bf16[512,3072]{1,0:T(8,128)(2,1)} %project.2.q_ref.k_ref.v_ref, bf16[512,3072]{1,0:T(8,128)(2,1)} %project.2.q_ref.k_ref.v_ref, bf16[512,3072]{1,0:T(8,128)(2,1)} %project.2.q_ref.k_ref.v_ref, s32[1,1,512]{2,1,0:T(1,128)} %get-tuple-element.431.segq_ref, s32[1,512,1]{2,1,0:T(8,128)} %copy.49.segk_ref), custom_call_target="tpu_custom_call" | custom-call | flops 4294967296 | bytes 6291456 | tf_op jit(solution)/shard_map/attend/pallas_call | solution.py:106
  214.6 13.0 %enter.2 = (bf16[512,4096]{1,0:T(8,128)(2,1)}, bf16[512,4096]{1,0:T(8,128)(2,1)}) custom-call(s32[2]{0:T(128)} %iota_xor_fusion.which_ref, bf16[512,1024]{1,0:T(8,128)(2,1)} %fusion.31.x_ref.refs_0_, bf16[256,2560]{1,0:T(8,128)(2,1)} %copy-done.6, bf16[256,2560]{1,0:T(8,128)(2,1)} %collective-permute-done.7.refs_3_.refs_1_, ...), custom_call_target="tpu_custom_call" | custom-call | flops 4294967296 | bytes 2097152 | tf_op jit(solution)/shard_map/enter/pallas_call | solution.py:192
  228.6 15.8 %branch.2 = f32[512,1024]{1,0:T(8,128)} custom-call(s32[2]{0:T(128)} %iota_xor_fusion.which_ref, bf16[1,512,4096]{2,1,0:T(8,128)(2,1)} %bitcast.198, bf16[1,512,4096]{2,1,0:T(8,128)(2,1)} %bitcast.199, bf16[256,2048]{1,0:T(8,128)(2,1)} %pad_maximum_fusion.5.refs_2_.refs_0_, bf16[256,2048]{1,0:T(8,128)(2,1)} %collective-permute-done.10.refs_3_.refs_1_, ...), custom_call_target="tpu_custom_call" | custom-call | flops 4294967296 | bytes 4194304 | tf_op jit(solution)/shard_map/branch/pallas_call | solution.py:246
  254.2 26.1 %all-gather.5.cloned.1.call-done.refs_0_.refs_1_.refs_2_.refs_3_ = bf16[2048,6144]{1,0:T(8,128)(2,1)} async-done(((bf16[64,6144]{1,0:T(8,128)(2,1)}), bf16[2048,6144]{1,0:T(8,128)(2,1)}) %all-gather.5.cloned.1.call-update) | async-done | bytes 25165840 | tf_op jit(solution)/shard_map/all_gather | solution.py:536
  280.3 8.5 %project.3.q_ref.k_ref.v_ref = bf16[512,3072]{1,0:T(8,128)(2,1)} custom-call(s32[2]{0:T(128)} %iota_xor_fusion.which_ref, bf16[512,1024]{1,0:T(8,128)(2,1)} %get-tuple-element.441.x_ref, bf16[2048,6144]{1,0:T(8,128)(2,1)} %all-gather.5.cloned.1.call-done.refs_0_.refs_1_.refs_2_.refs_3_, ...), custom_call_target="tpu_custom_call" | custom-call | flops 3221225472 | bytes 2097152 | tf_op jit(solution)/shard_map/project/pallas_call | solution.py:192
  288.9 13.4 %attend.3 = bf16[512,1024]{1,0:T(8,128)(2,1)} custom-call(bf16[512,3072]{1,0:T(8,128)(2,1)} %project.3.q_ref.k_ref.v_ref, bf16[512,3072]{1,0:T(8,128)(2,1)} %project.3.q_ref.k_ref.v_ref, bf16[512,3072]{1,0:T(8,128)(2,1)} %project.3.q_ref.k_ref.v_ref, s32[1,1,512]{2,1,0:T(1,128)} %get-tuple-element.431.segq_ref, s32[1,512,1]{2,1,0:T(8,128)} %copy.49.segk_ref), custom_call_target="tpu_custom_call" | custom-call | flops 4294967296 | bytes 6291456 | tf_op jit(solution)/shard_map/attend/pallas_call | solution.py:106
  313.3 13.3 %enter.3 = (bf16[512,4096]{1,0:T(8,128)(2,1)}, bf16[512,4096]{1,0:T(8,128)(2,1)}) custom-call(s32[2]{0:T(128)} %iota_xor_fusion.which_ref, bf16[512,1024]{1,0:T(8,128)(2,1)} %copy-done.20, bf16[2048,6144]{1,0:T(8,128)(2,1)} %all-gather.5.cloned.1.call-done.refs_0_.refs_1_.refs_2_.refs_3_, ...), custom_call_target="tpu_custom_call" | custom-call | flops 4294967296 | bytes 2097152 | tf_op jit(solution)/shard_map/enter/pallas_call | solution.py:192
  326.6 10.0 %branch.3 = f32[512,1024]{1,0:T(8,128)} custom-call(s32[2]{0:T(128)} %iota_xor_fusion.which_ref, bf16[1,512,4096]{2,1,0:T(8,128)(2,1)} %bitcast.192, bf16[1,512,4096]{2,1,0:T(8,128)(2,1)} %bitcast.193, bf16[2048,6144]{1,0:T(8,128)(2,1)} %all-gather.5.cloned.1.call-done.refs_0_.refs_1_.refs_2_.refs_3_, ...), custom_call_target="tpu_custom_call" | custom-call | flops 4294967296 | bytes 4194304 | tf_op jit(solution)/shard_map/branch/pallas_call | solution.py:246
  346.8 10.7 %leave.2 = bf16[512,4096]{1,0:T(8,128)(2,1)} custom-call(s32[2]{0:T(128)} %iota_xor_fusion.which_ref, bf16[512,1024]{1,0:T(8,128)(2,1)} %copy-done.17, bf16[2048,6144]{1,0:T(8,128)(2,1)} %all-gather.5.cloned.1.call-done.refs_0_.refs_1_.refs_2_.refs_3_, bf16[2048,6144]{1,0:T(8,128)(2,1)} %all-gather.5.cloned.1.call-done.refs_0_.refs_1_.refs_2_.refs_3_, ...), custom_call_target="tpu_custom_call" | custom-call | flops 536870912 | bytes 262144 | tf_op jit(solution)/shard_map/leave/pallas_call | solution.py:192
  357.5 10.9 %mlp_send.2 = bf16[2,512,4096]{2,1,0:T(8,128)(2,1)} custom-call(bf16[512,1024]{1,0:T(8,128)(2,1)} %fusion.33.refs_0_, bf16[1,512,4096]{2,1,0:T(8,128)(2,1)} %bitcast.180, bf16[1,512,4096]{2,1,0:T(8,128)(2,1)} %bitcast.181, bf16[512,1024]{1,0:T(8,128)(2,1)} %fusion.34.refs_3_, bf16[1,512,4096]{2,1,0:T(8,128)(2,1)} %bitcast.194, bf16[1,512,4096]{2,1,0:T(8,128)(2,1)} %bitcast.195), custom_call_target="tpu_custom_call" | custom-call | flops 536870912 | bytes 1048576 | tf_op jit(solution)/shard_map/mlp_send/pallas_call | solution.py:323
  371.0 10.0 %grad_mid.2 = f32[512,1024]{1,0:T(8,128)} custom-call(s32[2]{0:T(128)} %iota_xor_fusion.which_ref, bf16[1,512,4096]{2,1,0:T(8,128)(2,1)} %bitcast.182, bf16[1,512,4096]{2,1,0:T(8,128)(2,1)} %bitcast.183, bf16[2048,6144]{1,0:T(8,128)(2,1)} %all-gather.5.cloned.1.call-done.refs_0_.refs_1_.refs_2_.refs_3_, ...), custom_call_target="tpu_custom_call" | custom-call | flops 536870912 | bytes 524288 | tf_op jit(solution)/shard_map/grad_mid/pallas_call | solution.py:246
  382.0 12.1 %mlp_keep.2 = (bf16[256,4096]{1,0:T(8,128)(2,1)}, bf16[256,4096]{1,0:T(8,128)(2,1)}, bf16[256,4096]{1,0:T(8,128)(2,1)}, bf16[256,4096]{1,0:T(8,128)(2,1)}) custom-call(bf16[512,1024]{1,0:T(8,128)(2,1)} %fusion.33.refs_0_, bf16[1,512,4096]{2,1,0:T(8,128)(2,1)} %bitcast.184, bf16[1,512,4096]{2,1,0:T(8,128)(2,1)} %bitcast.185, ...), custom_call_target="tpu_custom_call" | custom-call | flops 536870912 | bytes 1048576 | tf_op jit(solution)/shard_map/mlp_keep/pallas_call | solution.py:323
  412.7 11.9 %collective-permute-done.23 = bf16[128,4096]{1,0:T(8,128)(2,1)} collective-permute-done((bf16[128,4096]{1,0:T(8,128)(2,1)}, bf16[128,4096]{1,0:T(8,128)(2,1)}, u32[]{:S(2)}, u32[]{:S(2)}) %collective-permute-start.23) | collective-permute-done | bytes 1048608 | tf_op jit(solution)/shard_map/ppermute | solution.py:376
  431.8 22.8 %attend_back.2.refs_1_.refs_2_.refs_0_ = bf16[3,512,1024]{2,1,0:T(8,128)(2,1)} custom-call(bf16[512,3072]{1,0:T(8,128)(2,1)} %project.3.q_ref.k_ref.v_ref, bf16[512,3072]{1,0:T(8,128)(2,1)} %project.3.q_ref.k_ref.v_ref, bf16[512,3072]{1,0:T(8,128)(2,1)} %project.3.q_ref.k_ref.v_ref, bf16[512,1024]{1,0:T(8,128)(2,1)} %grad_mix.2.grad_ref, ...), custom_call_target="tpu_custom_call" | custom-call | flops 1342177280 | bytes 1572864 | tf_op jit(solution)/shard_map/attend_back/pallas_call | solution.py:134
  464.0 8.6 %grad_stream.2 = f32[512,1024]{1,0:T(8,128)} custom-call(s32[2]{0:T(128)} %iota_xor_fusion.which_ref, bf16[3,512,1024]{2,1,0:T(8,128)(2,1)} %attend_back.2.refs_1_.refs_2_.refs_0_, bf16[3,512,1024]{2,1,0:T(8,128)(2,1)} %attend_back.2.refs_1_.refs_2_.refs_0_, bf16[2048,6144]{1,0:T(8,128)(2,1)} %all-gather.5.cloned.1.call-done.refs_0_.refs_1_.refs_2_.refs_3_, ...), custom_call_target="tpu_custom_call" | custom-call | flops 402653184 | bytes 393216 | tf_op jit(solution)/shard_map/grad_stream/pallas_call | solution.py:246
  472.6 9.0 %attn_keep.2 = (bf16[256,2048]{1,0:T(8,128)(2,1)}, bf16[256,2048]{1,0:T(8,128)(2,1)}, bf16[256,2048]{1,0:T(8,128)(2,1)}, bf16[256,2048]{1,0:T(8,128)(2,1)}) custom-call(bf16[512,1024]{1,0:T(8,128)(2,1)} %fusion.35.refs_0_, bf16[3,512,1024]{2,1,0:T(8,128)(2,1)} %attend_back.2.refs_1_.refs_2_.refs_0_, ...), custom_call_target="tpu_custom_call" | custom-call | flops 268435456 | bytes 524288 | tf_op jit(solution)/shard_map/attn_keep/pallas_call | solution.py:323
  493.8 11.2 %leave.3 = bf16[512,4096]{1,0:T(8,128)(2,1)} custom-call(s32[2]{0:T(128)} %iota_xor_fusion.which_ref, bf16[512,1024]{1,0:T(8,128)(2,1)} %convert_element_type.434.x_ref.refs_3_, bf16[256,2048]{1,0:T(8,128)(2,1)} %pad_maximum_fusion.5.refs_2_.refs_0_, bf16[256,2048]{1,0:T(8,128)(2,1)} %collective-permute-done.10.refs_3_.refs_1_, ...), custom_call_target="tpu_custom_call" | custom-call | flops 536870912 | bytes 262144 | tf_op jit(solution)/shard_map/leave/pallas_call | solution.py:192
  511.3 10.1 %collective-permute-done.26 = bf16[128,2048]{1,0:T(8,128)(2,1)} collective-permute-done((bf16[128,2048]{1,0:T(8,128)(2,1)}, bf16[128,2048]{1,0:T(8,128)(2,1)}, u32[]{:S(2)}, u32[]{:S(2)}) %collective-permute-start.26) | collective-permute-done | bytes 524320 | tf_op jit(solution)/shard_map/ppermute | solution.py:376
  530.7 10.6 %mlp_send.3 = bf16[2,512,4096]{2,1,0:T(8,128)(2,1)} custom-call(bf16[512,1024]{1,0:T(8,128)(2,1)} %fusion.31.x_ref.refs_0_, bf16[1,512,4096]{2,1,0:T(8,128)(2,1)} %bitcast.186, bf16[1,512,4096]{2,1,0:T(8,128)(2,1)} %bitcast.187, bf16[512,1024]{1,0:T(8,128)(2,1)} %convert_element_type.434.x_ref.refs_3_, bf16[1,512,4096]{2,1,0:T(8,128)(2,1)} %bitcast.200, ...), custom_call_target="tpu_custom_call" | custom-call | flops 536870912 | bytes 1048576 | tf_op jit(solution)/shard_map/mlp_send/pallas_call | solution.py:323
  547.3 15.5 %grad_mid.3 = f32[512,1024]{1,0:T(8,128)} custom-call(s32[2]{0:T(128)} %iota_xor_fusion.which_ref, bf16[1,512,4096]{2,1,0:T(8,128)(2,1)} %bitcast.188, bf16[1,512,4096]{2,1,0:T(8,128)(2,1)} %bitcast.189, bf16[256,2560]{1,0:T(8,128)(2,1)} %copy-done.6, bf16[256,2560]{1,0:T(8,128)(2,1)} %collective-permute-done.7.refs_3_.refs_1_, ...), custom_call_target="tpu_custom_call" | custom-call | flops 536870912 | bytes 524288 | tf_op jit(solution)/shard_map/grad_mid/pallas_call | solution.py:246
  562.9 12.1 %mlp_keep.3 = (bf16[256,4096]{1,0:T(8,128)(2,1)}, bf16[256,4096]{1,0:T(8,128)(2,1)}, bf16[256,4096]{1,0:T(8,128)(2,1)}, bf16[256,4096]{1,0:T(8,128)(2,1)}) custom-call(bf16[512,1024]{1,0:T(8,128)(2,1)} %fusion.31.x_ref.refs_0_, bf16[1,512,4096]{2,1,0:T(8,128)(2,1)} %bitcast.190, bf16[1,512,4096]{2,1,0:T(8,128)(2,1)} %bitcast.191, ...), custom_call_target="tpu_custom_call" | custom-call | flops 536870912 | bytes 1048576 | tf_op jit(solution)/shard_map/mlp_keep/pallas_call | solution.py:323
  617.9 23.0 %attend_back.3.refs_1_.refs_2_.refs_0_ = bf16[3,512,1024]{2,1,0:T(8,128)(2,1)} custom-call(bf16[512,3072]{1,0:T(8,128)(2,1)} %project.2.q_ref.k_ref.v_ref, bf16[512,3072]{1,0:T(8,128)(2,1)} %project.2.q_ref.k_ref.v_ref, bf16[512,3072]{1,0:T(8,128)(2,1)} %project.2.q_ref.k_ref.v_ref, bf16[512,1024]{1,0:T(8,128)(2,1)} %grad_mix.3.grad_ref, ...), custom_call_target="tpu_custom_call" | custom-call | flops 1342177280 | bytes 1572864 | tf_op jit(solution)/shard_map/attend_back/pallas_call | solution.py:134
  648.3 8.8 %collective-permute-done.41 = bf16[256,4096]{1,0:T(8,128)(2,1)} collective-permute-done((bf16[256,4096]{1,0:T(8,128)(2,1)}, bf16[256,4096]{1,0:T(8,128)(2,1)}, u32[]{:S(2)}, u32[]{:S(2)}) %collective-permute-start.41) | collective-permute-done | bytes 2097184 | tf_op jit(solution)/shard_map/ppermute | solution.py:376
  676.7 8.6 %grad_stream.3 = f32[512,1024]{1,0:T(8,128)} custom-call(s32[2]{0:T(128)} %iota_xor_fusion.which_ref, bf16[3,512,1024]{2,1,0:T(8,128)(2,1)} %attend_back.3.refs_1_.refs_2_.refs_0_, bf16[3,512,1024]{2,1,0:T(8,128)(2,1)} %attend_back.3.refs_1_.refs_2_.refs_0_, bf16[2048,1664]{1,0:T(8,128)(2,1)} %all-gather.3.cloned.1.call-done.refs_0_.refs_1_.refs_2_.refs_3_, ...), custom_call_target="tpu_custom_call" | custom-call | flops 402653184 | bytes 393216 | tf_op jit(solution)/shard_map/grad_stream/pallas_call | solution.py:246
  685.3 8.7 %attn_keep.3 = (bf16[256,2048]{1,0:T(8,128)(2,1)}, bf16[256,2048]{1,0:T(8,128)(2,1)}, bf16[256,2048]{1,0:T(8,128)(2,1)}, bf16[256,2048]{1,0:T(8,128)(2,1)}) custom-call(bf16[512,1024]{1,0:T(8,128)(2,1)} %get-tuple-element.444.refs_0_, bf16[3,512,1024]{2,1,0:T(8,128)(2,1)} %attend_back.3.refs_1_.refs_2_.refs_0_, ...), custom_call_target="tpu_custom_call" | custom-call | flops 268435456 | bytes 524288 | tf_op jit(solution)/shard_map/attn_keep/pallas_call | solution.py:323
  734.6 8.1 %collective-permute-done.46 = bf16[256,2048]{1,0:T(8,128)(2,1)S(1)} collective-permute-done((bf16[256,2048]{1,0:T(8,128)(2,1)S(1)}, bf16[256,2048]{1,0:T(8,128)(2,1)S(1)}, u32[]{:S(2)}, u32[]{:S(2)}) %collective-permute-start.46) | collective-permute-done | bytes 1048608 | tf_op jit(solution)/shard_map/ppermute | solution.py:376
  (566 shorter events, 344.1 us)
Async XLA Ops:
  7.2 121.5 %all-gather.3.cloned.1.call-start = ((), (), s32[]{:S(2)}) async-start(), calls=%async_computation | async-start | bytes 7028736 | tf_op jit(solution)/shard_map/all_gather | solution.py:536
  11.5 268.8 %all-gather.5.cloned.1.call-start = ((), (), s32[]{:S(2)}) async-start(), calls=%async_computation.1 | async-start | bytes 25952256 | tf_op jit(solution)/shard_map/all_gather | solution.py:536
  14.1 29.1 %collective-permute-start.2 = (bf16[64,2560]{1,0:T(8,128)(2,1)S(1)}, bf16[64,2560]{1,0:T(8,128)(2,1)S(1)}, u32[]{:S(2)}, u32[]{:S(2)}) collective-permute-start(bf16[64,2560]{1,0:T(8,128)(2,1)S(1)} %pad_maximum_fusion.14), channel_id=1, source_target_pairs={{0,24},{2,26},{4,28},{6,30},{8,16},{10,18},{12,20},{14,22},{16,8},... | collective-permute-start | bytes 983048 | tf_op jit(solution)/shard_map/ppermute | solution.py:376
  15.7 32.6 %collective-permute-start.1 = (bf16[64,2560]{1,0:T(8,128)(2,1)S(1)}, bf16[64,2560]{1,0:T(8,128)(2,1)S(1)}, u32[]{:S(2)}, u32[]{:S(2)}) collective-permute-start(bf16[64,2560]{1,0:T(8,128)(2,1)S(1)} %pad_maximum_fusion.14), channel_id=1, source_target_pairs={{0,16},{2,18},{4,20},{6,22},{8,24},{10,26},{12,28},{14,30},{16,0},... | collective-permute-start | bytes 983048 | tf_op jit(solution)/shard_map/ppermute | solution.py:376
  16.8 31.5 %collective-permute-start = (bf16[64,2560]{1,0:T(8,128)(2,1)S(1)}, bf16[64,2560]{1,0:T(8,128)(2,1)}, u32[]{:S(2)}, u32[]{:S(2)}) collective-permute-start(bf16[64,2560]{1,0:T(8,128)(2,1)S(1)} %pad_maximum_fusion.14), channel_id=1, source_target_pairs={{0,8},{2,10},{4,12},{6,14},{8,0},{10,2},{12,4},{14,6},{16,24},{18,... | collective-permute-start | bytes 983048 | tf_op jit(solution)/shard_map/ppermute | solution.py:376
  49.5 40.5 %collective-permute-start.6 = (bf16[256,2560]{1,0:T(8,128)(2,1)S(1)}, bf16[256,2560]{1,0:T(8,128)(2,1)S(1)}, u32[]{:S(2)}, u32[]{:S(2)}) collective-permute-start(bf16[256,2560]{1,0:T(8,128)(2,1)S(1)} %pad_maximum_fusion.4.refs_2_.refs_0_), channel_id=1, source_target_pairs={{0,1},{1,0},{2,3},{3,2},{4,5},{5,4},{6,7},{7,6},{8,9},{9,8},{10,11... | collective-permute-start | bytes 3932168 | tf_op jit(solution)/shard_map/ppermute | solution.py:381
  51.2 46.9 %collective-permute-start.7 = (bf16[256,2560]{1,0:T(8,128)(2,1)S(1)}, bf16[256,2560]{1,0:T(8,128)(2,1)}, u32[]{:S(2)}, u32[]{:S(2)}) collective-permute-start(bf16[256,2560]{1,0:T(8,128)(2,1)S(1)} %pad_maximum_fusion.4.refs_2_.refs_0_), channel_id=1, source_target_pairs={{0,4},{2,6},{4,0},{6,2},{8,12},{10,14},{12,8},{14,10},{16,20},{18,... | collective-permute-start | bytes 3932168 | tf_op jit(solution)/shard_map/ppermute | solution.py:376
  90.9 32.5 %collective-permute-start.8 = (bf16[128,2560]{1,0:T(8,128)(2,1)}, bf16[128,2560]{1,0:T(8,128)(2,1)S(1)}, u32[]{:S(2)}, u32[]{:S(2)}) collective-permute-start(bf16[128,2560]{1,0:T(8,128)(2,1)} %slice.665), channel_id=1, source_target_pairs={{0,4},{2,6},{4,0},{6,2},{8,12},{10,14},{12,8},{14,10},{16,20},{18,... | collective-permute-start | bytes 1966088 | tf_op jit(solution)/shard_map/ppermute | solution.py:376
  92.9 27.7 %collective-permute-start.4 = (bf16[64,2048]{1,0:T(8,128)(2,1)S(1)}, bf16[64,2048]{1,0:T(8,128)(2,1)}, u32[]{:S(2)}, u32[]{:S(2)}) collective-permute-start(bf16[64,2048]{1,0:T(8,128)(2,1)S(1)} %slice_bitcast_fusion.6), channel_id=1, source_target_pairs={{0,16},{2,18},{4,20},{6,22},{8,24},{10,26},{12,28},{14,30},{16,0},... | collective-permute-start | bytes 786440 | tf_op jit(solution)/shard_map/ppermute | solution.py:376
  118.2 84.8 %collective-permute-start.14 = (bf16[256,2560]{1,0:T(8,128)(2,1)S(1)}, bf16[256,2560]{1,0:T(8,128)(2,1)}, u32[]{:S(2)}, u32[]{:S(2)}) collective-permute-start(bf16[256,2560]{1,0:T(8,128)(2,1)S(1)} %pad_maximum_fusion.4.refs_2_.refs_0_), channel_id=1, source_target_pairs={{0,2},{2,0},{4,6},{6,4},{8,10},{10,8},{12,14},{14,12},{16,18},{18,... | collective-permute-start | bytes 3932168 | tf_op jit(solution)/shard_map/ppermute | solution.py:376
  122.9 80.7 %collective-permute-start.15 = (bf16[256,2560]{1,0:T(8,128)(2,1)}, bf16[256,2560]{1,0:T(8,128)(2,1)}, u32[]{:S(2)}, u32[]{:S(2)}) collective-permute-start(bf16[256,2560]{1,0:T(8,128)(2,1)} %collective-permute-done.7.refs_3_.refs_1_), channel_id=1, source_target_pairs={{0,2},{2,0},{4,6},{6,4},{8,10},{10,8},{12,14},{14,12},{16,18},{18,... | collective-permute-start | bytes 3932168 | tf_op jit(solution)/shard_map/ppermute | solution.py:376
  122.9 80.8 %collective-permute-start.16 = (bf16[256,2560]{1,0:T(8,128)(2,1)S(1)}, bf16[256,2560]{1,0:T(8,128)(2,1)}, u32[]{:S(2)}, u32[]{:S(2)}) collective-permute-start(bf16[256,2560]{1,0:T(8,128)(2,1)S(1)} %collective-permute-done.6.refs_6_.refs_4_), channel_id=1, source_target_pairs={{0,2},{2,0},{4,6},{6,4},{8,10},{10,8},{12,14},{14,12},{16,18},{18,... | collective-permute-start | bytes 3932168 | tf_op jit(solution)/shard_map/ppermute | solution.py:376
  126.2 31.0 %collective-permute-start.10 = (bf16[256,2048]{1,0:T(8,128)(2,1)}, bf16[256,2048]{1,0:T(8,128)(2,1)}, u32[]{:S(2)}, u32[]{:S(2)}) collective-permute-start(bf16[256,2048]{1,0:T(8,128)(2,1)} %pad_maximum_fusion.5.refs_2_.refs_0_), channel_id=1, source_target_pairs={{0,4},{2,6},{4,0},{6,2},{8,12},{10,14},{12,8},{14,10},{16,20},{18,... | collective-permute-start | bytes 3145736 | tf_op jit(solution)/shard_map/ppermute | solution.py:376
  126.8 30.9 %collective-permute-start.11 = (bf16[256,2048]{1,0:T(8,128)(2,1)}, bf16[256,2048]{1,0:T(8,128)(2,1)}, u32[]{:S(2)}, u32[]{:S(2)}) collective-permute-start(bf16[256,2048]{1,0:T(8,128)(2,1)} %pad_maximum_fusion.5.refs_2_.refs_0_), channel_id=1, source_target_pairs={{0,1},{1,0},{2,3},{3,2},{4,5},{5,4},{6,7},{7,6},{8,9},{9,8},{10,11... | collective-permute-start | bytes 3145736 | tf_op jit(solution)/shard_map/ppermute | solution.py:381
  157.2 46.8 %collective-permute-start.17 = (bf16[256,2560]{1,0:T(8,128)(2,1)}, bf16[256,2560]{1,0:T(8,128)(2,1)}, u32[]{:S(2)}, u32[]{:S(2)}) collective-permute-start(bf16[256,2560]{1,0:T(8,128)(2,1)} %constant_dynamic-update-slice_fusion.refs_7_.refs_5_), channel_id=1, source_target_pairs={{0,2},{2,0},{4,6},{6,4},{8,10},{10,8},{12,14},{14,12},{16,18},{18,... | collective-permute-start | bytes 3932168 | tf_op jit(solution)/shard_map/ppermute | solution.py:376
  461.9 48.8 %collective-permute-start.28 = (bf16[256,4096]{1,0:T(8,128)(2,1)}, bf16[256,4096]{1,0:T(8,128)(2,1)}, u32[]{:S(2)}, u32[]{:S(2)}) collective-permute-start(bf16[256,4096]{1,0:T(8,128)(2,1)} %pad_maximum_fusion), channel_id=1, source_target_pairs={{0,4},{2,6},{4,0},{6,2},{8,12},{10,14},{12,8},{14,10},{16,20},{18,... | collective-permute-start | bytes 6291464 | tf_op jit(solution)/shard_map/ppermute | solution.py:376
  462.5 48.8 %collective-permute-start.29 = (bf16[256,4096]{1,0:T(8,128)(2,1)}, bf16[256,4096]{1,0:T(8,128)(2,1)}, u32[]{:S(2)}, u32[]{:S(2)}) collective-permute-start(bf16[256,4096]{1,0:T(8,128)(2,1)} %pad_maximum_fusion.1), channel_id=1, source_target_pairs={{0,1},{1,0},{2,3},{3,2},{4,5},{5,4},{6,7},{7,6},{8,9},{9,8},{10,11... | collective-permute-start | bytes 6291464 | tf_op jit(solution)/shard_map/ppermute | solution.py:381
  485.4 36.0 %collective-permute-start.26 = (bf16[128,2048]{1,0:T(8,128)(2,1)}, bf16[128,2048]{1,0:T(8,128)(2,1)}, u32[]{:S(2)}, u32[]{:S(2)}) collective-permute-start(bf16[128,2048]{1,0:T(8,128)(2,1)} %get-tuple-element.410), channel_id=1, source_target_pairs={{0,4},{2,6},{4,0},{6,2},{8,12},{10,14},{12,8},{14,10},{16,20},{18,... | collective-permute-start | bytes 1572872 | tf_op jit(solution)/shard_map/ppermute | solution.py:376
  486.1 35.7 %collective-permute-start.27 = (bf16[128,2048]{1,0:T(8,128)(2,1)}, bf16[128,2048]{1,0:T(8,128)(2,1)}, u32[]{:S(2)}, u32[]{:S(2)}) collective-permute-start(bf16[128,2048]{1,0:T(8,128)(2,1)} %get-tuple-element.409), channel_id=1, source_target_pairs={{0,1},{1,0},{2,3},{3,2},{4,5},{5,4},{6,7},{7,6},{8,9},{9,8},{10,11... | collective-permute-start | bytes 1572872 | tf_op jit(solution)/shard_map/ppermute | solution.py:381
  541.3 51.7 %collective-permute-start.31 = (bf16[256,2048]{1,0:T(8,128)(2,1)}, bf16[256,2048]{1,0:T(8,128)(2,1)}, u32[]{:S(2)}, u32[]{:S(2)}) collective-permute-start(bf16[256,2048]{1,0:T(8,128)(2,1)} %pad_maximum_fusion.7), channel_id=1, source_target_pairs={{0,4},{2,6},{4,0},{6,2},{8,12},{10,14},{12,8},{14,10},{16,20},{18,... | collective-permute-start | bytes 3145736 | tf_op jit(solution)/shard_map/ppermute | solution.py:376
  542.8 50.2 %collective-permute-start.32 = (bf16[256,2048]{1,0:T(8,128)(2,1)}, bf16[256,2048]{1,0:T(8,128)(2,1)}, u32[]{:S(2)}, u32[]{:S(2)}) collective-permute-start(bf16[256,2048]{1,0:T(8,128)(2,1)} %pad_maximum_fusion.8), channel_id=1, source_target_pairs={{0,1},{1,0},{2,3},{3,2},{4,5},{5,4},{6,7},{7,6},{8,9},{9,8},{10,11... | collective-permute-start | bytes 3145736 | tf_op jit(solution)/shard_map/ppermute | solution.py:381
  543.4 36.1 %collective-permute-start.33 = (bf16[64,4096]{1,0:T(8,128)(2,1)}, bf16[64,4096]{1,0:T(8,128)(2,1)}, u32[]{:S(2)}, u32[]{:S(2)}) collective-permute-start(bf16[64,4096]{1,0:T(8,128)(2,1)} %get-tuple-element.220), channel_id=1, source_target_pairs={{0,8},{2,10},{4,12},{6,14},{8,0},{10,2},{12,4},{14,6},{16,24},{18,... | collective-permute-start | bytes 1572872 | tf_op jit(solution)/shard_map/ppermute | solution.py:376
  545.8 36.6 %collective-permute-start.34 = (bf16[64,4096]{1,0:T(8,128)(2,1)}, bf16[64,4096]{1,0:T(8,128)(2,1)}, u32[]{:S(2)}, u32[]{:S(2)}) collective-permute-start(bf16[64,4096]{1,0:T(8,128)(2,1)} %get-tuple-element.221), channel_id=1, source_target_pairs={{0,16},{2,18},{4,20},{6,22},{8,24},{10,26},{12,28},{14,30},{16,0},... | collective-permute-start | bytes 1572872 | tf_op jit(solution)/shard_map/ppermute | solution.py:376
  562.8 30.2 %collective-permute-start.35 = (bf16[64,4096]{1,0:T(8,128)(2,1)}, bf16[64,4096]{1,0:T(8,128)(2,1)}, u32[]{:S(2)}, u32[]{:S(2)}) collective-permute-start(bf16[64,4096]{1,0:T(8,128)(2,1)} %get-tuple-element.222), channel_id=1, source_target_pairs={{0,24},{2,26},{4,28},{6,30},{8,16},{10,18},{12,20},{14,22},{16,8},... | collective-permute-start | bytes 1572872 | tf_op jit(solution)/shard_map/ppermute | solution.py:376
  611.9 45.3 %collective-permute-start.41 = (bf16[256,4096]{1,0:T(8,128)(2,1)}, bf16[256,4096]{1,0:T(8,128)(2,1)}, u32[]{:S(2)}, u32[]{:S(2)}) collective-permute-start(bf16[256,4096]{1,0:T(8,128)(2,1)} %pad_maximum_fusion.2), channel_id=1, source_target_pairs={{0,4},{2,6},{4,0},{6,2},{8,12},{10,14},{12,8},{14,10},{16,20},{18,... | collective-permute-start | bytes 6291464 | tf_op jit(solution)/shard_map/ppermute | solution.py:376
  612.4 45.9 %collective-permute-start.42 = (bf16[256,4096]{1,0:T(8,128)(2,1)}, bf16[256,4096]{1,0:T(8,128)(2,1)}, u32[]{:S(2)}, u32[]{:S(2)}) collective-permute-start(bf16[256,4096]{1,0:T(8,128)(2,1)} %pad_maximum_fusion.3), channel_id=1, source_target_pairs={{0,1},{1,0},{2,3},{3,2},{4,5},{5,4},{6,7},{7,6},{8,9},{9,8},{10,11... | collective-permute-start | bytes 6291464 | tf_op jit(solution)/shard_map/ppermute | solution.py:381
  613.8 34.5 %collective-permute-start.38 = (bf16[64,2048]{1,0:T(8,128)(2,1)}, bf16[64,2048]{1,0:T(8,128)(2,1)S(1)}, u32[]{:S(2)}, u32[]{:S(2)}) collective-permute-start(bf16[64,2048]{1,0:T(8,128)(2,1)} %get-tuple-element.236), channel_id=1, source_target_pairs={{0,8},{2,10},{4,12},{6,14},{8,0},{10,2},{12,4},{14,6},{16,24},{18,... | collective-permute-start | bytes 786440 | tf_op jit(solution)/shard_map/ppermute | solution.py:376
  616.4 31.9 %collective-permute-start.39 = (bf16[64,2048]{1,0:T(8,128)(2,1)}, bf16[64,2048]{1,0:T(8,128)(2,1)}, u32[]{:S(2)}, u32[]{:S(2)}) collective-permute-start(bf16[64,2048]{1,0:T(8,128)(2,1)} %get-tuple-element.237), channel_id=1, source_target_pairs={{0,16},{2,18},{4,20},{6,22},{8,24},{10,26},{12,28},{14,30},{16,0},... | collective-permute-start | bytes 786440 | tf_op jit(solution)/shard_map/ppermute | solution.py:376
  617.0 31.3 %collective-permute-start.40 = (bf16[64,2048]{1,0:T(8,128)(2,1)}, bf16[64,2048]{1,0:T(8,128)(2,1)}, u32[]{:S(2)}, u32[]{:S(2)}) collective-permute-start(bf16[64,2048]{1,0:T(8,128)(2,1)} %get-tuple-element.238), channel_id=1, source_target_pairs={{0,24},{2,26},{4,28},{6,30},{8,16},{10,18},{12,20},{14,22},{16,8},... | collective-permute-start | bytes 786440 | tf_op jit(solution)/shard_map/ppermute | solution.py:376
  673.0 48.8 %collective-permute-start.48 = (bf16[64,4096]{1,0:T(8,128)(2,1)}, bf16[64,4096]{1,0:T(8,128)(2,1)}, u32[]{:S(2)}, u32[]{:S(2)}) collective-permute-start(bf16[64,4096]{1,0:T(8,128)(2,1)} %get-tuple-element.274), channel_id=1, source_target_pairs={{0,8},{2,10},{4,12},{6,14},{8,0},{10,2},{12,4},{14,6},{16,24},{18,... | collective-permute-start | bytes 1572872 | tf_op jit(solution)/shard_map/ppermute | solution.py:376
  675.2 46.7 %collective-permute-start.49 = (bf16[64,4096]{1,0:T(8,128)(2,1)}, bf16[64,4096]{1,0:T(8,128)(2,1)}, u32[]{:S(2)}, u32[]{:S(2)}) collective-permute-start(bf16[64,4096]{1,0:T(8,128)(2,1)} %get-tuple-element.275), channel_id=1, source_target_pairs={{0,16},{2,18},{4,20},{6,22},{8,24},{10,26},{12,28},{14,30},{16,0},... | collective-permute-start | bytes 1572872 | tf_op jit(solution)/shard_map/ppermute | solution.py:376
  675.8 47.3 %collective-permute-start.50 = (bf16[64,4096]{1,0:T(8,128)(2,1)}, bf16[64,4096]{1,0:T(8,128)(2,1)}, u32[]{:S(2)}, u32[]{:S(2)}) collective-permute-start(bf16[64,4096]{1,0:T(8,128)(2,1)} %get-tuple-element.276), channel_id=1, source_target_pairs={{0,24},{2,26},{4,28},{6,30},{8,16},{10,18},{12,20},{14,22},{16,8},... | collective-permute-start | bytes 1572872 | tf_op jit(solution)/shard_map/ppermute | solution.py:376
  (116 other events, 1311.5 us)
Sparse Core Ops, SparseCore 0:
  11.6 104.9 all-gather.2
  120.1 160.2 all-gather.4

commit v4 on v3

--- a/solution.py
+++ b/solution.py
@@ -733,8 +733,9 @@
         else:
             attn_send, grad_proj = hold(attn_send, grad_proj)
         attn_came = over_dp(attn_send, 1)
-        back = times_transposed(relative_t, grad_proj, qkv, "grad_stream")
-        back, attn_came = hold(back, attn_came)
+        if l > 0:
+            back = times_transposed(relative_t, grad_proj, qkv, "grad_stream")
+            back, attn_came = hold(back, attn_came)
         attn_line = weight_grads(
             attn_pairs, blocks, 0, 2, add=attn_came, blocks=2, name="attn_keep"
         )
@@ -746,10 +747,15 @@
             wide_grad, gains_grad = reorder(wide_grad, places), reorder(gains_grad, places)
         small_grads[l] = gains_grad, wide_grad, grad_proj, grad_pre
         if l == 0:
-            attn_line, back = hold(attn_line, back)
+            attn_line, grad_proj = hold(attn_line, grad_proj)
             attn_corners = scatter_corners(attn_line)
-            held = after(small_grads, attn_line)
+            back = times_transposed(relative_t, grad_proj, qkv, "grad_stream")
+            held = after(small_grads, back)
             heads_grads = [jnp.stack([over_rows(h[2][0]), over_rows(h[2][2])]) for h in held]
+            ups_grads = jnp.stack([over_rows(h[3]) for h in held])
+            attn_sums = scatter_sum(*after((attn_line, attn_corners), back))
+            attn_sums, heads_grads, ups_grads = hold(attn_sums, heads_grads, ups_grads)
+            attn_sides = scatter_sides(attn_sums)
             smalls = (
                 jnp.stack([h[0] for h in held]),
                 jnp.concatenate(
@@ -759,23 +765,21 @@
                     ],
                     axis=1,
                 ),
-                reorder(jnp.stack([over_rows(h[3]) for h in held]), relative_t),
+                reorder(ups_grads, relative_t),
             )
             small_sums = relative_small(
                 jnp.concatenate([fold(whole) for whole in smalls], axis=1)
             )
-            attn_sums = scatter_sum(*after((attn_line, attn_corners), small_sums))
-            attn_sides = scatter_sides(attn_sums)
-            mlp_addends, small_sums = after((mlp_addends, small_sums), attn_sums)
+            mlp_addends, small_sums = hold(mlp_addends, small_sums)
             mlp_done[l] = scatter_end(mlp_addends)
-            small_sums = scatter_small(after(small_sums, mlp_done[l]), 4 * blocks)
+            small_sums = scatter_small(small_sums, 4 * blocks)
             attn_sides, small_sums = hold(attn_sides, small_sums)
             attn_pieces = scatter_pieces(attn_line, attn_sides)
             attn_pieces, small_sums = hold(attn_pieces, small_sums)
             attn_addends = scatter_far(attn_pieces)
             summed = scatter_small(small_sums, 1)[0]
             attn_done[l] = scatter_end(after(attn_addends, summed))
-            input_grad = select_wide(after(grad_first, attn_line), unpick) + back
+            input_grad = select_wide(after(grad_first, attn_sums), unpick) + back
         else:
             attn_line, back = hold(attn_line, back)
             flying = attn_line, scatter_corners(attn_line), mlp_line, mlp_sides

time: 796 us -> 789 us (level)
  transfers between devices with their start and end apart: 61 -> 61, of which waited for: 31 -> 32; matrix products, arithmetic and copies ran while one was open for 16% -> 16% of each run, Pallas kernels for 23% -> 23%
where the time goes in v4:
time: 789 us; the launch traced here: 781 us
  Pallas kernels  306 us (39%)
  waiting for transfers between devices  218 us (28%)
  other arithmetic  94.1 us (12%)
  local copies, waits for them, and re-layouts  60.7 us (8%)
  starting transfers between devices  55.9 us (7%)
  matrix products  30.6 us (4%)
  between operations  16.1 us (2%)
    ppermute x42, waiting for transfers between devices, over_dp(): return lax.ppermute(value, 'dp', [(i, i ^ mask) for i in range(count)])  135 us
    pallas_call x8, Pallas kernels, times_transposed(): pl.pallas_call(kernel, grid_spec=pltpu.PrefetchScalarGridSpec(num_scalar_...  80 us
    pallas_call x8, Pallas kernels, weight_grads(): pl.pallas_call(kernel, grid=(sum(counts),), in_specs=in_specs, out_specs=...  77.6 us
    pallas_call x8, Pallas kernels, times_weight(): pl.pallas_call(kernel, grid_spec=pltpu.PrefetchScalarGridSpec(num_scalar_...  75.4 us
    ppermute x12, waiting for transfers between devices, over_tensor(): lax.ppermute(value, ('thi', 'tlo'), [(i, i ^ mask) for i in range(count)])  51.4 us
    pallas_call x2, Pallas kernels, attend_back(): pl.pallas_call(attend_back_kernel, grid=(sets, parts * pairs), in_specs=s...  45.9 us
    ppermute x42, starting transfers between devices, over_dp(): return lax.ppermute(value, 'dp', [(i, i ^ mask) for i in range(count)])  39.5 us
    dot_general x14, matrix products, dot(): return jnp.dot(a, b, preferred_element_type=F32)  30.6 us
  transfers between devices with their start and end apart: 61, of which 32 were waited for; matrix products, arithmetic and copies ran while one was open for 16% of the time, Pallas kernels for 23%

profile of v4, /device:TPU:8, one launch (start us, length us, event | category | flops | bytes accessed | tf_op | source)
XLA Modules:
  0.0 781.3 jit_solution(11076836507730227160)
XLA Ops:
  18.8 24.4 %collective-permute-done.2 = bf16[64,2560]{1,0:T(8,128)(2,1)S(1)} collective-permute-done((bf16[64,2560]{1,0:T(8,128)(2,1)S(1)}, bf16[64,2560]{1,0:T(8,128)(2,1)S(1)}, u32[]{:S(2)}, u32[]{:S(2)}) %collective-permute-start.2) | collective-permute-done | bytes 327712 | tf_op jit(solution)/shard_map/ppermute | solution.py:376
  58.3 31.7 %collective-permute-done.6.refs_6_.refs_4_ = bf16[256,2560]{1,0:T(8,128)(2,1)S(1)} collective-permute-done((bf16[256,2560]{1,0:T(8,128)(2,1)S(1)}, bf16[256,2560]{1,0:T(8,128)(2,1)S(1)}, u32[]{:S(2)}, u32[]{:S(2)}) %collective-permute-start.6) | collective-permute-done | bytes 1310752 | tf_op jit(solution)/shard_map/ppermute | solution.py:381
  103.4 14.8 %collective-permute-done.5 = bf16[64,2048]{1,0:T(8,128)(2,1)} collective-permute-done((bf16[64,2048]{1,0:T(8,128)(2,1)S(1)}, bf16[64,2048]{1,0:T(8,128)(2,1)}, u32[]{:S(2)}, u32[]{:S(2)}) %collective-permute-start.5) | collective-permute-done | bytes 262176 | tf_op jit(solution)/shard_map/ppermute | solution.py:376
  139.3 8.7 %project.2.q_ref.k_ref.v_ref = bf16[512,3072]{1,0:T(8,128)(2,1)} custom-call(s32[2]{0:T(128)} %iota_xor_fusion.which_ref, bf16[512,1024]{1,0:T(8,128)(2,1)} %x_ref.1, bf16[2048,1664]{1,0:T(8,128)(2,1)} %all-gather.3.cloned.1.call-done.refs_0_.refs_1_.refs_2_.refs_3_, bf16[2048,1664]{1,0:T(8,128)(2,1)} %all-gather.3.cloned.1.call-done.refs_0_.refs_1_.refs_2_.refs_3_, ...), custom_call_target="tpu_custom_call" | custom-call | flops 3221225472 | bytes 2097152 | tf_op jit(solution)/shard_map/project/pallas_call | solution.py:192
  148.0 9.2 %collective-permute-done.10.refs_3_.refs_1_ = bf16[256,2048]{1,0:T(8,128)(2,1)} collective-permute-done((bf16[256,2048]{1,0:T(8,128)(2,1)}, bf16[256,2048]{1,0:T(8,128)(2,1)}, u32[]{:S(2)}, u32[]{:S(2)}) %collective-permute-start.10) | collective-permute-done | bytes 1048608 | tf_op jit(solution)/shard_map/ppermute | solution.py:376
  170.8 13.6 %collective-permute-done.13 = bf16[128,2048]{1,0:T(8,128)(2,1)} collective-permute-done((bf16[128,2048]{1,0:T(8,128)(2,1)}, bf16[128,2048]{1,0:T(8,128)(2,1)}, u32[]{:S(2)}, u32[]{:S(2)}) %collective-permute-start.13) | collective-permute-done | bytes 524320 | tf_op jit(solution)/shard_map/ppermute | solution.py:381
  187.4 13.3 %attend.2 = bf16[512,1024]{1,0:T(8,128)(2,1)} custom-call(bf16[512,3072]{1,0:T(8,128)(2,1)} %project.2.q_ref.k_ref.v_ref, bf16[512,3072]{1,0:T(8,128)(2,1)} %project.2.q_ref.k_ref.v_ref, bf16[512,3072]{1,0:T(8,128)(2,1)} %project.2.q_ref.k_ref.v_ref, s32[1,1,512]{2,1,0:T(1,128)} %get-tuple-element.435.segq_ref, s32[1,512,1]{2,1,0:T(8,128)} %copy.49.segk_ref), custom_call_target="tpu_custom_call" | custom-call | flops 4294967296 | bytes 6291456 | tf_op jit(solution)/shard_map/attend/pallas_call | solution.py:106
  214.6 13.0 %enter.2 = (bf16[512,4096]{1,0:T(8,128)(2,1)}, bf16[512,4096]{1,0:T(8,128)(2,1)}) custom-call(s32[2]{0:T(128)} %iota_xor_fusion.which_ref, bf16[512,1024]{1,0:T(8,128)(2,1)} %fusion.31.x_ref.refs_0_, bf16[256,2560]{1,0:T(8,128)(2,1)} %copy-done.7, bf16[256,2560]{1,0:T(8,128)(2,1)} %collective-permute-done.7.refs_3_.refs_1_, ...), custom_call_target="tpu_custom_call" | custom-call | flops 4294967296 | bytes 2097152 | tf_op jit(solution)/shard_map/enter/pallas_call | solution.py:192
  228.6 15.8 %branch.2 = f32[512,1024]{1,0:T(8,128)} custom-call(s32[2]{0:T(128)} %iota_xor_fusion.which_ref, bf16[1,512,4096]{2,1,0:T(8,128)(2,1)} %bitcast.201, bf16[1,512,4096]{2,1,0:T(8,128)(2,1)} %bitcast.202, bf16[256,2048]{1,0:T(8,128)(2,1)} %pad_maximum_fusion.5.refs_2_.refs_0_, bf16[256,2048]{1,0:T(8,128)(2,1)} %collective-permute-done.10.refs_3_.refs_1_, ...), custom_call_target="tpu_custom_call" | custom-call | flops 4294967296 | bytes 4194304 | tf_op jit(solution)/shard_map/branch/pallas_call | solution.py:246
  254.1 26.2 %all-gather.5.cloned.1.call-done.refs_0_.refs_1_.refs_2_.refs_3_ = bf16[2048,6144]{1,0:T(8,128)(2,1)} async-done(((bf16[64,6144]{1,0:T(8,128)(2,1)}), bf16[2048,6144]{1,0:T(8,128)(2,1)}) %all-gather.5.cloned.1.call-update) | async-done | bytes 25165840 | tf_op jit(solution)/shard_map/all_gather | solution.py:536
  280.3 8.6 %project.3.q_ref.k_ref.v_ref = bf16[512,3072]{1,0:T(8,128)(2,1)} custom-call(s32[2]{0:T(128)} %iota_xor_fusion.which_ref, bf16[512,1024]{1,0:T(8,128)(2,1)} %get-tuple-element.445.x_ref, bf16[2048,6144]{1,0:T(8,128)(2,1)} %all-gather.5.cloned.1.call-done.refs_0_.refs_1_.refs_2_.refs_3_, ...), custom_call_target="tpu_custom_call" | custom-call | flops 3221225472 | bytes 2097152 | tf_op jit(solution)/shard_map/project/pallas_call | solution.py:192
  288.9 13.4 %attend.3 = bf16[512,1024]{1,0:T(8,128)(2,1)} custom-call(bf16[512,3072]{1,0:T(8,128)(2,1)} %project.3.q_ref.k_ref.v_ref, bf16[512,3072]{1,0:T(8,128)(2,1)} %project.3.q_ref.k_ref.v_ref, bf16[512,3072]{1,0:T(8,128)(2,1)} %project.3.q_ref.k_ref.v_ref, s32[1,1,512]{2,1,0:T(1,128)} %get-tuple-element.435.segq_ref, s32[1,512,1]{2,1,0:T(8,128)} %copy.49.segk_ref), custom_call_target="tpu_custom_call" | custom-call | flops 4294967296 | bytes 6291456 | tf_op jit(solution)/shard_map/attend/pallas_call | solution.py:106
  313.3 13.3 %enter.3 = (bf16[512,4096]{1,0:T(8,128)(2,1)}, bf16[512,4096]{1,0:T(8,128)(2,1)}) custom-call(s32[2]{0:T(128)} %iota_xor_fusion.which_ref, bf16[512,1024]{1,0:T(8,128)(2,1)} %copy-done.21, bf16[2048,6144]{1,0:T(8,128)(2,1)} %all-gather.5.cloned.1.call-done.refs_0_.refs_1_.refs_2_.refs_3_, ...), custom_call_target="tpu_custom_call" | custom-call | flops 4294967296 | bytes 2097152 | tf_op jit(solution)/shard_map/enter/pallas_call | solution.py:192
  326.5 10.0 %branch.3 = f32[512,1024]{1,0:T(8,128)} custom-call(s32[2]{0:T(128)} %iota_xor_fusion.which_ref, bf16[1,512,4096]{2,1,0:T(8,128)(2,1)} %bitcast.195, bf16[1,512,4096]{2,1,0:T(8,128)(2,1)} %bitcast.196, bf16[2048,6144]{1,0:T(8,128)(2,1)} %all-gather.5.cloned.1.call-done.refs_0_.refs_1_.refs_2_.refs_3_, ...), custom_call_target="tpu_custom_call" | custom-call | flops 4294967296 | bytes 4194304 | tf_op jit(solution)/shard_map/branch/pallas_call | solution.py:246
  346.8 10.7 %leave.2 = bf16[512,4096]{1,0:T(8,128)(2,1)} custom-call(s32[2]{0:T(128)} %iota_xor_fusion.which_ref, bf16[512,1024]{1,0:T(8,128)(2,1)} %copy-done.18, bf16[2048,6144]{1,0:T(8,128)(2,1)} %all-gather.5.cloned.1.call-done.refs_0_.refs_1_.refs_2_.refs_3_, bf16[2048,6144]{1,0:T(8,128)(2,1)} %all-gather.5.cloned.1.call-done.refs_0_.refs_1_.refs_2_.refs_3_, ...), custom_call_target="tpu_custom_call" | custom-call | flops 536870912 | bytes 262144 | tf_op jit(solution)/shard_map/leave/pallas_call | solution.py:192
  357.5 10.9 %mlp_send.2 = bf16[2,512,4096]{2,1,0:T(8,128)(2,1)} custom-call(bf16[512,1024]{1,0:T(8,128)(2,1)} %fusion.33.refs_0_, bf16[1,512,4096]{2,1,0:T(8,128)(2,1)} %bitcast.183, bf16[1,512,4096]{2,1,0:T(8,128)(2,1)} %bitcast.184, bf16[512,1024]{1,0:T(8,128)(2,1)} %fusion.34.refs_3_, bf16[1,512,4096]{2,1,0:T(8,128)(2,1)} %bitcast.197, bf16[1,512,4096]{2,1,0:T(8,128)(2,1)} %bitcast.198), custom_call_target="tpu_custom_call" | custom-call | flops 536870912 | bytes 1048576 | tf_op jit(solution)/shard_map/mlp_send/pallas_call | solution.py:323
  371.0 10.0 %grad_mid.2 = f32[512,1024]{1,0:T(8,128)} custom-call(s32[2]{0:T(128)} %iota_xor_fusion.which_ref, bf16[1,512,4096]{2,1,0:T(8,128)(2,1)} %bitcast.185, bf16[1,512,4096]{2,1,0:T(8,128)(2,1)} %bitcast.186, bf16[2048,6144]{1,0:T(8,128)(2,1)} %all-gather.5.cloned.1.call-done.refs_0_.refs_1_.refs_2_.refs_3_, ...), custom_call_target="tpu_custom_call" | custom-call | flops 536870912 | bytes 524288 | tf_op jit(solution)/shard_map/grad_mid/pallas_call | solution.py:246
  381.9 12.1 %mlp_keep.2 = (bf16[256,4096]{1,0:T(8,128)(2,1)}, bf16[256,4096]{1,0:T(8,128)(2,1)}, bf16[256,4096]{1,0:T(8,128)(2,1)}, bf16[256,4096]{1,0:T(8,128)(2,1)}) custom-call(bf16[512,1024]{1,0:T(8,128)(2,1)} %fusion.33.refs_0_, bf16[1,512,4096]{2,1,0:T(8,128)(2,1)} %bitcast.187, bf16[1,512,4096]{2,1,0:T(8,128)(2,1)} %bitcast.188, ...), custom_call_target="tpu_custom_call" | custom-call | flops 536870912 | bytes 1048576 | tf_op jit(solution)/shard_map/mlp_keep/pallas_call | solution.py:323
  412.6 11.9 %collective-permute-done.23 = bf16[128,4096]{1,0:T(8,128)(2,1)} collective-permute-done((bf16[128,4096]{1,0:T(8,128)(2,1)}, bf16[128,4096]{1,0:T(8,128)(2,1)}, u32[]{:S(2)}, u32[]{:S(2)}) %collective-permute-start.23) | collective-permute-done | bytes 1048608 | tf_op jit(solution)/shard_map/ppermute | solution.py:376
  431.6 22.8 %attend_back.2.refs_1_.refs_2_.refs_0_ = bf16[3,512,1024]{2,1,0:T(8,128)(2,1)} custom-call(bf16[512,3072]{1,0:T(8,128)(2,1)} %project.3.q_ref.k_ref.v_ref, bf16[512,3072]{1,0:T(8,128)(2,1)} %project.3.q_ref.k_ref.v_ref, bf16[512,3072]{1,0:T(8,128)(2,1)} %project.3.q_ref.k_ref.v_ref, bf16[512,1024]{1,0:T(8,128)(2,1)} %grad_mix.2.grad_ref, ...), custom_call_target="tpu_custom_call" | custom-call | flops 1342177280 | bytes 1572864 | tf_op jit(solution)/shard_map/attend_back/pallas_call | solution.py:134
  463.9 8.6 %grad_stream.2 = f32[512,1024]{1,0:T(8,128)} custom-call(s32[2]{0:T(128)} %iota_xor_fusion.which_ref, bf16[3,512,1024]{2,1,0:T(8,128)(2,1)} %attend_back.2.refs_1_.refs_2_.refs_0_, bf16[3,512,1024]{2,1,0:T(8,128)(2,1)} %attend_back.2.refs_1_.refs_2_.refs_0_, bf16[2048,6144]{1,0:T(8,128)(2,1)} %all-gather.5.cloned.1.call-done.refs_0_.refs_1_.refs_2_.refs_3_, ...), custom_call_target="tpu_custom_call" | custom-call | flops 402653184 | bytes 393216 | tf_op jit(solution)/shard_map/grad_stream/pallas_call | solution.py:246
  472.5 9.0 %attn_keep.2 = (bf16[256,2048]{1,0:T(8,128)(2,1)}, bf16[256,2048]{1,0:T(8,128)(2,1)}, bf16[256,2048]{1,0:T(8,128)(2,1)}, bf16[256,2048]{1,0:T(8,128)(2,1)}) custom-call(bf16[512,1024]{1,0:T(8,128)(2,1)} %fusion.35.refs_0_, bf16[3,512,1024]{2,1,0:T(8,128)(2,1)} %attend_back.2.refs_1_.refs_2_.refs_0_, ...), custom_call_target="tpu_custom_call" | custom-call | flops 268435456 | bytes 524288 | tf_op jit(solution)/shard_map/attn_keep/pallas_call | solution.py:323
  493.7 11.2 %leave.3 = bf16[512,4096]{1,0:T(8,128)(2,1)} custom-call(s32[2]{0:T(128)} %iota_xor_fusion.which_ref, bf16[512,1024]{1,0:T(8,128)(2,1)} %convert_element_type.434.x_ref.refs_3_, bf16[256,2048]{1,0:T(8,128)(2,1)} %pad_maximum_fusion.5.refs_2_.refs_0_, bf16[256,2048]{1,0:T(8,128)(2,1)} %collective-permute-done.10.refs_3_.refs_1_, ...), custom_call_target="tpu_custom_call" | custom-call | flops 536870912 | bytes 262144 | tf_op jit(solution)/shard_map/leave/pallas_call | solution.py:192
  511.2 10.1 %collective-permute-done.26 = bf16[128,2048]{1,0:T(8,128)(2,1)} collective-permute-done((bf16[128,2048]{1,0:T(8,128)(2,1)}, bf16[128,2048]{1,0:T(8,128)(2,1)}, u32[]{:S(2)}, u32[]{:S(2)}) %collective-permute-start.26) | collective-permute-done | bytes 524320 | tf_op jit(solution)/shard_map/ppermute | solution.py:376
  530.6 10.6 %mlp_send.3 = bf16[2,512,4096]{2,1,0:T(8,128)(2,1)} custom-call(bf16[512,1024]{1,0:T(8,128)(2,1)} %fusion.31.x_ref.refs_0_, bf16[1,512,4096]{2,1,0:T(8,128)(2,1)} %bitcast.189, bf16[1,512,4096]{2,1,0:T(8,128)(2,1)} %bitcast.190, bf16[512,1024]{1,0:T(8,128)(2,1)} %convert_element_type.434.x_ref.refs_3_, bf16[1,512,4096]{2,1,0:T(8,128)(2,1)} %bitcast.203, ...), custom_call_target="tpu_custom_call" | custom-call | flops 536870912 | bytes 1048576 | tf_op jit(solution)/shard_map/mlp_send/pallas_call | solution.py:323
  547.2 15.5 %grad_mid.3 = f32[512,1024]{1,0:T(8,128)} custom-call(s32[2]{0:T(128)} %iota_xor_fusion.which_ref, bf16[1,512,4096]{2,1,0:T(8,128)(2,1)} %bitcast.191, bf16[1,512,4096]{2,1,0:T(8,128)(2,1)} %bitcast.192, bf16[256,2560]{1,0:T(8,128)(2,1)} %copy-done.7, bf16[256,2560]{1,0:T(8,128)(2,1)} %collective-permute-done.7.refs_3_.refs_1_, ...), custom_call_target="tpu_custom_call" | custom-call | flops 536870912 | bytes 524288 | tf_op jit(solution)/shard_map/grad_mid/pallas_call | solution.py:246
  562.8 12.1 %mlp_keep.3 = (bf16[256,4096]{1,0:T(8,128)(2,1)}, bf16[256,4096]{1,0:T(8,128)(2,1)}, bf16[256,4096]{1,0:T(8,128)(2,1)}, bf16[256,4096]{1,0:T(8,128)(2,1)}) custom-call(bf16[512,1024]{1,0:T(8,128)(2,1)} %fusion.31.x_ref.refs_0_, bf16[1,512,4096]{2,1,0:T(8,128)(2,1)} %bitcast.193, bf16[1,512,4096]{2,1,0:T(8,128)(2,1)} %bitcast.194, ...), custom_call_target="tpu_custom_call" | custom-call | flops 536870912 | bytes 1048576 | tf_op jit(solution)/shard_map/mlp_keep/pallas_call | solution.py:323
  617.6 23.0 %attend_back.3.refs_1_.refs_2_.refs_0_ = bf16[3,512,1024]{2,1,0:T(8,128)(2,1)} custom-call(bf16[512,3072]{1,0:T(8,128)(2,1)} %project.2.q_ref.k_ref.v_ref, bf16[512,3072]{1,0:T(8,128)(2,1)} %project.2.q_ref.k_ref.v_ref, bf16[512,3072]{1,0:T(8,128)(2,1)} %project.2.q_ref.k_ref.v_ref, bf16[512,1024]{1,0:T(8,128)(2,1)} %grad_mix.3.grad_ref, ...), custom_call_target="tpu_custom_call" | custom-call | flops 1342177280 | bytes 1572864 | tf_op jit(solution)/shard_map/attend_back/pallas_call | solution.py:134
  648.0 8.9 %collective-permute-done.41 = bf16[256,4096]{1,0:T(8,128)(2,1)} collective-permute-done((bf16[256,4096]{1,0:T(8,128)(2,1)}, bf16[256,4096]{1,0:T(8,128)(2,1)}, u32[]{:S(2)}, u32[]{:S(2)}) %collective-permute-start.41) | collective-permute-done | bytes 2097184 | tf_op jit(solution)/shard_map/ppermute | solution.py:376
  676.5 8.4 %attn_keep.3 = (bf16[256,2048]{1,0:T(8,128)(2,1)}, bf16[256,2048]{1,0:T(8,128)(2,1)}, bf16[256,2048]{1,0:T(8,128)(2,1)}, bf16[256,2048]{1,0:T(8,128)(2,1)}) custom-call(bf16[512,1024]{1,0:T(8,128)(2,1)} %get-tuple-element.448.refs_0_, bf16[3,512,1024]{2,1,0:T(8,128)(2,1)} %attend_back.3.refs_1_.refs_2_.refs_0_, ...), custom_call_target="tpu_custom_call" | custom-call | flops 268435456 | bytes 524288 | tf_op jit(solution)/shard_map/attn_keep/pallas_call | solution.py:323
  689.2 9.1 %grad_stream.3 = f32[512,1024]{1,0:T(8,128)} custom-call(s32[2]{0:T(128)} %iota_xor_fusion.which_ref, bf16[3,512,1024]{2,1,0:T(8,128)(2,1)} %attend_back.3.refs_1_.refs_2_.refs_0_, bf16[3,512,1024]{2,1,0:T(8,128)(2,1)} %attend_back.3.refs_1_.refs_2_.refs_0_, bf16[2048,1664]{1,0:T(8,128)(2,1)} %all-gather.3.cloned.1.call-done.refs_0_.refs_1_.refs_2_.refs_3_, ...), custom_call_target="tpu_custom_call" | custom-call | flops 402653184 | bytes 393216 | tf_op jit(solution)/shard_map/grad_stream/pallas_call | solution.py:246
  758.2 7.6 collective-permute-done.54
  (574 shorter events, 337.0 us)
Async XLA Ops:
  7.2 121.5 %all-gather.3.cloned.1.call-start = ((), (), s32[]{:S(2)}) async-start(), calls=%async_computation | async-start | bytes 7028736 | tf_op jit(solution)/shard_map/all_gather | solution.py:536
  11.5 268.8 %all-gather.5.cloned.1.call-start = ((), (), s32[]{:S(2)}) async-start(), calls=%async_computation.1 | async-start | bytes 25952256 | tf_op jit(solution)/shard_map/all_gather | solution.py:536
  14.1 29.1 %collective-permute-start.2 = (bf16[64,2560]{1,0:T(8,128)(2,1)S(1)}, bf16[64,2560]{1,0:T(8,128)(2,1)S(1)}, u32[]{:S(2)}, u32[]{:S(2)}) collective-permute-start(bf16[64,2560]{1,0:T(8,128)(2,1)S(1)} %pad_maximum_fusion.14), channel_id=1, source_target_pairs={{0,24},{2,26},{4,28},{6,30},{8,16},{10,18},{12,20},{14,22},{16,8},... | collective-permute-start | bytes 983048 | tf_op jit(solution)/shard_map/ppermute | solution.py:376
  15.7 32.6 %collective-permute-start.1 = (bf16[64,2560]{1,0:T(8,128)(2,1)S(1)}, bf16[64,2560]{1,0:T(8,128)(2,1)S(1)}, u32[]{:S(2)}, u32[]{:S(2)}) collective-permute-start(bf16[64,2560]{1,0:T(8,128)(2,1)S(1)} %pad_maximum_fusion.14), channel_id=1, source_target_pairs={{0,16},{2,18},{4,20},{6,22},{8,24},{10,26},{12,28},{14,30},{16,0},... | collective-permute-start | bytes 983048 | tf_op jit(solution)/shard_map/ppermute | solution.py:376
  16.8 31.5 %collective-permute-start = (bf16[64,2560]{1,0:T(8,128)(2,1)S(1)}, bf16[64,2560]{1,0:T(8,128)(2,1)}, u32[]{:S(2)}, u32[]{:S(2)}) collective-permute-start(bf16[64,2560]{1,0:T(8,128)(2,1)S(1)} %pad_maximum_fusion.14), channel_id=1, source_target_pairs={{0,8},{2,10},{4,12},{6,14},{8,0},{10,2},{12,4},{14,6},{16,24},{18,... | collective-permute-start | bytes 983048 | tf_op jit(solution)/shard_map/ppermute | solution.py:376
  49.5 40.5 %collective-permute-start.6 = (bf16[256,2560]{1,0:T(8,128)(2,1)S(1)}, bf16[256,2560]{1,0:T(8,128)(2,1)S(1)}, u32[]{:S(2)}, u32[]{:S(2)}) collective-permute-start(bf16[256,2560]{1,0:T(8,128)(2,1)S(1)} %pad_maximum_fusion.4.refs_2_.refs_0_), channel_id=1, source_target_pairs={{0,1},{1,0},{2,3},{3,2},{4,5},{5,4},{6,7},{7,6},{8,9},{9,8},{10,11... | collective-permute-start | bytes 3932168 | tf_op jit(solution)/shard_map/ppermute | solution.py:381
  51.2 46.9 %collective-permute-start.7 = (bf16[256,2560]{1,0:T(8,128)(2,1)S(1)}, bf16[256,2560]{1,0:T(8,128)(2,1)}, u32[]{:S(2)}, u32[]{:S(2)}) collective-permute-start(bf16[256,2560]{1,0:T(8,128)(2,1)S(1)} %pad_maximum_fusion.4.refs_2_.refs_0_), channel_id=1, source_target_pairs={{0,4},{2,6},{4,0},{6,2},{8,12},{10,14},{12,8},{14,10},{16,20},{18,... | collective-permute-start | bytes 3932168 | tf_op jit(solution)/shard_map/ppermute | solution.py:376
  90.9 32.4 %collective-permute-start.8 = (bf16[128,2560]{1,0:T(8,128)(2,1)}, bf16[128,2560]{1,0:T(8,128)(2,1)S(1)}, u32[]{:S(2)}, u32[]{:S(2)}) collective-permute-start(bf16[128,2560]{1,0:T(8,128)(2,1)} %slice.665), channel_id=1, source_target_pairs={{0,4},{2,6},{4,0},{6,2},{8,12},{10,14},{12,8},{14,10},{16,20},{18,... | collective-permute-start | bytes 1966088 | tf_op jit(solution)/shard_map/ppermute | solution.py:376
  92.9 27.7 %collective-permute-start.4 = (bf16[64,2048]{1,0:T(8,128)(2,1)S(1)}, bf16[64,2048]{1,0:T(8,128)(2,1)}, u32[]{:S(2)}, u32[]{:S(2)}) collective-permute-start(bf16[64,2048]{1,0:T(8,128)(2,1)S(1)} %slice_bitcast_fusion.6), channel_id=1, source_target_pairs={{0,16},{2,18},{4,20},{6,22},{8,24},{10,26},{12,28},{14,30},{16,0},... | collective-permute-start | bytes 786440 | tf_op jit(solution)/shard_map/ppermute | solution.py:376
  118.2 84.8 %collective-permute-start.14 = (bf16[256,2560]{1,0:T(8,128)(2,1)S(1)}, bf16[256,2560]{1,0:T(8,128)(2,1)}, u32[]{:S(2)}, u32[]{:S(2)}) collective-permute-start(bf16[256,2560]{1,0:T(8,128)(2,1)S(1)} %pad_maximum_fusion.4.refs_2_.refs_0_), channel_id=1, source_target_pairs={{0,2},{2,0},{4,6},{6,4},{8,10},{10,8},{12,14},{14,12},{16,18},{18,... | collective-permute-start | bytes 3932168 | tf_op jit(solution)/shard_map/ppermute | solution.py:376
  122.8 80.7 %collective-permute-start.15 = (bf16[256,2560]{1,0:T(8,128)(2,1)}, bf16[256,2560]{1,0:T(8,128)(2,1)}, u32[]{:S(2)}, u32[]{:S(2)}) collective-permute-start(bf16[256,2560]{1,0:T(8,128)(2,1)} %collective-permute-done.7.refs_3_.refs_1_), channel_id=1, source_target_pairs={{0,2},{2,0},{4,6},{6,4},{8,10},{10,8},{12,14},{14,12},{16,18},{18,... | collective-permute-start | bytes 3932168 | tf_op jit(solution)/shard_map/ppermute | solution.py:376
  122.8 80.7 %collective-permute-start.16 = (bf16[256,2560]{1,0:T(8,128)(2,1)S(1)}, bf16[256,2560]{1,0:T(8,128)(2,1)}, u32[]{:S(2)}, u32[]{:S(2)}) collective-permute-start(bf16[256,2560]{1,0:T(8,128)(2,1)S(1)} %collective-permute-done.6.refs_6_.refs_4_), channel_id=1, source_target_pairs={{0,2},{2,0},{4,6},{6,4},{8,10},{10,8},{12,14},{14,12},{16,18},{18,... | collective-permute-start | bytes 3932168 | tf_op jit(solution)/shard_map/ppermute | solution.py:376
  126.2 31.0 %collective-permute-start.10 = (bf16[256,2048]{1,0:T(8,128)(2,1)}, bf16[256,2048]{1,0:T(8,128)(2,1)}, u32[]{:S(2)}, u32[]{:S(2)}) collective-permute-start(bf16[256,2048]{1,0:T(8,128)(2,1)} %pad_maximum_fusion.5.refs_2_.refs_0_), channel_id=1, source_target_pairs={{0,4},{2,6},{4,0},{6,2},{8,12},{10,14},{12,8},{14,10},{16,20},{18,... | collective-permute-start | bytes 3145736 | tf_op jit(solution)/shard_map/ppermute | solution.py:376
  126.8 30.9 %collective-permute-start.11 = (bf16[256,2048]{1,0:T(8,128)(2,1)}, bf16[256,2048]{1,0:T(8,128)(2,1)}, u32[]{:S(2)}, u32[]{:S(2)}) collective-permute-start(bf16[256,2048]{1,0:T(8,128)(2,1)} %pad_maximum_fusion.5.refs_2_.refs_0_), channel_id=1, source_target_pairs={{0,1},{1,0},{2,3},{3,2},{4,5},{5,4},{6,7},{7,6},{8,9},{9,8},{10,11... | collective-permute-start | bytes 3145736 | tf_op jit(solution)/shard_map/ppermute | solution.py:381
  157.2 46.8 %collective-permute-start.17 = (bf16[256,2560]{1,0:T(8,128)(2,1)}, bf16[256,2560]{1,0:T(8,128)(2,1)}, u32[]{:S(2)}, u32[]{:S(2)}) collective-permute-start(bf16[256,2560]{1,0:T(8,128)(2,1)} %constant_dynamic-update-slice_fusion.refs_7_.refs_5_), channel_id=1, source_target_pairs={{0,2},{2,0},{4,6},{6,4},{8,10},{10,8},{12,14},{14,12},{16,18},{18,... | collective-permute-start | bytes 3932168 | tf_op jit(solution)/shard_map/ppermute | solution.py:376
  461.8 48.8 %collective-permute-start.28 = (bf16[256,4096]{1,0:T(8,128)(2,1)}, bf16[256,4096]{1,0:T(8,128)(2,1)}, u32[]{:S(2)}, u32[]{:S(2)}) collective-permute-start(bf16[256,4096]{1,0:T(8,128)(2,1)} %pad_maximum_fusion), channel_id=1, source_target_pairs={{0,4},{2,6},{4,0},{6,2},{8,12},{10,14},{12,8},{14,10},{16,20},{18,... | collective-permute-start | bytes 6291464 | tf_op jit(solution)/shard_map/ppermute | solution.py:376
  462.4 48.8 %collective-permute-start.29 = (bf16[256,4096]{1,0:T(8,128)(2,1)}, bf16[256,4096]{1,0:T(8,128)(2,1)}, u32[]{:S(2)}, u32[]{:S(2)}) collective-permute-start(bf16[256,4096]{1,0:T(8,128)(2,1)} %pad_maximum_fusion.1), channel_id=1, source_target_pairs={{0,1},{1,0},{2,3},{3,2},{4,5},{5,4},{6,7},{7,6},{8,9},{9,8},{10,11... | collective-permute-start | bytes 6291464 | tf_op jit(solution)/shard_map/ppermute | solution.py:381
  485.3 36.0 %collective-permute-start.26 = (bf16[128,2048]{1,0:T(8,128)(2,1)}, bf16[128,2048]{1,0:T(8,128)(2,1)}, u32[]{:S(2)}, u32[]{:S(2)}) collective-permute-start(bf16[128,2048]{1,0:T(8,128)(2,1)} %get-tuple-element.414), channel_id=1, source_target_pairs={{0,4},{2,6},{4,0},{6,2},{8,12},{10,14},{12,8},{14,10},{16,20},{18,... | collective-permute-start | bytes 1572872 | tf_op jit(solution)/shard_map/ppermute | solution.py:376
  486.0 35.7 %collective-permute-start.27 = (bf16[128,2048]{1,0:T(8,128)(2,1)}, bf16[128,2048]{1,0:T(8,128)(2,1)}, u32[]{:S(2)}, u32[]{:S(2)}) collective-permute-start(bf16[128,2048]{1,0:T(8,128)(2,1)} %get-tuple-element.413), channel_id=1, source_target_pairs={{0,1},{1,0},{2,3},{3,2},{4,5},{5,4},{6,7},{7,6},{8,9},{9,8},{10,11... | collective-permute-start | bytes 1572872 | tf_op jit(solution)/shard_map/ppermute | solution.py:381
  541.2 51.7 %collective-permute-start.31 = (bf16[256,2048]{1,0:T(8,128)(2,1)}, bf16[256,2048]{1,0:T(8,128)(2,1)}, u32[]{:S(2)}, u32[]{:S(2)}) collective-permute-start(bf16[256,2048]{1,0:T(8,128)(2,1)} %pad_maximum_fusion.7), channel_id=1, source_target_pairs={{0,4},{2,6},{4,0},{6,2},{8,12},{10,14},{12,8},{14,10},{16,20},{18,... | collective-permute-start | bytes 3145736 | tf_op jit(solution)/shard_map/ppermute | solution.py:376
  542.6 50.2 %collective-permute-start.32 = (bf16[256,2048]{1,0:T(8,128)(2,1)}, bf16[256,2048]{1,0:T(8,128)(2,1)}, u32[]{:S(2)}, u32[]{:S(2)}) collective-permute-start(bf16[256,2048]{1,0:T(8,128)(2,1)} %pad_maximum_fusion.8), channel_id=1, source_target_pairs={{0,1},{1,0},{2,3},{3,2},{4,5},{5,4},{6,7},{7,6},{8,9},{9,8},{10,11... | collective-permute-start | bytes 3145736 | tf_op jit(solution)/shard_map/ppermute | solution.py:381
  543.3 36.1 %collective-permute-start.33 = (bf16[64,4096]{1,0:T(8,128)(2,1)}, bf16[64,4096]{1,0:T(8,128)(2,1)}, u32[]{:S(2)}, u32[]{:S(2)}) collective-permute-start(bf16[64,4096]{1,0:T(8,128)(2,1)} %get-tuple-element.222), channel_id=1, source_target_pairs={{0,8},{2,10},{4,12},{6,14},{8,0},{10,2},{12,4},{14,6},{16,24},{18,... | collective-permute-start | bytes 1572872 | tf_op jit(solution)/shard_map/ppermute | solution.py:376
  545.7 36.6 %collective-permute-start.34 = (bf16[64,4096]{1,0:T(8,128)(2,1)}, bf16[64,4096]{1,0:T(8,128)(2,1)}, u32[]{:S(2)}, u32[]{:S(2)}) collective-permute-start(bf16[64,4096]{1,0:T(8,128)(2,1)} %get-tuple-element.223), channel_id=1, source_target_pairs={{0,16},{2,18},{4,20},{6,22},{8,24},{10,26},{12,28},{14,30},{16,0},... | collective-permute-start | bytes 1572872 | tf_op jit(solution)/shard_map/ppermute | solution.py:376
  562.7 30.2 %collective-permute-start.35 = (bf16[64,4096]{1,0:T(8,128)(2,1)}, bf16[64,4096]{1,0:T(8,128)(2,1)}, u32[]{:S(2)}, u32[]{:S(2)}) collective-permute-start(bf16[64,4096]{1,0:T(8,128)(2,1)} %get-tuple-element.224), channel_id=1, source_target_pairs={{0,24},{2,26},{4,28},{6,30},{8,16},{10,18},{12,20},{14,22},{16,8},... | collective-permute-start | bytes 1572872 | tf_op jit(solution)/shard_map/ppermute | solution.py:376
  611.6 45.3 %collective-permute-start.41 = (bf16[256,4096]{1,0:T(8,128)(2,1)}, bf16[256,4096]{1,0:T(8,128)(2,1)}, u32[]{:S(2)}, u32[]{:S(2)}) collective-permute-start(bf16[256,4096]{1,0:T(8,128)(2,1)} %pad_maximum_fusion.2), channel_id=1, source_target_pairs={{0,4},{2,6},{4,0},{6,2},{8,12},{10,14},{12,8},{14,10},{16,20},{18,... | collective-permute-start | bytes 6291464 | tf_op jit(solution)/shard_map/ppermute | solution.py:376
  612.2 46.0 %collective-permute-start.42 = (bf16[256,4096]{1,0:T(8,128)(2,1)}, bf16[256,4096]{1,0:T(8,128)(2,1)}, u32[]{:S(2)}, u32[]{:S(2)}) collective-permute-start(bf16[256,4096]{1,0:T(8,128)(2,1)} %pad_maximum_fusion.3), channel_id=1, source_target_pairs={{0,1},{1,0},{2,3},{3,2},{4,5},{5,4},{6,7},{7,6},{8,9},{9,8},{10,11... | collective-permute-start | bytes 6291464 | tf_op jit(solution)/shard_map/ppermute | solution.py:381
  613.6 34.4 %collective-permute-start.38 = (bf16[64,2048]{1,0:T(8,128)(2,1)}, bf16[64,2048]{1,0:T(8,128)(2,1)S(1)}, u32[]{:S(2)}, u32[]{:S(2)}) collective-permute-start(bf16[64,2048]{1,0:T(8,128)(2,1)} %get-tuple-element.238), channel_id=1, source_target_pairs={{0,8},{2,10},{4,12},{6,14},{8,0},{10,2},{12,4},{14,6},{16,24},{18,... | collective-permute-start | bytes 786440 | tf_op jit(solution)/shard_map/ppermute | solution.py:376
  616.2 31.9 %collective-permute-start.39 = (bf16[64,2048]{1,0:T(8,128)(2,1)}, bf16[64,2048]{1,0:T(8,128)(2,1)}, u32[]{:S(2)}, u32[]{:S(2)}) collective-permute-start(bf16[64,2048]{1,0:T(8,128)(2,1)} %get-tuple-element.239), channel_id=1, source_target_pairs={{0,16},{2,18},{4,20},{6,22},{8,24},{10,26},{12,28},{14,30},{16,0},... | collective-permute-start | bytes 786440 | tf_op jit(solution)/shard_map/ppermute | solution.py:376
  616.8 31.2 %collective-permute-start.40 = (bf16[64,2048]{1,0:T(8,128)(2,1)}, bf16[64,2048]{1,0:T(8,128)(2,1)}, u32[]{:S(2)}, u32[]{:S(2)}) collective-permute-start(bf16[64,2048]{1,0:T(8,128)(2,1)} %get-tuple-element.240), channel_id=1, source_target_pairs={{0,24},{2,26},{4,28},{6,30},{8,16},{10,18},{12,20},{14,22},{16,8},... | collective-permute-start | bytes 786440 | tf_op jit(solution)/shard_map/ppermute | solution.py:376
  672.9 43.9 %collective-permute-start.48 = (bf16[64,4096]{1,0:T(8,128)(2,1)}, bf16[64,4096]{1,0:T(8,128)(2,1)}, u32[]{:S(2)}, u32[]{:S(2)}) collective-permute-start(bf16[64,4096]{1,0:T(8,128)(2,1)} %get-tuple-element.272), channel_id=1, source_target_pairs={{0,8},{2,10},{4,12},{6,14},{8,0},{10,2},{12,4},{14,6},{16,24},{18,... | collective-permute-start | bytes 1572872 | tf_op jit(solution)/shard_map/ppermute | solution.py:376
  674.9 41.9 %collective-permute-start.49 = (bf16[64,4096]{1,0:T(8,128)(2,1)}, bf16[64,4096]{1,0:T(8,128)(2,1)}, u32[]{:S(2)}, u32[]{:S(2)}) collective-permute-start(bf16[64,4096]{1,0:T(8,128)(2,1)} %get-tuple-element.273), channel_id=1, source_target_pairs={{0,16},{2,18},{4,20},{6,22},{8,24},{10,26},{12,28},{14,30},{16,0},... | collective-permute-start | bytes 1572872 | tf_op jit(solution)/shard_map/ppermute | solution.py:376
  675.6 47.3 %collective-permute-start.50 = (bf16[64,4096]{1,0:T(8,128)(2,1)}, bf16[64,4096]{1,0:T(8,128)(2,1)}, u32[]{:S(2)}, u32[]{:S(2)}) collective-permute-start(bf16[64,4096]{1,0:T(8,128)(2,1)} %get-tuple-element.274), channel_id=1, source_target_pairs={{0,24},{2,26},{4,28},{6,30},{8,16},{10,18},{12,20},{14,22},{16,8},... | collective-permute-start | bytes 1572872 | tf_op jit(solution)/shard_map/ppermute | solution.py:376
  (119 other events, 1301.2 us)
Sparse Core Ops, SparseCore 0:
  11.6 104.9 all-gather.2
  120.1 160.2 all-gather.4

commit v5 on v4

--- a/solution.py
+++ b/solution.py
@@ -221,26 +221,18 @@
 
     def kernel(which_ref, *refs):
         out_ref = refs[-1]
-        begin = pl.program_id(0) == 0
+
+        @pl.when(pl.program_id(0) == 0)
+        def _():
+            out_ref[...] = jnp.zeros_like(out_ref)
+
         place = 0
         for b, height in enumerate(heights):
             cols = slice(place, place + height)
-            total = sum(
-                dot_nt(refs[t][...], refs[parts + t * len(heights) + b][...])
-                for t in range(parts)
-            )
-            if stack * per == 1:
-                out_ref[:, cols] = total
-            else:
-
-                @pl.when(begin)
-                def _():
-                    out_ref[:, cols] = total
-
-                @pl.when(jnp.logical_not(begin))
-                def _():
-                    out_ref[:, cols] += total
-
+            total = out_ref[:, cols]
+            for t in range(parts):
+                total += dot_nt(refs[t][...], refs[parts + t * len(heights) + b][...])
+            out_ref[:, cols] = total
             place += height
 
     return pl.pallas_call(
@@ -676,12 +668,11 @@
         second_low = grad_second.astype(BF)
         (grad_pre,) = times_weight(relative_t, second_low, down, hidden, leave, [slopes], [BF], "leave")
         if flying is not None:
-            line, corners, other_line, other_sides = flying
-            grad_pre, corners, other_sides = hold(grad_pre, corners, other_sides)
+            line, corners, other_addends = flying
+            grad_pre, corners = hold(grad_pre, corners)
             sums = scatter_sum(line, corners)
-            pieces = scatter_pieces(other_line, other_sides)
-            grad_pre, sums, pieces = hold(grad_pre, sums, pieces)
-            sides, other_addends = scatter_sides(sums), scatter_far(pieces)
+            grad_pre, sums = hold(grad_pre, sums)
+            sides = scatter_sides(sums)
         turned = (lambda v: v) if l == 0 else (lambda v: dot(v, pick).astype(BF))
         mlp_pairs = [(turned(mid_low), grad_pre[None]), (turned(second_low), hidden_out[None])]
         mlp_send = weight_grads(mlp_pairs, blocks, 1, 2, name="mlp_send")
@@ -725,13 +716,10 @@
         if flying is not None:
             attn_send, addends = hold(attn_send, addends)
             attn_done[l + 1] = scatter_end(addends)
-        if l == 0:
-            attn_send, grad_proj, mlp_sides = hold(attn_send, grad_proj, mlp_sides)
-            mlp_pieces = scatter_pieces(mlp_line, mlp_sides)
-            attn_send, grad_proj, mlp_pieces = hold(attn_send, grad_proj, mlp_pieces)
-            mlp_addends = scatter_far(mlp_pieces)
-        else:
-            attn_send, grad_proj = hold(attn_send, grad_proj)
+        attn_send, grad_proj, mlp_sides = hold(attn_send, grad_proj, mlp_sides)
+        mlp_pieces = scatter_pieces(mlp_line, mlp_sides)
+        attn_send, grad_proj, mlp_pieces = hold(attn_send, grad_proj, mlp_pieces)
+        mlp_addends = scatter_far(mlp_pieces)
         attn_came = over_dp(attn_send, 1)
         if l > 0:
             back = times_transposed(relative_t, grad_proj, qkv, "grad_stream")
@@ -782,7 +770,7 @@
             input_grad = select_wide(after(grad_first, attn_sums), unpick) + back
         else:
             attn_line, back = hold(attn_line, back)
-            flying = attn_line, scatter_corners(attn_line), mlp_line, mlp_sides
+            flying = attn_line, scatter_corners(attn_line), mlp_addends
             grad_stream = grad_first + back
 
     return (

time: 789 us -> 785 us (level)
  Pallas kernels: 306 us -> 294 us
    pallas_call x8, Pallas kernels: 80 us -> 68.2 us  [times_transposed(): pl.pallas_call(kernel, grid_spec=pltpu.PrefetchScalarGridSpec(num_scalar_...]
  transfers between devices with their start and end apart: 61 -> 61, of which waited for: 32 -> 29; matrix products, arithmetic and copies ran while one was open for 16% -> 15% of each run, Pallas kernels for 23% -> 24%
where the time goes in v5:
time: 785 us; the launch traced here: 777 us
  Pallas kernels  294 us (37%)
  waiting for transfers between devices  225 us (29%)
  other arithmetic  91.1 us (12%)
  local copies, waits for them, and re-layouts  62.6 us (8%)
  starting transfers between devices  56.8 us (7%)
  matrix products  32.2 us (4%)
  between operations  16 us (2%)
    ppermute x42, waiting for transfers between devices, over_dp(): return lax.ppermute(value, 'dp', [(i, i ^ mask) for i in range(count)])  135 us
    pallas_call x8, Pallas kernels, weight_grads(): pl.pallas_call(kernel, grid=(sum(counts),), in_specs=in_specs, out_specs=...  77.7 us
    pallas_call x8, Pallas kernels, times_weight(): pl.pallas_call(kernel, grid_spec=pltpu.PrefetchScalarGridSpec(num_scalar_...  75.4 us
    pallas_call x8, Pallas kernels, times_transposed(): pl.pallas_call(kernel, grid_spec=pltpu.PrefetchScalarGridSpec(num_scalar_...  68.2 us
    ppermute x12, waiting for transfers between devices, over_tensor(): lax.ppermute(value, ('thi', 'tlo'), [(i, i ^ mask) for i in range(count)])  52.8 us
    pallas_call x2, Pallas kernels, attend_back(): pl.pallas_call(attend_back_kernel, grid=(sets, parts * pairs), in_specs=s...  45.6 us
    ppermute x42, starting transfers between devices, over_dp(): return lax.ppermute(value, 'dp', [(i, i ^ mask) for i in range(count)])  42.1 us
    dot_general x14, matrix products, dot(): return jnp.dot(a, b, preferred_element_type=F32)  32.2 us
  transfers between devices with their start and end apart: 61, of which 29 were waited for; matrix products, arithmetic and copies ran while one was open for 15% of the time, Pallas kernels for 24%

profile of v5, /device:TPU:8, one launch (start us, length us, event | category | flops | bytes accessed | tf_op | source)
XLA Modules:
  0.0 777.5 jit_solution(5863141733013498384)
XLA Ops:
  18.8 24.3 %collective-permute-done.2 = bf16[64,2560]{1,0:T(8,128)(2,1)S(1)} collective-permute-done((bf16[64,2560]{1,0:T(8,128)(2,1)S(1)}, bf16[64,2560]{1,0:T(8,128)(2,1)S(1)}, u32[]{:S(2)}, u32[]{:S(2)}) %collective-permute-start.2) | collective-permute-done | bytes 327712 | tf_op jit(solution)/shard_map/ppermute | solution.py:368
  58.2 31.7 %collective-permute-done.6.refs_6_.refs_4_ = bf16[256,2560]{1,0:T(8,128)(2,1)S(1)} collective-permute-done((bf16[256,2560]{1,0:T(8,128)(2,1)S(1)}, bf16[256,2560]{1,0:T(8,128)(2,1)S(1)}, u32[]{:S(2)}, u32[]{:S(2)}) %collective-permute-start.6) | collective-permute-done | bytes 1310752 | tf_op jit(solution)/shard_map/ppermute | solution.py:373
  103.4 14.8 %collective-permute-done.5 = bf16[64,2048]{1,0:T(8,128)(2,1)} collective-permute-done((bf16[64,2048]{1,0:T(8,128)(2,1)S(1)}, bf16[64,2048]{1,0:T(8,128)(2,1)}, u32[]{:S(2)}, u32[]{:S(2)}) %collective-permute-start.5) | collective-permute-done | bytes 262176 | tf_op jit(solution)/shard_map/ppermute | solution.py:368
  139.3 9.0 %project.2.q_ref.k_ref.v_ref = bf16[512,3072]{1,0:T(8,128)(2,1)} custom-call(s32[2]{0:T(128)} %iota_xor_fusion.which_ref, bf16[512,1024]{1,0:T(8,128)(2,1)} %x_ref.1, bf16[2048,1664]{1,0:T(8,128)(2,1)} %all-gather.3.cloned.1.call-done.refs_0_.refs_1_.refs_2_.refs_3_, bf16[2048,1664]{1,0:T(8,128)(2,1)} %all-gather.3.cloned.1.call-done.refs_0_.refs_1_.refs_2_.refs_3_, ...), custom_call_target="tpu_custom_call" | custom-call | flops 3221225472 | bytes 2097152 | tf_op jit(solution)/shard_map/project/pallas_call | solution.py:192
  148.4 8.9 %collective-permute-done.10.refs_3_.refs_1_ = bf16[256,2048]{1,0:T(8,128)(2,1)} collective-permute-done((bf16[256,2048]{1,0:T(8,128)(2,1)}, bf16[256,2048]{1,0:T(8,128)(2,1)}, u32[]{:S(2)}, u32[]{:S(2)}) %collective-permute-start.10) | collective-permute-done | bytes 1048608 | tf_op jit(solution)/shard_map/ppermute | solution.py:368
  170.8 13.7 %collective-permute-done.13 = bf16[128,2048]{1,0:T(8,128)(2,1)} collective-permute-done((bf16[128,2048]{1,0:T(8,128)(2,1)}, bf16[128,2048]{1,0:T(8,128)(2,1)}, u32[]{:S(2)}, u32[]{:S(2)}) %collective-permute-start.13) | collective-permute-done | bytes 524320 | tf_op jit(solution)/shard_map/ppermute | solution.py:373
  187.4 13.3 %attend.2 = bf16[512,1024]{1,0:T(8,128)(2,1)} custom-call(bf16[512,3072]{1,0:T(8,128)(2,1)} %project.2.q_ref.k_ref.v_ref, bf16[512,3072]{1,0:T(8,128)(2,1)} %project.2.q_ref.k_ref.v_ref, bf16[512,3072]{1,0:T(8,128)(2,1)} %project.2.q_ref.k_ref.v_ref, s32[1,1,512]{2,1,0:T(1,128)} %get-tuple-element.439.segq_ref, s32[1,512,1]{2,1,0:T(8,128)} %copy.49.segk_ref), custom_call_target="tpu_custom_call" | custom-call | flops 4294967296 | bytes 6291456 | tf_op jit(solution)/shard_map/attend/pallas_call | solution.py:106
  214.6 13.0 %enter.2 = (bf16[512,4096]{1,0:T(8,128)(2,1)}, bf16[512,4096]{1,0:T(8,128)(2,1)}) custom-call(s32[2]{0:T(128)} %iota_xor_fusion.which_ref, bf16[512,1024]{1,0:T(8,128)(2,1)} %fusion.31.x_ref.refs_0_, bf16[256,2560]{1,0:T(8,128)(2,1)} %copy-done.7, bf16[256,2560]{1,0:T(8,128)(2,1)} %collective-permute-done.7.refs_3_.refs_1_, ...), custom_call_target="tpu_custom_call" | custom-call | flops 4294967296 | bytes 2097152 | tf_op jit(solution)/shard_map/enter/pallas_call | solution.py:192
  228.6 10.1 %branch.2 = f32[512,1024]{1,0:T(8,128)} custom-call(s32[2]{0:T(128)} %iota_xor_fusion.which_ref, bf16[1,512,4096]{2,1,0:T(8,128)(2,1)} %bitcast.201, bf16[1,512,4096]{2,1,0:T(8,128)(2,1)} %bitcast.202, bf16[256,2048]{1,0:T(8,128)(2,1)} %pad_maximum_fusion.5.refs_2_.refs_0_, bf16[256,2048]{1,0:T(8,128)(2,1)} %collective-permute-done.10.refs_3_.refs_1_, ...), custom_call_target="tpu_custom_call" | custom-call | flops 4294967296 | bytes 4194304 | tf_op jit(solution)/shard_map/branch/pallas_call | solution.py:238
  248.5 31.8 %all-gather.5.cloned.1.call-done.refs_0_.refs_1_.refs_2_.refs_3_ = bf16[2048,6144]{1,0:T(8,128)(2,1)} async-done(((bf16[64,6144]{1,0:T(8,128)(2,1)}), bf16[2048,6144]{1,0:T(8,128)(2,1)}) %all-gather.5.cloned.1.call-update) | async-done | bytes 25165840 | tf_op jit(solution)/shard_map/all_gather | solution.py:528
  280.3 8.5 %project.3.q_ref.k_ref.v_ref = bf16[512,3072]{1,0:T(8,128)(2,1)} custom-call(s32[2]{0:T(128)} %iota_xor_fusion.which_ref, bf16[512,1024]{1,0:T(8,128)(2,1)} %get-tuple-element.449.x_ref, bf16[2048,6144]{1,0:T(8,128)(2,1)} %all-gather.5.cloned.1.call-done.refs_0_.refs_1_.refs_2_.refs_3_, ...), custom_call_target="tpu_custom_call" | custom-call | flops 3221225472 | bytes 2097152 | tf_op jit(solution)/shard_map/project/pallas_call | solution.py:192
  288.9 13.4 %attend.3 = bf16[512,1024]{1,0:T(8,128)(2,1)} custom-call(bf16[512,3072]{1,0:T(8,128)(2,1)} %project.3.q_ref.k_ref.v_ref, bf16[512,3072]{1,0:T(8,128)(2,1)} %project.3.q_ref.k_ref.v_ref, bf16[512,3072]{1,0:T(8,128)(2,1)} %project.3.q_ref.k_ref.v_ref, s32[1,1,512]{2,1,0:T(1,128)} %get-tuple-element.439.segq_ref, s32[1,512,1]{2,1,0:T(8,128)} %copy.49.segk_ref), custom_call_target="tpu_custom_call" | custom-call | flops 4294967296 | bytes 6291456 | tf_op jit(solution)/shard_map/attend/pallas_call | solution.py:106
  313.2 13.1 %enter.3 = (bf16[512,4096]{1,0:T(8,128)(2,1)}, bf16[512,4096]{1,0:T(8,128)(2,1)}) custom-call(s32[2]{0:T(128)} %iota_xor_fusion.which_ref, bf16[512,1024]{1,0:T(8,128)(2,1)} %copy-done.23, bf16[2048,6144]{1,0:T(8,128)(2,1)} %all-gather.5.cloned.1.call-done.refs_0_.refs_1_.refs_2_.refs_3_, ...), custom_call_target="tpu_custom_call" | custom-call | flops 4294967296 | bytes 2097152 | tf_op jit(solution)/shard_map/enter/pallas_call | solution.py:192
  326.4 9.8 %branch.3 = f32[512,1024]{1,0:T(8,128)} custom-call(s32[2]{0:T(128)} %iota_xor_fusion.which_ref, bf16[1,512,4096]{2,1,0:T(8,128)(2,1)} %bitcast.195, bf16[1,512,4096]{2,1,0:T(8,128)(2,1)} %bitcast.196, bf16[2048,6144]{1,0:T(8,128)(2,1)} %all-gather.5.cloned.1.call-done.refs_0_.refs_1_.refs_2_.refs_3_, ...), custom_call_target="tpu_custom_call" | custom-call | flops 4294967296 | bytes 4194304 | tf_op jit(solution)/shard_map/branch/pallas_call | solution.py:238
  346.5 10.7 %leave.2 = bf16[512,4096]{1,0:T(8,128)(2,1)} custom-call(s32[2]{0:T(128)} %iota_xor_fusion.which_ref, bf16[512,1024]{1,0:T(8,128)(2,1)} %copy-done.20, bf16[2048,6144]{1,0:T(8,128)(2,1)} %all-gather.5.cloned.1.call-done.refs_0_.refs_1_.refs_2_.refs_3_, bf16[2048,6144]{1,0:T(8,128)(2,1)} %all-gather.5.cloned.1.call-done.refs_0_.refs_1_.refs_2_.refs_3_, ...), custom_call_target="tpu_custom_call" | custom-call | flops 536870912 | bytes 262144 | tf_op jit(solution)/shard_map/leave/pallas_call | solution.py:192
  357.2 11.0 %mlp_send.2 = bf16[2,512,4096]{2,1,0:T(8,128)(2,1)} custom-call(bf16[512,1024]{1,0:T(8,128)(2,1)} %fusion.33.refs_0_, bf16[1,512,4096]{2,1,0:T(8,128)(2,1)} %bitcast.183, bf16[1,512,4096]{2,1,0:T(8,128)(2,1)} %bitcast.184, bf16[512,1024]{1,0:T(8,128)(2,1)} %fusion.34.refs_3_, bf16[1,512,4096]{2,1,0:T(8,128)(2,1)} %bitcast.197, bf16[1,512,4096]{2,1,0:T(8,128)(2,1)} %bitcast.198), custom_call_target="tpu_custom_call" | custom-call | flops 536870912 | bytes 1048576 | tf_op jit(solution)/shard_map/mlp_send/pallas_call | solution.py:315
  368.4 9.8 %grad_mid.2 = f32[512,1024]{1,0:T(8,128)} custom-call(s32[2]{0:T(128)} %iota_xor_fusion.which_ref, bf16[1,512,4096]{2,1,0:T(8,128)(2,1)} %bitcast.185, bf16[1,512,4096]{2,1,0:T(8,128)(2,1)} %bitcast.186, bf16[2048,6144]{1,0:T(8,128)(2,1)} %all-gather.5.cloned.1.call-done.refs_0_.refs_1_.refs_2_.refs_3_, ...), custom_call_target="tpu_custom_call" | custom-call | flops 536870912 | bytes 524288 | tf_op jit(solution)/shard_map/grad_mid/pallas_call | solution.py:238
  381.7 12.1 %mlp_keep.2 = (bf16[256,4096]{1,0:T(8,128)(2,1)}, bf16[256,4096]{1,0:T(8,128)(2,1)}, bf16[256,4096]{1,0:T(8,128)(2,1)}, bf16[256,4096]{1,0:T(8,128)(2,1)}) custom-call(bf16[512,1024]{1,0:T(8,128)(2,1)} %fusion.33.refs_0_, bf16[1,512,4096]{2,1,0:T(8,128)(2,1)} %bitcast.187, bf16[1,512,4096]{2,1,0:T(8,128)(2,1)} %bitcast.188, ...), custom_call_target="tpu_custom_call" | custom-call | flops 536870912 | bytes 1048576 | tf_op jit(solution)/shard_map/mlp_keep/pallas_call | solution.py:315
  409.4 13.2 %collective-permute-done.23 = bf16[128,4096]{1,0:T(8,128)(2,1)S(1)} collective-permute-done((bf16[128,4096]{1,0:T(8,128)(2,1)}, bf16[128,4096]{1,0:T(8,128)(2,1)S(1)}, u32[]{:S(2)}, u32[]{:S(2)}) %collective-permute-start.23) | collective-permute-done | bytes 1048608 | tf_op jit(solution)/shard_map/ppermute | solution.py:368
  435.7 22.8 %attend_back.2.refs_1_.refs_2_.refs_0_ = bf16[3,512,1024]{2,1,0:T(8,128)(2,1)} custom-call(bf16[512,3072]{1,0:T(8,128)(2,1)} %project.3.q_ref.k_ref.v_ref, bf16[512,3072]{1,0:T(8,128)(2,1)} %project.3.q_ref.k_ref.v_ref, bf16[512,3072]{1,0:T(8,128)(2,1)} %project.3.q_ref.k_ref.v_ref, bf16[512,1024]{1,0:T(8,128)(2,1)} %grad_mix.2.grad_ref, ...), custom_call_target="tpu_custom_call" | custom-call | flops 1342177280 | bytes 1572864 | tf_op jit(solution)/shard_map/attend_back/pallas_call | solution.py:134
  465.9 10.1 %collective-permute-done.25 = bf16[256,4096]{1,0:T(8,128)(2,1)} collective-permute-done((bf16[256,4096]{1,0:T(8,128)(2,1)}, bf16[256,4096]{1,0:T(8,128)(2,1)}, u32[]{:S(2)}, u32[]{:S(2)}) %collective-permute-start.25) | collective-permute-done | bytes 2097184 | tf_op jit(solution)/shard_map/ppermute | solution.py:368
  480.4 8.4 %grad_stream.2 = f32[512,1024]{1,0:T(8,128)} custom-call(s32[2]{0:T(128)} %iota_xor_fusion.which_ref, bf16[3,512,1024]{2,1,0:T(8,128)(2,1)} %attend_back.2.refs_1_.refs_2_.refs_0_, bf16[3,512,1024]{2,1,0:T(8,128)(2,1)} %attend_back.2.refs_1_.refs_2_.refs_0_, bf16[2048,6144]{1,0:T(8,128)(2,1)} %all-gather.5.cloned.1.call-done.refs_0_.refs_1_.refs_2_.refs_3_, ...), custom_call_target="tpu_custom_call" | custom-call | flops 402653184 | bytes 393216 | tf_op jit(solution)/shard_map/grad_stream/pallas_call | solution.py:238
  488.8 8.8 %attn_keep.2 = (bf16[256,2048]{1,0:T(8,128)(2,1)}, bf16[256,2048]{1,0:T(8,128)(2,1)}, bf16[256,2048]{1,0:T(8,128)(2,1)}, bf16[256,2048]{1,0:T(8,128)(2,1)}) custom-call(bf16[512,1024]{1,0:T(8,128)(2,1)} %fusion.35.refs_0_, bf16[3,512,1024]{2,1,0:T(8,128)(2,1)} %attend_back.2.refs_1_.refs_2_.refs_0_, ...), custom_call_target="tpu_custom_call" | custom-call | flops 268435456 | bytes 524288 | tf_op jit(solution)/shard_map/attn_keep/pallas_call | solution.py:315
  511.6 11.1 %leave.3 = bf16[512,4096]{1,0:T(8,128)(2,1)} custom-call(s32[2]{0:T(128)} %iota_xor_fusion.which_ref, bf16[512,1024]{1,0:T(8,128)(2,1)} %convert_element_type.449.x_ref.refs_3_, bf16[256,2048]{1,0:T(8,128)(2,1)} %pad_maximum_fusion.5.refs_2_.refs_0_, bf16[256,2048]{1,0:T(8,128)(2,1)} %collective-permute-done.10.refs_3_.refs_1_, ...), custom_call_target="tpu_custom_call" | custom-call | flops 536870912 | bytes 262144 | tf_op jit(solution)/shard_map/leave/pallas_call | solution.py:192
  527.8 10.5 %mlp_send.3 = bf16[2,512,4096]{2,1,0:T(8,128)(2,1)} custom-call(bf16[512,1024]{1,0:T(8,128)(2,1)} %fusion.31.x_ref.refs_0_, bf16[1,512,4096]{2,1,0:T(8,128)(2,1)} %bitcast.189, bf16[1,512,4096]{2,1,0:T(8,128)(2,1)} %bitcast.190, bf16[512,1024]{1,0:T(8,128)(2,1)} %convert_element_type.449.x_ref.refs_3_, bf16[1,512,4096]{2,1,0:T(8,128)(2,1)} %bitcast.203, ...), custom_call_target="tpu_custom_call" | custom-call | flops 536870912 | bytes 1048576 | tf_op jit(solution)/shard_map/mlp_send/pallas_call | solution.py:315
  543.7 10.2 %grad_mid.3 = f32[512,1024]{1,0:T(8,128)} custom-call(s32[2]{0:T(128)} %iota_xor_fusion.which_ref, bf16[1,512,4096]{2,1,0:T(8,128)(2,1)} %bitcast.191, bf16[1,512,4096]{2,1,0:T(8,128)(2,1)} %bitcast.192, bf16[256,2560]{1,0:T(8,128)(2,1)} %copy-done.7, bf16[256,2560]{1,0:T(8,128)(2,1)} %collective-permute-done.7.refs_3_.refs_1_, ...), custom_call_target="tpu_custom_call" | custom-call | flops 536870912 | bytes 524288 | tf_op jit(solution)/shard_map/grad_mid/pallas_call | solution.py:238
  554.6 12.0 %mlp_keep.3 = (bf16[256,4096]{1,0:T(8,128)(2,1)}, bf16[256,4096]{1,0:T(8,128)(2,1)}, bf16[256,4096]{1,0:T(8,128)(2,1)}, bf16[256,4096]{1,0:T(8,128)(2,1)}) custom-call(bf16[512,1024]{1,0:T(8,128)(2,1)} %fusion.31.x_ref.refs_0_, bf16[1,512,4096]{2,1,0:T(8,128)(2,1)} %bitcast.193, bf16[1,512,4096]{2,1,0:T(8,128)(2,1)} %bitcast.194, ...), custom_call_target="tpu_custom_call" | custom-call | flops 536870912 | bytes 1048576 | tf_op jit(solution)/shard_map/mlp_keep/pallas_call | solution.py:315
  613.8 22.8 %attend_back.3.refs_1_.refs_2_.refs_0_ = bf16[3,512,1024]{2,1,0:T(8,128)(2,1)} custom-call(bf16[512,3072]{1,0:T(8,128)(2,1)} %project.2.q_ref.k_ref.v_ref, bf16[512,3072]{1,0:T(8,128)(2,1)} %project.2.q_ref.k_ref.v_ref, bf16[512,3072]{1,0:T(8,128)(2,1)} %project.2.q_ref.k_ref.v_ref, bf16[512,1024]{1,0:T(8,128)(2,1)} %grad_mix.3.grad_ref, ...), custom_call_target="tpu_custom_call" | custom-call | flops 1342177280 | bytes 1572864 | tf_op jit(solution)/shard_map/attend_back/pallas_call | solution.py:134
  644.2 9.2 %collective-permute-done.41 = bf16[256,4096]{1,0:T(8,128)(2,1)} collective-permute-done((bf16[256,4096]{1,0:T(8,128)(2,1)}, bf16[256,4096]{1,0:T(8,128)(2,1)}, u32[]{:S(2)}, u32[]{:S(2)}) %collective-permute-start.41) | collective-permute-done | bytes 2097184 | tf_op jit(solution)/shard_map/ppermute | solution.py:368
  673.0 8.4 %attn_keep.3 = (bf16[256,2048]{1,0:T(8,128)(2,1)}, bf16[256,2048]{1,0:T(8,128)(2,1)}, bf16[256,2048]{1,0:T(8,128)(2,1)}, bf16[256,2048]{1,0:T(8,128)(2,1)}) custom-call(bf16[512,1024]{1,0:T(8,128)(2,1)} %get-tuple-element.452.refs_0_, bf16[3,512,1024]{2,1,0:T(8,128)(2,1)} %attend_back.3.refs_1_.refs_2_.refs_0_, ...), custom_call_target="tpu_custom_call" | custom-call | flops 268435456 | bytes 524288 | tf_op jit(solution)/shard_map/attn_keep/pallas_call | solution.py:315
  685.7 8.7 %grad_stream.3 = f32[512,1024]{1,0:T(8,128)} custom-call(s32[2]{0:T(128)} %iota_xor_fusion.which_ref, bf16[3,512,1024]{2,1,0:T(8,128)(2,1)} %attend_back.3.refs_1_.refs_2_.refs_0_, bf16[3,512,1024]{2,1,0:T(8,128)(2,1)} %attend_back.3.refs_1_.refs_2_.refs_0_, bf16[2048,1664]{1,0:T(8,128)(2,1)} %all-gather.3.cloned.1.call-done.refs_0_.refs_1_.refs_2_.refs_3_, ...), custom_call_target="tpu_custom_call" | custom-call | flops 402653184 | bytes 393216 | tf_op jit(solution)/shard_map/grad_stream/pallas_call | solution.py:238
  754.7 8.0 %collective-permute-done.54 = bf16[64,2048]{1,0:T(8,128)(2,1)S(1)} collective-permute-done((bf16[64,2048]{1,0:T(8,128)(2,1)S(1)}, bf16[64,2048]{1,0:T(8,128)(2,1)S(1)}, u32[]{:S(2)}, u32[]{:S(2)}) %collective-permute-start.54) | collective-permute-done | bytes 262176 | tf_op jit(solution)/shard_map/ppermute | solution.py:368
  (580 shorter events, 337.9 us)
Async XLA Ops:
  7.2 121.5 %all-gather.3.cloned.1.call-start = ((), (), s32[]{:S(2)}) async-start(), calls=%async_computation | async-start | bytes 7028736 | tf_op jit(solution)/shard_map/all_gather | solution.py:528
  11.5 268.8 %all-gather.5.cloned.1.call-start = ((), (), s32[]{:S(2)}) async-start(), calls=%async_computation.1 | async-start | bytes 25952256 | tf_op jit(solution)/shard_map/all_gather | solution.py:528
  14.1 29.1 %collective-permute-start.2 = (bf16[64,2560]{1,0:T(8,128)(2,1)S(1)}, bf16[64,2560]{1,0:T(8,128)(2,1)S(1)}, u32[]{:S(2)}, u32[]{:S(2)}) collective-permute-start(bf16[64,2560]{1,0:T(8,128)(2,1)S(1)} %pad_maximum_fusion.14), channel_id=1, source_target_pairs={{0,24},{2,26},{4,28},{6,30},{8,16},{10,18},{12,20},{14,22},{16,8},... | collective-permute-start | bytes 983048 | tf_op jit(solution)/shard_map/ppermute | solution.py:368
  15.7 32.6 %collective-permute-start.1 = (bf16[64,2560]{1,0:T(8,128)(2,1)S(1)}, bf16[64,2560]{1,0:T(8,128)(2,1)S(1)}, u32[]{:S(2)}, u32[]{:S(2)}) collective-permute-start(bf16[64,2560]{1,0:T(8,128)(2,1)S(1)} %pad_maximum_fusion.14), channel_id=1, source_target_pairs={{0,16},{2,18},{4,20},{6,22},{8,24},{10,26},{12,28},{14,30},{16,0},... | collective-permute-start | bytes 983048 | tf_op jit(solution)/shard_map/ppermute | solution.py:368
  16.8 31.5 %collective-permute-start = (bf16[64,2560]{1,0:T(8,128)(2,1)S(1)}, bf16[64,2560]{1,0:T(8,128)(2,1)}, u32[]{:S(2)}, u32[]{:S(2)}) collective-permute-start(bf16[64,2560]{1,0:T(8,128)(2,1)S(1)} %pad_maximum_fusion.14), channel_id=1, source_target_pairs={{0,8},{2,10},{4,12},{6,14},{8,0},{10,2},{12,4},{14,6},{16,24},{18,... | collective-permute-start | bytes 983048 | tf_op jit(solution)/shard_map/ppermute | solution.py:368
  49.5 40.5 %collective-permute-start.6 = (bf16[256,2560]{1,0:T(8,128)(2,1)S(1)}, bf16[256,2560]{1,0:T(8,128)(2,1)S(1)}, u32[]{:S(2)}, u32[]{:S(2)}) collective-permute-start(bf16[256,2560]{1,0:T(8,128)(2,1)S(1)} %pad_maximum_fusion.4.refs_2_.refs_0_), channel_id=1, source_target_pairs={{0,1},{1,0},{2,3},{3,2},{4,5},{5,4},{6,7},{7,6},{8,9},{9,8},{10,11... | collective-permute-start | bytes 3932168 | tf_op jit(solution)/shard_map/ppermute | solution.py:373
  51.2 46.9 %collective-permute-start.7 = (bf16[256,2560]{1,0:T(8,128)(2,1)S(1)}, bf16[256,2560]{1,0:T(8,128)(2,1)}, u32[]{:S(2)}, u32[]{:S(2)}) collective-permute-start(bf16[256,2560]{1,0:T(8,128)(2,1)S(1)} %pad_maximum_fusion.4.refs_2_.refs_0_), channel_id=1, source_target_pairs={{0,4},{2,6},{4,0},{6,2},{8,12},{10,14},{12,8},{14,10},{16,20},{18,... | collective-permute-start | bytes 3932168 | tf_op jit(solution)/shard_map/ppermute | solution.py:368
  90.9 32.4 %collective-permute-start.8 = (bf16[128,2560]{1,0:T(8,128)(2,1)}, bf16[128,2560]{1,0:T(8,128)(2,1)S(1)}, u32[]{:S(2)}, u32[]{:S(2)}) collective-permute-start(bf16[128,2560]{1,0:T(8,128)(2,1)} %slice.665), channel_id=1, source_target_pairs={{0,4},{2,6},{4,0},{6,2},{8,12},{10,14},{12,8},{14,10},{16,20},{18,... | collective-permute-start | bytes 1966088 | tf_op jit(solution)/shard_map/ppermute | solution.py:368
  92.4 25.8 %collective-permute-start.5 = (bf16[64,2048]{1,0:T(8,128)(2,1)S(1)}, bf16[64,2048]{1,0:T(8,128)(2,1)}, u32[]{:S(2)}, u32[]{:S(2)}) collective-permute-start(bf16[64,2048]{1,0:T(8,128)(2,1)S(1)} %slice_bitcast_fusion.6), channel_id=1, source_target_pairs={{0,24},{2,26},{4,28},{6,30},{8,16},{10,18},{12,20},{14,22},{16,8},... | collective-permute-start | bytes 786440 | tf_op jit(solution)/shard_map/ppermute | solution.py:368
  93.0 27.7 %collective-permute-start.4 = (bf16[64,2048]{1,0:T(8,128)(2,1)S(1)}, bf16[64,2048]{1,0:T(8,128)(2,1)}, u32[]{:S(2)}, u32[]{:S(2)}) collective-permute-start(bf16[64,2048]{1,0:T(8,128)(2,1)S(1)} %slice_bitcast_fusion.6), channel_id=1, source_target_pairs={{0,16},{2,18},{4,20},{6,22},{8,24},{10,26},{12,28},{14,30},{16,0},... | collective-permute-start | bytes 786440 | tf_op jit(solution)/shard_map/ppermute | solution.py:368
  118.2 84.8 %collective-permute-start.14 = (bf16[256,2560]{1,0:T(8,128)(2,1)S(1)}, bf16[256,2560]{1,0:T(8,128)(2,1)}, u32[]{:S(2)}, u32[]{:S(2)}) collective-permute-start(bf16[256,2560]{1,0:T(8,128)(2,1)S(1)} %pad_maximum_fusion.4.refs_2_.refs_0_), channel_id=1, source_target_pairs={{0,2},{2,0},{4,6},{6,4},{8,10},{10,8},{12,14},{14,12},{16,18},{18,... | collective-permute-start | bytes 3932168 | tf_op jit(solution)/shard_map/ppermute | solution.py:368
  122.9 80.7 %collective-permute-start.15 = (bf16[256,2560]{1,0:T(8,128)(2,1)}, bf16[256,2560]{1,0:T(8,128)(2,1)}, u32[]{:S(2)}, u32[]{:S(2)}) collective-permute-start(bf16[256,2560]{1,0:T(8,128)(2,1)} %collective-permute-done.7.refs_3_.refs_1_), channel_id=1, source_target_pairs={{0,2},{2,0},{4,6},{6,4},{8,10},{10,8},{12,14},{14,12},{16,18},{18,... | collective-permute-start | bytes 3932168 | tf_op jit(solution)/shard_map/ppermute | solution.py:368
  122.9 80.8 %collective-permute-start.16 = (bf16[256,2560]{1,0:T(8,128)(2,1)S(1)}, bf16[256,2560]{1,0:T(8,128)(2,1)}, u32[]{:S(2)}, u32[]{:S(2)}) collective-permute-start(bf16[256,2560]{1,0:T(8,128)(2,1)S(1)} %collective-permute-done.6.refs_6_.refs_4_), channel_id=1, source_target_pairs={{0,2},{2,0},{4,6},{6,4},{8,10},{10,8},{12,14},{14,12},{16,18},{18,... | collective-permute-start | bytes 3932168 | tf_op jit(solution)/shard_map/ppermute | solution.py:368
  126.3 31.0 %collective-permute-start.10 = (bf16[256,2048]{1,0:T(8,128)(2,1)}, bf16[256,2048]{1,0:T(8,128)(2,1)}, u32[]{:S(2)}, u32[]{:S(2)}) collective-permute-start(bf16[256,2048]{1,0:T(8,128)(2,1)} %pad_maximum_fusion.5.refs_2_.refs_0_), channel_id=1, source_target_pairs={{0,4},{2,6},{4,0},{6,2},{8,12},{10,14},{12,8},{14,10},{16,20},{18,... | collective-permute-start | bytes 3145736 | tf_op jit(solution)/shard_map/ppermute | solution.py:368
  126.8 30.9 %collective-permute-start.11 = (bf16[256,2048]{1,0:T(8,128)(2,1)}, bf16[256,2048]{1,0:T(8,128)(2,1)}, u32[]{:S(2)}, u32[]{:S(2)}) collective-permute-start(bf16[256,2048]{1,0:T(8,128)(2,1)} %pad_maximum_fusion.5.refs_2_.refs_0_), channel_id=1, source_target_pairs={{0,1},{1,0},{2,3},{3,2},{4,5},{5,4},{6,7},{7,6},{8,9},{9,8},{10,11... | collective-permute-start | bytes 3145736 | tf_op jit(solution)/shard_map/ppermute | solution.py:373
  157.3 46.8 %collective-permute-start.17 = (bf16[256,2560]{1,0:T(8,128)(2,1)}, bf16[256,2560]{1,0:T(8,128)(2,1)}, u32[]{:S(2)}, u32[]{:S(2)}) collective-permute-start(bf16[256,2560]{1,0:T(8,128)(2,1)} %constant_dynamic-update-slice_fusion.refs_7_.refs_5_), channel_id=1, source_target_pairs={{0,2},{2,0},{4,6},{6,4},{8,10},{10,8},{12,14},{14,12},{16,18},{18,... | collective-permute-start | bytes 3932168 | tf_op jit(solution)/shard_map/ppermute | solution.py:368
  429.0 47.0 %collective-permute-start.25 = (bf16[256,4096]{1,0:T(8,128)(2,1)}, bf16[256,4096]{1,0:T(8,128)(2,1)}, u32[]{:S(2)}, u32[]{:S(2)}) collective-permute-start(bf16[256,4096]{1,0:T(8,128)(2,1)} %pad_maximum_fusion), channel_id=1, source_target_pairs={{0,4},{2,6},{4,0},{6,2},{8,12},{10,14},{12,8},{14,10},{16,20},{18,... | collective-permute-start | bytes 6291464 | tf_op jit(solution)/shard_map/ppermute | solution.py:368
  429.6 46.7 %collective-permute-start.26 = (bf16[256,4096]{1,0:T(8,128)(2,1)}, bf16[256,4096]{1,0:T(8,128)(2,1)}, u32[]{:S(2)}, u32[]{:S(2)}) collective-permute-start(bf16[256,4096]{1,0:T(8,128)(2,1)} %pad_maximum_fusion.1), channel_id=1, source_target_pairs={{0,1},{1,0},{2,3},{3,2},{4,5},{5,4},{6,7},{7,6},{8,9},{9,8},{10,11... | collective-permute-start | bytes 6291464 | tf_op jit(solution)/shard_map/ppermute | solution.py:373
  538.3 32.8 %collective-permute-start.33 = (bf16[64,4096]{1,0:T(8,128)(2,1)}, bf16[64,4096]{1,0:T(8,128)(2,1)}, u32[]{:S(2)}, u32[]{:S(2)}) collective-permute-start(bf16[64,4096]{1,0:T(8,128)(2,1)} %get-tuple-element.226), channel_id=1, source_target_pairs={{0,8},{2,10},{4,12},{6,14},{8,0},{10,2},{12,4},{14,6},{16,24},{18,... | collective-permute-start | bytes 1572872 | tf_op jit(solution)/shard_map/ppermute | solution.py:368
  540.8 36.6 %collective-permute-start.34 = (bf16[64,4096]{1,0:T(8,128)(2,1)}, bf16[64,4096]{1,0:T(8,128)(2,1)}, u32[]{:S(2)}, u32[]{:S(2)}) collective-permute-start(bf16[64,4096]{1,0:T(8,128)(2,1)} %get-tuple-element.227), channel_id=1, source_target_pairs={{0,16},{2,18},{4,20},{6,22},{8,24},{10,26},{12,28},{14,30},{16,0},... | collective-permute-start | bytes 1572872 | tf_op jit(solution)/shard_map/ppermute | solution.py:368
  542.2 46.3 %collective-permute-start.35 = (bf16[64,4096]{1,0:T(8,128)(2,1)}, bf16[64,4096]{1,0:T(8,128)(2,1)}, u32[]{:S(2)}, u32[]{:S(2)}) collective-permute-start(bf16[64,4096]{1,0:T(8,128)(2,1)} %get-tuple-element.228), channel_id=1, source_target_pairs={{0,24},{2,26},{4,28},{6,30},{8,16},{10,18},{12,20},{14,22},{16,8},... | collective-permute-start | bytes 1572872 | tf_op jit(solution)/shard_map/ppermute | solution.py:368
  542.3 46.2 %collective-permute-start.31 = (bf16[256,2048]{1,0:T(8,128)(2,1)}, bf16[256,2048]{1,0:T(8,128)(2,1)}, u32[]{:S(2)}, u32[]{:S(2)}) collective-permute-start(bf16[256,2048]{1,0:T(8,128)(2,1)} %pad_maximum_fusion.7), channel_id=1, source_target_pairs={{0,4},{2,6},{4,0},{6,2},{8,12},{10,14},{12,8},{14,10},{16,20},{18,... | collective-permute-start | bytes 3145736 | tf_op jit(solution)/shard_map/ppermute | solution.py:368
  554.0 34.6 %collective-permute-start.32 = (bf16[256,2048]{1,0:T(8,128)(2,1)}, bf16[256,2048]{1,0:T(8,128)(2,1)}, u32[]{:S(2)}, u32[]{:S(2)}) collective-permute-start(bf16[256,2048]{1,0:T(8,128)(2,1)} %pad_maximum_fusion.8), channel_id=1, source_target_pairs={{0,1},{1,0},{2,3},{3,2},{4,5},{5,4},{6,7},{7,6},{8,9},{9,8},{10,11... | collective-permute-start | bytes 3145736 | tf_op jit(solution)/shard_map/ppermute | solution.py:373
  571.1 26.9 %collective-permute-start.36 = (bf16[128,4096]{1,0:T(8,128)(2,1)}, bf16[128,4096]{1,0:T(8,128)(2,1)}, u32[]{:S(2)}, u32[]{:S(2)}) collective-permute-start(bf16[128,4096]{1,0:T(8,128)(2,1)} %get-tuple-element.408), channel_id=1, source_target_pairs={{0,4},{2,6},{4,0},{6,2},{8,12},{10,14},{12,8},{14,10},{16,20},{18,... | collective-permute-start | bytes 3145736 | tf_op jit(solution)/shard_map/ppermute | solution.py:368
  607.7 45.6 %collective-permute-start.41 = (bf16[256,4096]{1,0:T(8,128)(2,1)}, bf16[256,4096]{1,0:T(8,128)(2,1)}, u32[]{:S(2)}, u32[]{:S(2)}) collective-permute-start(bf16[256,4096]{1,0:T(8,128)(2,1)} %pad_maximum_fusion.2), channel_id=1, source_target_pairs={{0,4},{2,6},{4,0},{6,2},{8,12},{10,14},{12,8},{14,10},{16,20},{18,... | collective-permute-start | bytes 6291464 | tf_op jit(solution)/shard_map/ppermute | solution.py:368
  608.9 45.1 %collective-permute-start.42 = (bf16[256,4096]{1,0:T(8,128)(2,1)}, bf16[256,4096]{1,0:T(8,128)(2,1)}, u32[]{:S(2)}, u32[]{:S(2)}) collective-permute-start(bf16[256,4096]{1,0:T(8,128)(2,1)} %pad_maximum_fusion.3), channel_id=1, source_target_pairs={{0,1},{1,0},{2,3},{3,2},{4,5},{5,4},{6,7},{7,6},{8,9},{9,8},{10,11... | collective-permute-start | bytes 6291464 | tf_op jit(solution)/shard_map/ppermute | solution.py:373
  609.7 34.4 %collective-permute-start.38 = (bf16[64,2048]{1,0:T(8,128)(2,1)}, bf16[64,2048]{1,0:T(8,128)(2,1)S(1)}, u32[]{:S(2)}, u32[]{:S(2)}) collective-permute-start(bf16[64,2048]{1,0:T(8,128)(2,1)} %get-tuple-element.242), channel_id=1, source_target_pairs={{0,8},{2,10},{4,12},{6,14},{8,0},{10,2},{12,4},{14,6},{16,24},{18,... | collective-permute-start | bytes 786440 | tf_op jit(solution)/shard_map/ppermute | solution.py:368
  612.3 31.8 %collective-permute-start.39 = (bf16[64,2048]{1,0:T(8,128)(2,1)}, bf16[64,2048]{1,0:T(8,128)(2,1)}, u32[]{:S(2)}, u32[]{:S(2)}) collective-permute-start(bf16[64,2048]{1,0:T(8,128)(2,1)} %get-tuple-element.243), channel_id=1, source_target_pairs={{0,16},{2,18},{4,20},{6,22},{8,24},{10,26},{12,28},{14,30},{16,0},... | collective-permute-start | bytes 786440 | tf_op jit(solution)/shard_map/ppermute | solution.py:368
  613.0 31.1 %collective-permute-start.40 = (bf16[64,2048]{1,0:T(8,128)(2,1)}, bf16[64,2048]{1,0:T(8,128)(2,1)}, u32[]{:S(2)}, u32[]{:S(2)}) collective-permute-start(bf16[64,2048]{1,0:T(8,128)(2,1)} %get-tuple-element.244), channel_id=1, source_target_pairs={{0,24},{2,26},{4,28},{6,30},{8,16},{10,18},{12,20},{14,22},{16,8},... | collective-permute-start | bytes 786440 | tf_op jit(solution)/shard_map/ppermute | solution.py:368
  668.7 44.2 %collective-permute-start.48 = (bf16[64,4096]{1,0:T(8,128)(2,1)}, bf16[64,4096]{1,0:T(8,128)(2,1)}, u32[]{:S(2)}, u32[]{:S(2)}) collective-permute-start(bf16[64,4096]{1,0:T(8,128)(2,1)} %get-tuple-element.276), channel_id=1, source_target_pairs={{0,8},{2,10},{4,12},{6,14},{8,0},{10,2},{12,4},{14,6},{16,24},{18,... | collective-permute-start | bytes 1572872 | tf_op jit(solution)/shard_map/ppermute | solution.py:368
  671.4 41.5 %collective-permute-start.49 = (bf16[64,4096]{1,0:T(8,128)(2,1)}, bf16[64,4096]{1,0:T(8,128)(2,1)}, u32[]{:S(2)}, u32[]{:S(2)}) collective-permute-start(bf16[64,4096]{1,0:T(8,128)(2,1)} %get-tuple-element.277), channel_id=1, source_target_pairs={{0,16},{2,18},{4,20},{6,22},{8,24},{10,26},{12,28},{14,30},{16,0},... | collective-permute-start | bytes 1572872 | tf_op jit(solution)/shard_map/ppermute | solution.py:368
  672.5 46.9 %collective-permute-start.50 = (bf16[64,4096]{1,0:T(8,128)(2,1)}, bf16[64,4096]{1,0:T(8,128)(2,1)}, u32[]{:S(2)}, u32[]{:S(2)}) collective-permute-start(bf16[64,4096]{1,0:T(8,128)(2,1)} %get-tuple-element.278), channel_id=1, source_target_pairs={{0,24},{2,26},{4,28},{6,30},{8,16},{10,18},{12,20},{14,22},{16,8},... | collective-permute-start | bytes 1572872 | tf_op jit(solution)/shard_map/ppermute | solution.py:368
  (122 other events, 1256.4 us)
Sparse Core Ops, SparseCore 0:
  11.6 104.9 all-gather.2
  120.1 160.2 all-gather.4
